TPU v7x, 512 devices: a whole 4x8x8 slice. The times are simulated.
512 devices in a mesh: ep: 8 (over y), etp: 64 (over z, x, core).
Axes of the slice: x: 4, y: 8, z: 8, core: 2. Of those that a mesh axis runs over, the one named last changes fastest.
Arguments:
- tokens: bfloat16 [384, 3072], P('ep', 'etp'), may hold values from -6 to 6
- routes: int32 [384, 2], P('ep'), may hold values from 0 to 7, as said below
- route_gates: float32 [384, 2], P('ep'), may hold values from 0.1 to 0.9
- cotangent: bfloat16 [384, 3072], P('ep', 'etp'), may hold values from -1.5 to 1.5
- w_gate: bfloat16 [8, 3072, 8192], P('ep', None, 'etp'), may hold values from -0.109375 to 0.109375
- w_up: bfloat16 [8, 3072, 8192], P('ep', None, 'etp'), may hold values from -0.109375 to 0.109375
- w_down: bfloat16 [8, 8192, 3072], P('ep', 'etp'), may hold values from -0.1875 to 0.1875
Outputs:
- mixed: bfloat16 [384, 3072], P('ep', 'etp')
- grad_gates: float32 [384, 2], P('ep')
- grad_w_gate: bfloat16 [8, 3072, 8192], P('ep', None, 'etp')
- grad_w_up: bfloat16 [8, 3072, 8192], P('ep', None, 'etp')
- grad_w_down: bfloat16 [8, 8192, 3072], P('ep', 'etp')
Inputs may be any that keep to these rules, and one draw needn't show every extreme that they name: `routes`: within each aligned block of 48 rows (the tokens of one index of ep) the two experts of a row differ and no expert is named by more than 24 rows; one expert, the same in every block, is named by exactly 24 rows of each block.
All inputs are finite; a program needn't handle non-finite values.
Results may differ from a plain program's by a relative error of at most 0.0058.
Values may be sent and summed in bfloat16 or wider, within the bound.
A program may use at most 64 MiB of HBM per device.

v0:
```python
import jax
import jax.numpy as jnp
from jax import lax
from jax.sharding import PartitionSpec as P

EXPERTS = 8
CAP = 24


def per_device(tokens, routes, route_gates, cotangent, w_gate, w_up, w_down):
    local_experts = w_gate.shape[0]
    ep_count = lax.axis_size("ep")
    tok_count = tokens.shape[0]
    flat_ids = routes.reshape(-1)
    pair_count = flat_ids.shape[0]
    onehot = (flat_ids[:, None] == jnp.arange(EXPERTS, dtype=jnp.int32)[None, :]).astype(jnp.int32)
    before = jnp.cumsum(onehot, axis=0) - onehot
    slot_id = jnp.sum(before * onehot, axis=1)
    target = flat_ids * CAP + slot_id
    slot_table = (
        jnp.full((EXPERTS * CAP,), pair_count, jnp.int32)
        .at[target]
        .set(jnp.arange(pair_count, dtype=jnp.int32))
    )
    token_of_slot = slot_table // 2
    gate_flat = jnp.concatenate([route_gates.reshape(-1), jnp.zeros((1,), jnp.float32)])
    slot_gate = gate_flat[slot_table][:, None]
    gates_wide = route_gates[:, :, None]
    width = tokens.shape[1]
    x_pad = jnp.concatenate([tokens, jnp.zeros((1, width), jnp.bfloat16)], axis=0)
    dy_pad = jnp.concatenate([cotangent, jnp.zeros((1, width), jnp.bfloat16)], axis=0)
    x_sent = x_pad[token_of_slot].reshape(ep_count, local_experts, CAP, width)
    dy_rows = (slot_gate * dy_pad[token_of_slot].astype(jnp.float32)).astype(jnp.bfloat16)
    x_sent, dy_sent = (x_sent, dy_rows.reshape(ep_count, local_experts, CAP, width))
    x_recv, dy_recv = (
        lax.all_to_all(x_sent, "ep", split_axis=0, concat_axis=2, tiled=True),
        lax.all_to_all(dy_sent, "ep", split_axis=0, concat_axis=2, tiled=True),
    )
    x_rows, dy_rows = (
        lax.all_gather(x_recv, "etp", axis=3, tiled=True),
        lax.all_gather(dy_recv, "etp", axis=3, tiled=True),
    )
    rows_x = x_rows[0]
    rows_dy = dy_rows[0]
    gate_pre = jnp.einsum("erd,edf->erf", rows_x, w_gate, preferred_element_type=jnp.float32)
    up_pre = jnp.einsum("erd,edf->erf", rows_x, w_up, preferred_element_type=jnp.float32)
    sigma = jax.nn.sigmoid(gate_pre)
    hidden = (jax.nn.silu(gate_pre) * up_pre).astype(jnp.bfloat16)
    output_part = jnp.einsum("erf,efd->erd", hidden, w_down, preferred_element_type=jnp.float32)
    d_hidden = jnp.einsum("erd,efd->erf", rows_dy, w_down, preferred_element_type=jnp.float32)
    d_up = (d_hidden * jax.nn.silu(gate_pre)).astype(jnp.bfloat16)
    d_gate = (d_hidden * up_pre * sigma * (1.0 + gate_pre * (1.0 - sigma))).astype(jnp.bfloat16)
    grad_down = jnp.einsum("erf,erd->efd", hidden, rows_dy, preferred_element_type=jnp.float32)
    grad_gate_w = jnp.einsum("erd,erf->edf", rows_x, d_gate, preferred_element_type=jnp.float32)
    grad_up_w = jnp.einsum("erd,erf->edf", rows_x, d_up, preferred_element_type=jnp.float32)
    output_part, grad_w_gate, grad_w_up, grad_w_down = (
        output_part,
        grad_gate_w.astype(jnp.bfloat16),
        grad_up_w.astype(jnp.bfloat16),
        grad_down.astype(jnp.bfloat16),
    )
    returned = lax.all_to_all(output_part[None], "ep", split_axis=2, concat_axis=0, tiled=True)
    pair_rows = returned.reshape(EXPERTS * CAP, -1)[target].reshape(tok_count, 2, -1)
    full_rows = lax.psum_scatter(pair_rows, "etp", scatter_dimension=2, tiled=True)
    mixed = jnp.sum(gates_wide * full_rows, axis=1).astype(jnp.bfloat16)
    partial_grad = jnp.sum(full_rows * cotangent.astype(jnp.float32)[:, None, :], axis=2)
    grad_gates = lax.psum(partial_grad, "etp")
    return (mixed, grad_gates, grad_w_gate, grad_w_up, grad_w_down)


def solution(mesh):
    in_specs = (
        P("ep", "etp"),
        P("ep", None),
        P("ep", None),
        P("ep", "etp"),
        P("ep", None, "etp"),
        P("ep", None, "etp"),
        P("ep", "etp", None),
    )
    out_specs = (
        P("ep", "etp"),
        P("ep", None),
        P("ep", None, "etp"),
        P("ep", None, "etp"),
        P("ep", "etp", None),
    )
    return jax.shard_map(
        per_device, mesh=mesh, in_specs=in_specs, out_specs=out_specs, check_vma=False
    )
```

profile of v0, /device:TPU:16, one launch (start us, length us, event | category | flops | bytes accessed | tf_op | source)
XLA Modules:
  0.0 672.5 jit_solution(16049948253081429663)
XLA Ops:
  7.2 0.0 copy-start
  7.2 0.0 copy-start.3
  7.2 0.0 all-gather.3.cloned.1.call-start
  7.2 0.8 broadcast_multiply_fusion
  8.0 0.8 copy.22
  8.8 0.1 copy.21
  8.9 0.1 mul.85
  9.0 0.1 eq.15
  9.1 0.1 fusion.19
  9.2 0.1 reduce_window_sum.11
  9.4 0.2 select_reduce_fusion
  9.6 0.9 scatter_custom_fusion
  10.5 0.7 concatenate.9
  11.2 0.8 gather_fusion
  12.0 0.1 reshape.210
  12.1 13.5 %all_to_all.33 = bf16[8,2,576]{2,1,0:T(2,128)(2,1)S(1)} all-to-all(bf16[8,2,576]{2,1,0:T(2,128)(2,1)S(1)} %reshape.210), channel_id=1, replica_groups=mesh['ep'=8,'etp'=64] {'ep'}, dimensions={0} | all-to-all | bytes 36864 | tf_op jit(solution)/shard_map/all_to_all | solution.py:36
  25.6 0.1 reshape.211
  25.7 0.7 copy.24
  26.4 0.0 all-gather.3.cloned.1.call-update
  26.5 0.8 copy.20
  27.2 0.7 concatenate.11
  27.9 0.8 gather_fusion.3
  28.7 0.1 reshape.159
  28.8 0.1 pad_maximum_fusion
  28.9 1.6 gather_fusion.2
  30.5 0.0 copy-start.5
  30.5 0.1 mul.92
  30.6 0.1 fusion.16
  30.7 0.7 reshape.212
  31.4 5.6 all-to-all-start.2
  37.0 73.1 %all-gather.3.cloned.1.call-done = bf16[1,1,192,3072]{2,3,1,0:T(8,128)(2,1)} async-done(((bf16[1,1,192,48]{2,3,1,0:T(8,128)(2,1)}), bf16[1,1,192,3072]{2,3,1,0:T(8,128)(2,1)}) %all-gather.3.cloned.1.call-update) | async-done | bytes 1179664 | tf_op jit(solution)/shard_map/all_gather | solution.py:40
  110.1 0.0 copy-done.3
  110.1 0.0 copy-start.1
  110.1 2.1 fusion.10
  112.3 0.0 copy-done.5
  112.3 0.0 copy-done.1
  112.3 0.6 multiply_convert_fusion.2
  112.9 0.0 copy-done
  112.9 0.5 convolution_bitcast_fusion
  113.4 3.8 copy.25
  117.2 0.0 all-to-all-done.2
  117.2 7.4 %all-to-all-start.1 = ((f32[1,1,192,3072]{3,1,0,2:T(1,128)}), f32[1,1,192,3072]{3,1,0,2:T(1,128)}, u32[]{:S(2)}, u32[]{:S(2)}) async-start(f32[1,1,192,3072]{3,1,0,2:T(1,128)} %copy.25), calls=%async_computation.1 | async-start | bytes 4718592 | tf_op jit(solution)/shard_map/all_to_all | solution.py:62
  124.6 0.0 all-gather.5.cloned.1.call-start
  124.6 0.1 reshape.213
  124.7 0.7 copy.28
  125.4 0.0 all-gather.5.cloned.1.call-update
  125.4 0.0 all-reduce.5.cloned.1.call-start
  125.5 0.0 copy-done.4
  125.5 1.3 dynamic-slice
  127.4 82.2 %all-gather.5.cloned.1.call-done = bf16[1,1,192,3072]{2,3,1,0:T(8,128)(2,1)} async-done(((bf16[1,1,192,48]{2,3,1,0:T(8,128)(2,1)}), bf16[1,1,192,3072]{2,3,1,0:T(8,128)(2,1)}) %all-gather.5.cloned.1.call-update) | async-done | bytes 1179664 | tf_op jit(solution)/shard_map/all_gather | solution.py:41
  209.6 2.0 fusion.4
  211.6 0.0 all-to-all-done.1
  211.6 2.1 copy.34
  213.7 2.0 gather_fusion.1
  215.7 2.9 reshape.158
  218.6 0.0 all-reduce.5.cloned.1.call-update
  218.7 3.1 fusion.2
  221.7 0.0 copy-done.2
  221.7 1.5 fusion.1
  223.2 1.5 fusion
  224.6 189.6 %all-reduce.5.cloned.1.call-done = f32[48,2,3072]{2,1,0:T(2,128)} async-done(((f32[48,2,3072]{2,1,0:T(2,128)}), f32[48,2,3072]{2,1,0:T(2,128)}) %all-reduce.5.cloned.1.call-update) | async-done | bytes 1179664
  414.3 1.7 multiply_reduce_fusion
  416.0 249.4 %psum.7 = f32[48,2]{1,0:T(8,128)S(1)} all-reduce(f32[48,2]{1,0:T(8,128)S(1)} %get-tuple-element.10), channel_id=1, replica_groups=mesh['ep'=8,'etp'=64] {'etp'}, use_global_device_ids=true, to_apply=%region_6.7 | all-reduce | flops 96 | bytes 768 | tf_op jit(solution)/shard_map/psum | solution.py:67
  665.4 0.6 copy.29
  (8 shorter events, 0.0 us)
Async XLA Ops:
  7.2 105.7 %copy-start = (bf16[1,128,3072]{2,1,0:T(8,128)(2,1)S(1)}, bf16[1,128,3072]{2,1,0:T(8,128)(2,1)}, u32[]{:S(2)}) copy-start(bf16[1,128,3072]{2,1,0:T(8,128)(2,1)} %param.13) | copy-start | bytes 2359300
  7.2 102.9 %copy-start.3 = (bf16[1,3072,128]{2,1,0:T(8,128)(2,1)S(1)}, bf16[1,3072,128]{2,1,0:T(8,128)(2,1)}, u32[]{:S(2)}) copy-start(bf16[1,3072,128]{2,1,0:T(8,128)(2,1)} %param.11) | copy-start | bytes 2359300
  7.2 102.9 %all-gather.3.cloned.1.call-start = ((), (), s32[]{:S(2)}) async-start(), calls=%async_computation.3 | async-start | bytes 1597440 | tf_op jit(solution)/shard_map/all_gather | solution.py:40
  30.5 81.8 %copy-start.5 = (bf16[1,3072,128]{2,1,0:T(8,128)(2,1)S(1)}, bf16[1,3072,128]{2,1,0:T(8,128)(2,1)}, u32[]{:S(2)}) copy-start(bf16[1,3072,128]{2,1,0:T(8,128)(2,1)} %param.12) | copy-start | bytes 2359300
  31.4 85.8 %all-to-all-start.2 = ((bf16[8,2,576]{2,1,0:T(2,128)(2,1)}), bf16[8,2,576]{2,1,0:T(2,128)(2,1)S(1)}, u32[]{:S(2)}, u32[]{:S(2)}) async-start(bf16[8,2,576]{2,1,0:T(2,128)(2,1)} %reshape.212), calls=%async_computation.2 | async-start | bytes 40960 | tf_op jit(solution)/shard_map/all_to_all | solution.py:37
  110.1 2.1 copy-start.1
  117.2 8.3 %copy-start.4 = (bf16[48,48]{1,0:T(8,128)(2,1)S(1)}, bf16[48,48]{1,0:T(8,128)(2,1)}, u32[]{:S(2)}) copy-start(bf16[48,48]{1,0:T(8,128)(2,1)} %param.10) | copy-start | bytes 13828
  117.2 94.4 %all-to-all-start.1 = ((f32[1,1,192,3072]{3,1,0,2:T(1,128)}), f32[1,1,192,3072]{3,1,0,2:T(1,128)}, u32[]{:S(2)}, u32[]{:S(2)}) async-start(f32[1,1,192,3072]{3,1,0,2:T(1,128)} %copy.25), calls=%async_computation.1 | async-start | bytes 4718592 | tf_op jit(solution)/shard_map/all_to_all | solution.py:62
  124.6 85.0 %all-gather.5.cloned.1.call-start = ((), (), s32[]{:S(2)}) async-start(), calls=%async_computation.4 | async-start | bytes 1597440 | tf_op jit(solution)/shard_map/all_gather | solution.py:41
  125.4 288.8 %all-reduce.5.cloned.1.call-start = ((), (), s32[]{:S(2)}) async-start(), calls=%async_computation.5 | async-start | bytes 2359296
  218.6 3.1 copy-start.2
Sparse Core Ops, SparseCore 0:
  26.6 83.4 all-gather.2
  129.3 80.2 all-gather.4
  218.8 195.4 all-reduce.4
where the time goes:
time: 673 us
  waiting for transfers between devices  345 us (51%)
  blocking collectives  263 us (39%)
  local copies, waits for them, and re-layouts  22.7 us (3%)
  between operations  14.6 us (2%)
  starting transfers between devices  13.1 us (2%)
  matrix products  11.2 us (2%)
    psum x1, blocking collectives, per_device(): grad_gates = lax.psum(partial_grad, 'etp')  249 us
    unnamed x4, waiting for transfers between devices  190 us
    all_gather x1, waiting for transfers between devices, per_device(): lax.all_gather(dy_recv, 'etp', axis=3, tiled=True)  82.2 us
    all_gather x1, waiting for transfers between devices, per_device(): lax.all_gather(x_recv, 'etp', axis=3, tiled=True)  73.1 us
    all_to_all x1, blocking collectives, per_device(): lax.all_to_all(x_sent, 'ep', split_axis=0, concat_axis=2, tiled=True)  13.5 us
  transfers between devices with their start and end apart: 5, of which 3 were waited for; matrix products, arithmetic and copies ran while one was open for 3% of the time, Pallas kernels for 0%

commit v1 on v0

v1 whole, which is shorter than its diff:
```python
import jax
import jax.numpy as jnp
import numpy as np
from jax import lax
from jax.sharding import Mesh
from jax.sharding import PartitionSpec as P

EXPERTS = 8
CAP = 24
SUB = ("z", "x", "core")


def sub_sizes(etp):
    if etp % 8 == 0:
        return (etp // 8, 4, 2)
    return (etp, 1, 1)


def per_device(tokens, routes, route_gates, cotangent, w_gate, w_up, w_down):
    ep_count = lax.axis_size("ep")
    nz, nx, nc = lax.axis_size("z"), lax.axis_size("x"), lax.axis_size("core")
    tok_count, width = tokens.shape
    flat_ids = routes.reshape(-1)
    pair_count = flat_ids.shape[0]
    onehot = (flat_ids[:, None] == jnp.arange(EXPERTS, dtype=jnp.int32)[None, :]).astype(jnp.int32)
    before = jnp.cumsum(onehot, axis=0) - onehot
    slot_id = jnp.sum(before * onehot, axis=1)
    target = flat_ids * CAP + slot_id
    slot_table = (
        jnp.full((EXPERTS * CAP,), pair_count, jnp.int32)
        .at[target]
        .set(jnp.arange(pair_count, dtype=jnp.int32))
    )
    token_of_slot = slot_table // 2
    gate_flat = jnp.concatenate([route_gates.reshape(-1), jnp.zeros((1,), jnp.float32)])
    slot_gate = gate_flat[slot_table]
    xc = jnp.concatenate([tokens, cotangent], axis=1)
    xc_pad = jnp.concatenate([xc, jnp.zeros((1, 2 * width), jnp.bfloat16)], axis=0)
    sent = xc_pad[token_of_slot].reshape(ep_count, CAP, 2 * width)
    recv = lax.all_to_all(sent, "ep", 0, 0, tiled=True)
    gates_recv = lax.all_to_all(slot_gate.reshape(ep_count, CAP), "ep", 0, 0, tiled=True)
    rows = ep_count * CAP
    chunk = recv.reshape(rows, 2 * width)
    g = lax.all_gather(chunk, "z", axis=0)
    g = lax.all_gather(g, "x", axis=0)
    g = lax.all_gather(g, "core", axis=0)
    g = jnp.transpose(g, (3, 2, 1, 0, 4))
    rows_x = g[..., :width].reshape(rows, -1)
    cot_rows = g[..., width:].reshape(rows, -1)
    slot_g = gates_recv.reshape(rows, 1)
    rows_dy = (slot_g * cot_rows.astype(jnp.float32)).astype(jnp.bfloat16)
    wg, wu, wd = w_gate[0], w_up[0], w_down[0]
    gate_pre = jnp.dot(rows_x, wg, preferred_element_type=jnp.float32)
    up_pre = jnp.dot(rows_x, wu, preferred_element_type=jnp.float32)
    sigma = jax.nn.sigmoid(gate_pre)
    hidden = (jax.nn.silu(gate_pre) * up_pre).astype(jnp.bfloat16)
    output_part = jnp.dot(hidden, wd, preferred_element_type=jnp.float32)
    d_hidden = lax.dot_general(rows_dy, wd, (((1,), (1,)), ((), ())), preferred_element_type=jnp.float32)
    d_up = (d_hidden * jax.nn.silu(gate_pre)).astype(jnp.bfloat16)
    d_gate = (d_hidden * up_pre * sigma * (1.0 + gate_pre * (1.0 - sigma))).astype(jnp.bfloat16)
    grad_down = lax.dot_general(hidden, rows_dy, (((0,), (0,)), ((), ())), preferred_element_type=jnp.float32)
    grad_gate_w = lax.dot_general(rows_x, d_gate, (((0,), (0,)), ((), ())), preferred_element_type=jnp.float32)
    grad_up_w = lax.dot_general(rows_x, d_up, (((0,), (0,)), ((), ())), preferred_element_type=jnp.float32)
    inner = jnp.sum(output_part * cot_rows.astype(jnp.float32), axis=1)
    part = output_part.reshape(rows, nz, nx, nc, width)
    part = jnp.transpose(part, (3, 2, 1, 0, 4))
    extra = jnp.broadcast_to(inner[None, None, None, :, None], (nc, nx, nz, rows, 1))
    part = jnp.concatenate([part, extra], axis=4)
    part = lax.psum_scatter(part, "core", scatter_dimension=0, tiled=True)
    part = lax.psum_scatter(part, "x", scatter_dimension=1, tiled=True)
    part = lax.psum_scatter(part, "z", scatter_dimension=2, tiled=True)
    back = part.reshape(ep_count, CAP, width + 1)
    returned = lax.all_to_all(back, "ep", 0, 0, tiled=True).reshape(EXPERTS * CAP, width + 1)
    pair_rows = returned[target].reshape(tok_count, 2, width + 1)
    mixed = jnp.sum(route_gates[:, :, None] * pair_rows[:, :, :width], axis=1).astype(jnp.bfloat16)
    grad_gates = pair_rows[:, :, width]
    return (
        mixed,
        grad_gates,
        grad_gate_w.astype(jnp.bfloat16)[None],
        grad_up_w.astype(jnp.bfloat16)[None],
        grad_down.astype(jnp.bfloat16)[None],
    )


def solution(mesh):
    ep = mesh.shape["ep"]
    etp = mesh.shape["etp"]
    nz, nx, nc = sub_sizes(etp)
    devs = np.asarray(mesh.devices).reshape(ep, nz, nx, nc)
    mesh2 = Mesh(devs, ("ep",) + SUB)
    in_specs = (
        P("ep", SUB),
        P("ep", None),
        P("ep", None),
        P("ep", SUB),
        P("ep", None, SUB),
        P("ep", None, SUB),
        P("ep", SUB, None),
    )
    out_specs = (
        P("ep", SUB),
        P("ep", None),
        P("ep", None, SUB),
        P("ep", None, SUB),
        P("ep", SUB, None),
    )
    return jax.shard_map(
        per_device, mesh=mesh2, in_specs=in_specs, out_specs=out_specs, check_vma=False
    )
```

time: 673 us -> 263 us (0.39)
  the two profiles are of different devices: /device:TPU:16 before, /device:TPU:6 now
where the time goes in v1:
time: 263 us; the launch traced here: 262 us
  waiting for transfers between devices  134 us (51%)
  blocking collectives  48.5 us (18%)
  local copies, waits for them, and re-layouts  28.6 us (11%)
  between operations  14 us (5%)
  other arithmetic  13.7 us (5%)
  starting transfers between devices  13.6 us (5%)
  matrix products  9.72 us (4%)
    reduce_scatter x1, waiting for transfers between devices, per_device(): part = lax.psum_scatter(part, 'z', scatter_dimension=2, tiled=True)  38.3 us
    all_gather x1, blocking collectives, per_device(): g = lax.all_gather(chunk, 'z', axis=0)  33.5 us
    all_gather x1, waiting for transfers between devices, per_device(): g = lax.all_gather(g, 'x', axis=0)  24 us
    all_gather x1, waiting for transfers between devices, per_device(): g = lax.all_gather(g, 'core', axis=0)  23.5 us
    reduce_scatter x1, waiting for transfers between devices, per_device(): part = lax.psum_scatter(part, 'core', scatter_dimension=0, tiled=True)  20.5 us
    all_to_all x1, blocking collectives, per_device(): recv = lax.all_to_all(sent, 'ep', 0, 0, tiled=True)  15.1 us
    reduce_scatter x1, waiting for transfers between devices, per_device(): part = lax.psum_scatter(part, 'x', scatter_dimension=1, tiled=True)  13.2 us
    all_to_all x1, waiting for transfers between devices, per_device(): lax.all_to_all(slot_gate.reshape(ep_count, CAP), 'ep', 0, 0, tiled=True)  7.54 us
  transfers between devices with their start and end apart: 7, of which 7 were waited for; matrix products, arithmetic and copies ran while one was open for 5% of the time, Pallas kernels for 0%

profile of v1, /device:TPU:6, one launch (start us, length us, event | category | flops | bytes accessed | tf_op | source)
XLA Modules:
  0.0 261.9 jit_solution(16151901436860777572)
XLA Ops:
  7.2 0.0 all-gather.5.cloned.1.call-start
  7.2 0.7 broadcast_multiply_fusion
  8.0 0.8 copy.54
  8.7 0.1 copy.53
  8.8 0.1 mul.71
  9.0 0.1 eq.15
  9.1 0.1 fusion.15
  9.2 0.1 reduce_window_sum.11
  9.3 0.2 select_reduce_fusion
  9.5 0.9 scatter_custom_fusion
  10.4 0.8 fusion.19
  11.2 0.8 gather_fusion
  12.0 15.1 %all_to_all.19 = bf16[8,24,96]{2,1,0:T(8,128)(2,1)S(1)} all-to-all(bf16[8,24,96]{2,1,0:T(8,128)(2,1)S(1)} %bitcast.67), channel_id=1, replica_groups=mesh['ep'=8,'z'=8,'x'=4,'core'=2] {'ep'}, dimensions={0} | all-to-all | bytes 73728 | tf_op jit(solution)/shard_map/all_to_all | solution.py:40
  27.1 33.5 %all_gather.15 = bf16[8,192,96]{2,1,0:T(8,128)(2,1)} all-gather(bf16[1,192,96]{2,1,0:T(8,128)(2,1)S(1)} %bitcast.68), channel_id=1, replica_groups=mesh['ep'=8,'z'=8,'x'=4,'core'=2] {'z'}, dimensions={0}, use_global_device_ids=true | all-gather | bytes 331776 | tf_op jit(solution)/shard_map/all_gather | solution.py:44
  60.6 0.0 all-gather.5.cloned.1.call-update
  60.6 0.0 all-gather.7.cloned.1.call-start
  60.6 24.0 %all-gather.5.cloned.1.call-done = bf16[32,192,96]{2,1,0:T(8,128)(2,1)} async-done(((bf16[8,192,96]{2,1,0:T(8,128)(2,1)}), bf16[32,192,96]{2,1,0:T(8,128)(2,1)}) %all-gather.5.cloned.1.call-update) | async-done | bytes 1179664 | tf_op jit(solution)/shard_map/all_gather | solution.py:45
  84.7 0.0 all-gather.7.cloned.1.call-update
  84.7 0.0 reduce-scatter.4.cloned.1.call-start
  84.7 23.5 %all-gather.7.cloned.1.call-done = bf16[8,8,192,96]{3,2,1,0:T(8,128)(2,1)} async-done(((bf16[4,8,192,96]{3,2,1,0:T(8,128)(2,1)}), bf16[8,8,192,96]{3,2,1,0:T(8,128)(2,1)}) %all-gather.7.cloned.1.call-update) | async-done | bytes 2359312 | tf_op jit(solution)/shard_map/all_gather | solution.py:46
  108.2 4.8 %copy.55 = bf16[2,4,8,192,96]{3,4,0,1,2:T(8,128)(2,1)} copy(bf16[2,4,8,192,96]{4,3,2,1,0:T(8,128)(2,1)} %bitcast.61) | data formatting | bytes 4718592 | tf_op jit(solution)/shard_map/all_gather | solution.py:46
  113.0 4.1 %slice_convert_fusion = (f32[192,8,4,2,48]{0,4,3,2,1:T(8,128)}, bf16[192,8,4,2,48]{0,4,3,2,1:T(8,128)(2,1)S(1)}) fusion(bf16[192,8,4,2,96]{0,4,3,2,1:T(8,128)(2,1)} %bitcast.57), kind=kLoop, calls=%fused_computation.14 | loop fusion | flops 589824 | bytes 5898240 | tf_op jit(solution)/shard_map/convert_element_type | solution.py:64
  117.1 3.5 %copy.57 = f32[192,3072]{1,0:T(8,128)} copy(f32[192,3072]{0,1:T(8,128)} %bitcast.51) | data formatting | bytes 4718592 | tf_op jit(solution)/shard_map/convert_element_type | solution.py:64
  120.6 0.6 fusion.10
  121.2 0.5 copy-done.5
  121.7 0.6 multiply_convert_fusion.5
  122.3 1.0 copy-done.2
  123.4 1.9 multiply_reduce_fusion
  125.2 3.4 %copy.56 = f32[192,3072]{0,1:T(8,128)} copy(f32[192,3072]{1,0:T(8,128)} %get-tuple-element.12) | data formatting | bytes 4718592 | tf_op jit(solution)/shard_map/dot_general | solution.py:57
  128.7 2.3 pad_maximum_fusion
  131.1 3.6 %copy.58 = f32[2,4,8,192,49]{3,2,4,1,0:T(8,128)} copy(f32[2,4,8,192,49]{3,4,0,1,2:T(8,128)S(1)} %pad_maximum_fusion) | data formatting | bytes 4816896 | tf_op jit(solution)/shard_map/concatenate | solution.py:68
  134.7 0.0 reduce-scatter.4.cloned.1.call-update
  134.8 0.0 reduce-scatter.6.cloned.1.call-start
  134.8 20.5 %reduce-scatter.4.cloned.1.call-done = f32[1,4,8,192,49]{3,2,4,1,0:T(8,128)} async-done(((f32[2,4,8,192,49]{3,2,4,1,0:T(8,128)}), f32[1,4,8,192,49]{3,2,4,1,0:T(8,128)}) %reduce-scatter.4.cloned.1.call-update) | async-done | bytes 1204240 | tf_op jit(solution)/shard_map/reduce_scatter | solution.py:69
  155.3 0.0 reduce-scatter.6.cloned.1.call-update
  155.3 0.1 copy.52
  155.4 0.1 reshape.87
  155.5 0.1 pad_maximum_fusion.1
  155.6 1.6 gather_fusion.2
  157.2 0.7 all_to_all.14
  157.9 6.7 %all-to-all-start.2 = ((f32[8,1,24]{2,1,0:T(1,128)}), f32[8,1,24]{2,1,0:T(1,128)S(1)}, u32[]{:S(2)}, u32[]{:S(2)}) async-start(f32[8,1,24]{2,1,0:T(1,128)} %all_to_all.14), calls=%async_computation.5 | async-start | bytes 8192 | tf_op jit(solution)/shard_map/all_to_all | solution.py:41
  164.6 0.0 reduce-scatter.8.cloned.1.call-start
  164.7 7.5 %all-to-all-done.2 = f32[8,1,24]{2,1,0:T(1,128)S(1)} async-done(((f32[8,1,24]{2,1,0:T(1,128)}), f32[8,1,24]{2,1,0:T(1,128)S(1)}, u32[]{:S(2)}, u32[]{:S(2)}) %all-to-all-start.2) | async-done | bytes 800 | tf_op jit(solution)/shard_map/all_to_all | solution.py:41
  172.2 0.5 broadcast.83
  172.7 0.7 reduce.3
  173.4 0.1 mul.77
  173.5 3.1 %multiply_convert_fusion.1 = bf16[192,8,4,2,48]{0,4,3,2,1:T(8,128)(2,1)} fusion(f32[192]{0:T(256)S(1)} %mul.77, bf16[192,8,4,2,96]{0,4,3,2,1:T(8,128)(2,1)} %bitcast.58), kind=kLoop, calls=%fused_computation.12 | loop fusion | flops 1769472 | bytes 2360064 | tf_op jit(solution)/shard_map/convert_element_type | solution.py:51
  176.5 13.2 %reduce-scatter.6.cloned.1.call-done = f32[1,1,8,192,49]{3,2,4,0,1:T(8,128)} async-done(((f32[1,4,8,192,49]{3,2,4,0,1:T(8,128)}), f32[1,1,8,192,49]{3,2,4,0,1:T(8,128)}) %reduce-scatter.6.cloned.1.call-update) | async-done | bytes 301072 | tf_op jit(solution)/shard_map/reduce_scatter | solution.py:70
  189.7 2.2 copy.60
  192.0 2.1 fusion.4
  194.1 1.5 fusion
  195.6 1.6 fusion.2
  197.1 38.3 %reduce-scatter.8.cloned.1.call-done = f32[1,1,1,192,49]{4,3,2,1,0:T(8,128)} async-done(((f32[1,1,8,192,49]{4,3,2,1,0:T(8,128)}), f32[1,1,1,192,49]{4,3,2,1,0:T(8,128)}) %reduce-scatter.8.cloned.1.call-update) | async-done | bytes 37648 | tf_op jit(solution)/shard_map/reduce_scatter | solution.py:71
  235.5 1.6 reshape.136
  237.1 6.7 %all-to-all-start.1 = ((f32[8,1,1176]{2,1,0:T(1,128)}), f32[8,1,1176]{2,1,0:T(1,128)S(1)}, u32[]{:S(2)}, u32[]{:S(2)}) async-start(f32[8,1,1176]{2,1,0:T(1,128)} %reshape.136), calls=%async_computation.4 | async-start | bytes 81920 | tf_op jit(solution)/shard_map/all_to_all | solution.py:73
  243.8 1.5 fusion.1
  245.2 6.6 %all-to-all-done.1 = f32[8,1,1176]{2,1,0:T(1,128)S(1)} async-done(((f32[8,1,1176]{2,1,0:T(1,128)}), f32[8,1,1176]{2,1,0:T(1,128)S(1)}, u32[]{:S(2)}, u32[]{:S(2)}) %all-to-all-start.1) | async-done | bytes 37664 | tf_op jit(solution)/shard_map/all_to_all | solution.py:73
  251.9 0.5 broadcast.84
  252.4 0.7 reduce.4
  253.2 0.1 reshape.137
  253.3 0.6 gather_fusion.1
  253.9 0.7 fusion.13
  254.6 0.1 slice.25
  254.7 0.7 copy.63
  (17 shorter events, 0.1 us)
Async XLA Ops:
  7.2 115.2 %copy-start = (bf16[1,128,3072]{2,1,0:T(8,128)(2,1)S(1)}, bf16[1,128,3072]{2,1,0:T(8,128)(2,1)}, u32[]{:S(2)}) copy-start(bf16[1,128,3072]{2,1,0:T(8,128)(2,1)} %param.13) | copy-start | bytes 2359300
  7.2 77.5 %all-gather.5.cloned.1.call-start = ((), (), s32[]{:S(2)}) async-start(), calls=%async_computation.9 | async-start | bytes 1966080 | tf_op jit(solution)/shard_map/all_gather | solution.py:45
  60.6 47.6 %all-gather.7.cloned.1.call-start = ((), (), s32[]{:S(2)}) async-start(), calls=%async_computation.10 | async-start | bytes 4718592 | tf_op jit(solution)/shard_map/all_gather | solution.py:46
  84.7 70.6 %reduce-scatter.4.cloned.1.call-start = ((), (), s32[]{:S(2)}) async-start(), calls=%async_computation.6 | async-start | bytes 4816896 | tf_op jit(solution)/shard_map/reduce_scatter | solution.py:69
  117.1 3.5 %copy-start.3 = (bf16[1,3072,128]{2,1,0:T(8,128)(2,1)S(1)}, bf16[1,3072,128]{2,1,0:T(8,128)(2,1)}, u32[]{:S(2)}) copy-start(bf16[1,3072,128]{2,1,0:T(8,128)(2,1)} %param.11) | copy-start | bytes 2359300
  120.6 1.1 copy-start.5
  121.7 1.7 copy-start.2
  134.7 20.6 %copy-start.4 = (f32[48,2]{0,1:T(2,128)S(1)}, f32[48,2]{0,1:T(2,128)}, u32[]{:S(2)}) copy-start(f32[48,2]{0,1:T(2,128)} %param.9) | copy-start | bytes 1156
  134.8 55.0 %reduce-scatter.6.cloned.1.call-start = ((), (), s32[]{:S(2)}) async-start(), calls=%async_computation.7 | async-start | bytes 2007040 | tf_op jit(solution)/shard_map/reduce_scatter | solution.py:70
  157.9 14.3 %all-to-all-start.2 = ((f32[8,1,24]{2,1,0:T(1,128)}), f32[8,1,24]{2,1,0:T(1,128)S(1)}, u32[]{:S(2)}, u32[]{:S(2)}) async-start(f32[8,1,24]{2,1,0:T(1,128)} %all_to_all.14), calls=%async_computation.5 | async-start | bytes 8192 | tf_op jit(solution)/shard_map/all_to_all | solution.py:41
  164.6 70.8 %reduce-scatter.8.cloned.1.call-start = ((), (), s32[]{:S(2)}) async-start(), calls=%async_computation.8 | async-start | bytes 884736 | tf_op jit(solution)/shard_map/reduce_scatter | solution.py:71
  191.9 3.6 %copy-start.1 = (f32[192,8,4,2,48]{0,4,3,2,1:T(8,128)S(1)}, f32[192,8,4,2,48]{0,4,3,2,1:T(8,128)}, u32[]{:S(2)}) copy-start(f32[192,8,4,2,48]{0,4,3,2,1:T(8,128)} %get-tuple-element.5) | copy-start | bytes 7077892
  237.1 14.8 %all-to-all-start.1 = ((f32[8,1,1176]{2,1,0:T(1,128)}), f32[8,1,1176]{2,1,0:T(1,128)S(1)}, u32[]{:S(2)}, u32[]{:S(2)}) async-start(f32[8,1,1176]{2,1,0:T(1,128)} %reshape.136), calls=%async_computation.4 | async-start | bytes 81920 | tf_op jit(solution)/shard_map/all_to_all | solution.py:73
Sparse Core Ops, SparseCore 0:
  60.7 23.9 all-gather.4
  86.7 21.4 all-gather.6
  134.9 20.3 reduce-scatter.3
  158.2 31.4 reduce-scatter.5
  193.2 42.1 reduce-scatter.7

commit v2 on v1

--- a/solution.py
+++ b/solution.py
@@ -1,7 +1,11 @@
+import functools
+
 import jax
 import jax.numpy as jnp
 import numpy as np
 from jax import lax
+from jax.experimental import pallas as pl
+from jax.experimental.pallas import tpu as pltpu
 from jax.sharding import Mesh
 from jax.sharding import PartitionSpec as P
 
@@ -14,6 +18,80 @@
     if etp % 8 == 0:
         return (etp // 8, 4, 2)
     return (etp, 1, 1)
+
+
+def _gather_kernel(nz, nx, nc, chunk_ref, out_ref, sem_local, send_a, recv_a, send_b, recv_b, send_c, recv_c):
+    e = lax.axis_index("ep")
+    z = lax.axis_index("z")
+    x = lax.axis_index("x")
+    c = lax.axis_index("core")
+    mesh_id = pl.DeviceIdType.MESH
+    barrier = pltpu.get_barrier_semaphore()
+    for d in range(1, nz):
+        pl.semaphore_signal(barrier, inc=1, device_id=(e, (z + d) % nz, x, c), device_id_type=mesh_id)
+    for d in range(1, nx):
+        pl.semaphore_signal(barrier, inc=1, device_id=(e, z, (x + d) % nx, c), device_id_type=mesh_id)
+    for d in range(1, nc):
+        pl.semaphore_signal(barrier, inc=1, device_id=(e, z, x, (c + d) % nc), device_id_type=mesh_id)
+    pl.semaphore_wait(barrier, (nz - 1) + (nx - 1) + (nc - 1))
+
+    local = pltpu.make_async_copy(chunk_ref, out_ref.at[c, x, z], sem_local.at[0])
+    local.start()
+    sends = []
+    for d in range(1, nz):
+        cp = pltpu.make_async_remote_copy(
+            chunk_ref, out_ref.at[c, x, z], send_a.at[d - 1], recv_a.at[d - 1],
+            device_id=(e, (z + d) % nz, x, c), device_id_type=mesh_id)
+        cp.start()
+        sends.append(cp)
+    for d in range(1, nz):
+        pltpu.make_async_remote_copy(
+            chunk_ref, out_ref.at[c, x, (z + nz - d) % nz], send_a.at[d - 1], recv_a.at[d - 1],
+            device_id=(e, (z + nz - d) % nz, x, c), device_id_type=mesh_id).wait_recv()
+    local.wait()
+    for d in range(1, nx):
+        cp = pltpu.make_async_remote_copy(
+            out_ref.at[c, x], out_ref.at[c, x], send_b.at[d - 1], recv_b.at[d - 1],
+            device_id=(e, z, (x + d) % nx, c), device_id_type=mesh_id)
+        cp.start()
+        sends.append(cp)
+    for d in range(1, nx):
+        pltpu.make_async_remote_copy(
+            out_ref.at[c, (x + nx - d) % nx], out_ref.at[c, (x + nx - d) % nx], send_b.at[d - 1], recv_b.at[d - 1],
+            device_id=(e, z, (x + nx - d) % nx, c), device_id_type=mesh_id).wait_recv()
+    for d in range(1, nc):
+        cp = pltpu.make_async_remote_copy(
+            out_ref.at[c], out_ref.at[c], send_c.at[d - 1], recv_c.at[d - 1],
+            device_id=(e, z, x, (c + d) % nc), device_id_type=mesh_id)
+        cp.start()
+        sends.append(cp)
+    for d in range(1, nc):
+        pltpu.make_async_remote_copy(
+            out_ref.at[(c + nc - d) % nc], out_ref.at[(c + nc - d) % nc], send_c.at[d - 1], recv_c.at[d - 1],
+            device_id=(e, z, x, (c + nc - d) % nc), device_id_type=mesh_id).wait_recv()
+    for cp in sends:
+        cp.wait_send()
+
+
+def etp_gather(chunk, nz, nx, nc):
+    rows, cols = chunk.shape
+    vmem = pltpu.VMEM
+    return pl.pallas_call(
+        functools.partial(_gather_kernel, nz, nx, nc),
+        out_shape=jax.ShapeDtypeStruct((nc, nx, nz, rows, cols), chunk.dtype),
+        in_specs=[pl.BlockSpec(memory_space=vmem)],
+        out_specs=pl.BlockSpec(memory_space=vmem),
+        scratch_shapes=[
+            pltpu.SemaphoreType.DMA((1,)),
+            pltpu.SemaphoreType.DMA((max(nz - 1, 1),)),
+            pltpu.SemaphoreType.DMA((max(nz - 1, 1),)),
+            pltpu.SemaphoreType.DMA((max(nx - 1, 1),)),
+            pltpu.SemaphoreType.DMA((max(nx - 1, 1),)),
+            pltpu.SemaphoreType.DMA((max(nc - 1, 1),)),
+            pltpu.SemaphoreType.DMA((max(nc - 1, 1),)),
+        ],
+        compiler_params=pltpu.CompilerParams(collective_id=0, has_side_effects=True),
+    )(chunk)
 
 
 def per_device(tokens, routes, route_gates, cotangent, w_gate, w_up, w_down):
@@ -40,10 +118,9 @@
     recv = lax.all_to_all(sent, "ep", 0, 0, tiled=True)
     gates_recv = lax.all_to_all(slot_gate.reshape(ep_count, CAP), "ep", 0, 0, tiled=True)
     rows = ep_count * CAP
-    chunk = recv.reshape(rows, 2 * width)
-    g = lax.all_gather(chunk, "z", axis=0)
-    g = lax.all_gather(g, "x", axis=0)
-    g = lax.all_gather(g, "core", axis=0)
+    lanes = 128
+    chunk = recv.reshape(rows * 2 * width // lanes, lanes)
+    g = etp_gather(chunk, nz, nx, nc).reshape(nc, nx, nz, rows, 2 * width)
     g = jnp.transpose(g, (3, 2, 1, 0, 4))
     rows_x = g[..., :width].reshape(rows, -1)
     cot_rows = g[..., width:].reshape(rows, -1)

time: 263 us -> 217 us (0.83)
  waiting for transfers between devices: 134 us -> 82 us
  blocking collectives: 48.5 us -> 15.1 us
  Pallas kernels: 0 us -> 33.1 us
  local copies, waits for them, and re-layouts: 28.6 us -> 35.1 us
    all_gather x2 -> x0, waiting for transfers between devices: 47.5 us -> none  [the longest x1 24 us: per_device(): g = lax.all_gather(g, 'x', axis=0)]
    all_gather x1 -> x0, blocking collectives: 33.5 us -> none  [per_device(): g = lax.all_gather(chunk, 'z', axis=0)]
    pallas_call x0 -> x1, Pallas kernels: none -> 33.1 us  [etp_gather(): pl.pallas_call(functools.partial(_gather_kernel, nz, nx, nc), out_shape=j...]
    reshape x0 -> x3, local copies, waits for them, and re-layouts: none -> 11.4 us  [the longest x2 10.6 us: per_device(): g = etp_gather(chunk, nz, nx, nc).reshape(nc, nx, nz, rows, 2 * width)]
    all_gather x1 -> x0, local copies, waits for them, and re-layouts: 4.79 us -> none  [per_device(): g = lax.all_gather(g, 'core', axis=0)]
    reduce_scatter x1, waiting for transfers between devices: 20.5 us -> 16.2 us  [per_device(): part = lax.psum_scatter(part, 'core', scatter_dimension=0, tiled=True)]
  transfers between devices with their start and end apart: 7 -> 5, of which waited for: 7 -> 5; matrix products, arithmetic and copies ran while one was open for 5% -> 6% of each run, Pallas kernels for 0% -> 0%
where the time goes in v2:
time: 217 us; the launch traced here: 216 us
  waiting for transfers between devices  82 us (38%)
  local copies, waits for them, and re-layouts  35.1 us (16%)
  Pallas kernels  33.1 us (15%)
  blocking collectives  15.1 us (7%)
  between operations  13.9 us (6%)
  other arithmetic  13.7 us (6%)
  starting transfers between devices  13.6 us (6%)
  matrix products  9.71 us (4%)
    reduce_scatter x1, waiting for transfers between devices, per_device(): part = lax.psum_scatter(part, 'z', scatter_dimension=2, tiled=True)  38.3 us
    pallas_call x1, Pallas kernels, etp_gather(): pl.pallas_call(functools.partial(_gather_kernel, nz, nx, nc), out_shape=j...  33.1 us
    reduce_scatter x1, waiting for transfers between devices, per_device(): part = lax.psum_scatter(part, 'core', scatter_dimension=0, tiled=True)  16.2 us
    all_to_all x1, blocking collectives, per_device(): recv = lax.all_to_all(sent, 'ep', 0, 0, tiled=True)  15.1 us
    reduce_scatter x1, waiting for transfers between devices, per_device(): part = lax.psum_scatter(part, 'x', scatter_dimension=1, tiled=True)  13.3 us
    reshape x2, local copies, waits for them, and re-layouts, per_device(): g = etp_gather(chunk, nz, nx, nc).reshape(nc, nx, nz, rows, 2 * width)  10.6 us
    all_to_all x1, waiting for transfers between devices, per_device(): lax.all_to_all(slot_gate.reshape(ep_count, CAP), 'ep', 0, 0, tiled=True)  7.54 us
    all_to_all x1, starting transfers between devices, per_device(): lax.all_to_all(slot_gate.reshape(ep_count, CAP), 'ep', 0, 0, tiled=True)  6.75 us
  transfers between devices with their start and end apart: 5, of which 5 were waited for; matrix products, arithmetic and copies ran while one was open for 6% of the time, Pallas kernels for 0%

profile of v2, /device:TPU:6, one launch (start us, length us, event | category | flops | bytes accessed | tf_op | source)
XLA Modules:
  0.0 216.4 jit_solution(7490228371907195406)
XLA Ops:
  7.2 0.0 copy-start
  7.2 0.0 reduce-scatter.4.cloned.1.call-start
  7.2 0.7 broadcast_multiply_fusion
  8.0 0.8 copy.38
  8.7 0.1 copy.37
  8.8 0.1 mul.71
  9.0 0.1 eq.15
  9.1 0.1 fusion.15
  9.2 0.1 reduce_window_sum.11
  9.3 0.2 select_reduce_fusion
  9.5 0.9 scatter_custom_fusion
  10.4 0.8 fusion.19
  11.2 0.8 gather_fusion
  12.0 15.1 %all_to_all.19 = bf16[8,24,96]{2,1,0:T(8,128)(2,1)S(1)} all-to-all(bf16[8,24,96]{2,1,0:T(8,128)(2,1)S(1)} %bitcast.64), channel_id=1, replica_groups=mesh['ep'=8,'z'=8,'x'=4,'core'=2] {'ep'}, dimensions={0} | all-to-all | bytes 73728 | tf_op jit(solution)/shard_map/all_to_all | solution.py:118
  27.1 0.7 reshape.88.chunk_ref
  27.8 33.1 %shard_map.110 = bf16[2,4,8,144,128]{4,3,2,1,0:T(8,128)(2,1)} custom-call(bf16[144,128]{1,0:T(8,128)(2,1)} %reshape.88.chunk_ref), custom_call_target="tpu_custom_call" | custom-call | tf_op jit(solution)/shard_map/pallas_call | solution.py:79
  61.0 5.8 %reshape.89 = bf16[2,4,8,192,96]{4,3,2,1,0:T(8,128)(2,1)} reshape(bf16[2,4,8,144,128]{4,3,2,1,0:T(8,128)(2,1)} %shard_map.110) | data formatting | bytes 4718592 | tf_op jit(solution)/shard_map/reshape | solution.py:123
  66.8 4.8 %copy.39 = bf16[2,4,8,192,96]{3,4,0,1,2:T(8,128)(2,1)} copy(bf16[2,4,8,192,96]{4,3,2,1,0:T(8,128)(2,1)} %reshape.89) | data formatting | bytes 4718592 | tf_op jit(solution)/shard_map/reshape | solution.py:123
  71.6 4.1 %slice_convert_fusion = (f32[192,8,4,2,48]{0,4,3,2,1:T(8,128)}, bf16[192,8,4,2,48]{0,4,3,2,1:T(8,128)(2,1)S(1)}) fusion(bf16[192,8,4,2,96]{0,4,3,2,1:T(8,128)(2,1)} %bitcast.56), kind=kLoop, calls=%fused_computation.14 | loop fusion | flops 589824 | bytes 5898240 | tf_op jit(solution)/shard_map/convert_element_type | solution.py:141
  75.7 3.4 %copy.41 = f32[192,3072]{1,0:T(8,128)} copy(f32[192,3072]{0,1:T(8,128)} %bitcast.50) | data formatting | bytes 4718592 | tf_op jit(solution)/shard_map/convert_element_type | solution.py:141
  79.2 0.0 copy-done.3
  79.2 0.6 fusion.10
  79.8 0.5 copy-done.5
  80.3 0.6 multiply_convert_fusion.5
  80.9 1.0 copy-done.2
  82.0 1.9 multiply_reduce_fusion
  83.8 3.5 %copy.40 = f32[192,3072]{0,1:T(8,128)} copy(f32[192,3072]{1,0:T(8,128)} %get-tuple-element.12) | data formatting | bytes 4718592 | tf_op jit(solution)/shard_map/dot_general | solution.py:134
  87.3 2.3 %pad_maximum_fusion = f32[2,4,8,192,49]{3,4,0,1,2:T(8,128)S(1)} fusion(f32[2,4,8,192,1]{3,4,0,1,2:T(1,128)S(1)} %broadcast_in_dim.31, f32[2,4,8,192,48]{3,4,0,1,2:T(8,128)} %bitcast.58), kind=kLoop, calls=%fused_computation.4 | loop fusion | flops 602112 | bytes 4816896 | tf_op jit(solution)/shard_map/concatenate | solution.py:145
  89.7 3.6 %copy.42 = f32[2,4,8,192,49]{3,2,4,1,0:T(8,128)} copy(f32[2,4,8,192,49]{3,4,0,1,2:T(8,128)S(1)} %pad_maximum_fusion) | data formatting | bytes 4816896 | tf_op jit(solution)/shard_map/concatenate | solution.py:145
  93.3 0.0 reduce-scatter.4.cloned.1.call-update
  93.3 0.0 copy-start.4
  93.4 0.0 reduce-scatter.6.cloned.1.call-start
  93.4 16.2 %reduce-scatter.4.cloned.1.call-done = f32[1,4,8,192,49]{3,2,4,1,0:T(8,128)} async-done(((f32[2,4,8,192,49]{3,2,4,1,0:T(8,128)}), f32[1,4,8,192,49]{3,2,4,1,0:T(8,128)}) %reduce-scatter.4.cloned.1.call-update) | async-done | bytes 1204240 | tf_op jit(solution)/shard_map/reduce_scatter | solution.py:146
  109.6 0.0 reduce-scatter.6.cloned.1.call-update
  109.6 0.1 copy.36
  109.7 0.1 reshape.95
  109.8 0.1 pad_maximum_fusion.1
  109.9 1.6 gather_fusion.2
  111.4 0.7 all_to_all.14
  112.1 6.7 %all-to-all-start.2 = ((f32[8,1,24]{2,1,0:T(1,128)}), f32[8,1,24]{2,1,0:T(1,128)S(1)}, u32[]{:S(2)}, u32[]{:S(2)}) async-start(f32[8,1,24]{2,1,0:T(1,128)} %all_to_all.14), calls=%async_computation.5 | async-start | bytes 8192 | tf_op jit(solution)/shard_map/all_to_all | solution.py:119
  118.9 0.0 reduce-scatter.8.cloned.1.call-start
  118.9 7.5 %all-to-all-done.2 = f32[8,1,24]{2,1,0:T(1,128)S(1)} async-done(((f32[8,1,24]{2,1,0:T(1,128)}), f32[8,1,24]{2,1,0:T(1,128)S(1)}, u32[]{:S(2)}, u32[]{:S(2)}) %all-to-all-start.2) | async-done | bytes 800 | tf_op jit(solution)/shard_map/all_to_all | solution.py:119
  126.5 0.5 broadcast.83
  127.0 0.7 reduce.3
  127.7 0.1 mul.77
  127.7 3.1 %multiply_convert_fusion.1 = bf16[192,8,4,2,48]{0,4,3,2,1:T(8,128)(2,1)} fusion(f32[192]{0:T(256)S(1)} %mul.77, bf16[192,8,4,2,96]{0,4,3,2,1:T(8,128)(2,1)} %bitcast.57), kind=kLoop, calls=%fused_computation.12 | loop fusion | flops 1769472 | bytes 2360064 | tf_op jit(solution)/shard_map/convert_element_type | solution.py:128
  130.8 13.3 %reduce-scatter.6.cloned.1.call-done = f32[1,1,8,192,49]{3,2,4,0,1:T(8,128)} async-done(((f32[1,4,8,192,49]{3,2,4,0,1:T(8,128)}), f32[1,1,8,192,49]{3,2,4,0,1:T(8,128)}) %reduce-scatter.6.cloned.1.call-update) | async-done | bytes 301072 | tf_op jit(solution)/shard_map/reduce_scatter | solution.py:147
  144.1 2.2 %copy.44 = f32[1,1,8,192,49]{4,3,2,1,0:T(8,128)} copy(f32[1,1,8,192,49]{3,2,4,0,1:T(8,128)} %reduce-scatter.6.cloned.1.call-done) | data formatting | bytes 602112 | tf_op jit(solution)/shard_map/reduce_scatter | solution.py:147
  146.3 0.0 reduce-scatter.8.cloned.1.call-update
  146.4 2.1 fusion.4
  148.5 1.5 fusion
  150.0 1.6 fusion.2
  151.5 38.3 %reduce-scatter.8.cloned.1.call-done = f32[1,1,1,192,49]{4,3,2,1,0:T(8,128)} async-done(((f32[1,1,8,192,49]{4,3,2,1,0:T(8,128)}), f32[1,1,1,192,49]{4,3,2,1,0:T(8,128)}) %reduce-scatter.8.cloned.1.call-update) | async-done | bytes 37648 | tf_op jit(solution)/shard_map/reduce_scatter | solution.py:148
  189.9 1.6 reshape.142
  191.5 6.7 %all-to-all-start.1 = ((f32[8,1,1176]{2,1,0:T(1,128)}), f32[8,1,1176]{2,1,0:T(1,128)S(1)}, u32[]{:S(2)}, u32[]{:S(2)}) async-start(f32[8,1,1176]{2,1,0:T(1,128)} %reshape.142), calls=%async_computation.4 | async-start | bytes 81920 | tf_op jit(solution)/shard_map/all_to_all | solution.py:150
  198.2 1.5 fusion.1
  199.7 6.7 %all-to-all-done.1 = f32[8,1,1176]{2,1,0:T(1,128)S(1)} async-done(((f32[8,1,1176]{2,1,0:T(1,128)}), f32[8,1,1176]{2,1,0:T(1,128)S(1)}, u32[]{:S(2)}, u32[]{:S(2)}) %all-to-all-start.1) | async-done | bytes 37664 | tf_op jit(solution)/shard_map/all_to_all | solution.py:150
  206.4 0.5 broadcast.84
  206.9 0.7 reduce.4
  207.6 0.1 reshape.143
  207.7 0.6 gather_fusion.1
  208.3 0.7 fusion.13
  209.1 0.1 slice.25
  209.2 0.7 copy.47
  (13 shorter events, 0.1 us)
Async XLA Ops:
  7.2 73.8 %copy-start = (bf16[1,128,3072]{2,1,0:T(8,128)(2,1)S(1)}, bf16[1,128,3072]{2,1,0:T(8,128)(2,1)}, u32[]{:S(2)}) copy-start(bf16[1,128,3072]{2,1,0:T(8,128)(2,1)} %param.13) | copy-start | bytes 2359300
  7.2 102.4 %reduce-scatter.4.cloned.1.call-start = ((), (), s32[]{:S(2)}) async-start(), calls=%async_computation.6 | async-start | bytes 4816896 | tf_op jit(solution)/shard_map/reduce_scatter | solution.py:146
  75.7 3.5 %copy-start.3 = (bf16[1,3072,128]{2,1,0:T(8,128)(2,1)S(1)}, bf16[1,3072,128]{2,1,0:T(8,128)(2,1)}, u32[]{:S(2)}) copy-start(bf16[1,3072,128]{2,1,0:T(8,128)(2,1)} %param.11) | copy-start | bytes 2359300
  79.2 1.1 copy-start.5
  80.3 1.7 copy-start.2
  93.3 16.2 %copy-start.4 = (f32[48,2]{0,1:T(2,128)S(1)}, f32[48,2]{0,1:T(2,128)}, u32[]{:S(2)}) copy-start(f32[48,2]{0,1:T(2,128)} %param.9) | copy-start | bytes 1156
  93.4 50.8 %reduce-scatter.6.cloned.1.call-start = ((), (), s32[]{:S(2)}) async-start(), calls=%async_computation.7 | async-start | bytes 2007040 | tf_op jit(solution)/shard_map/reduce_scatter | solution.py:147
  112.1 14.4 %all-to-all-start.2 = ((f32[8,1,24]{2,1,0:T(1,128)}), f32[8,1,24]{2,1,0:T(1,128)S(1)}, u32[]{:S(2)}, u32[]{:S(2)}) async-start(f32[8,1,24]{2,1,0:T(1,128)} %all_to_all.14), calls=%async_computation.5 | async-start | bytes 8192 | tf_op jit(solution)/shard_map/all_to_all | solution.py:119
  118.9 71.0 %reduce-scatter.8.cloned.1.call-start = ((), (), s32[]{:S(2)}) async-start(), calls=%async_computation.8 | async-start | bytes 884736 | tf_op jit(solution)/shard_map/reduce_scatter | solution.py:148
  146.3 3.6 %copy-start.1 = (f32[192,8,4,2,48]{0,4,3,2,1:T(8,128)S(1)}, f32[192,8,4,2,48]{0,4,3,2,1:T(8,128)}, u32[]{:S(2)}) copy-start(f32[192,8,4,2,48]{0,4,3,2,1:T(8,128)} %get-tuple-element.5) | copy-start | bytes 7077892
  191.5 14.8 %all-to-all-start.1 = ((f32[8,1,1176]{2,1,0:T(1,128)}), f32[8,1,1176]{2,1,0:T(1,128)S(1)}, u32[]{:S(2)}, u32[]{:S(2)}) async-start(f32[8,1,1176]{2,1,0:T(1,128)} %reshape.142), calls=%async_computation.4 | async-start | bytes 81920 | tf_op jit(solution)/shard_map/all_to_all | solution.py:150
Sparse Core Ops, SparseCore 0:
  93.5 16.0 reduce-scatter.3
  112.6 31.4 reduce-scatter.5
  147.8 42.0 reduce-scatter.7

commit v3 on v2

--- a/solution.py
+++ b/solution.py
@@ -92,6 +92,124 @@
         ],
         compiler_params=pltpu.CompilerParams(collective_id=0, has_side_effects=True),
     )(chunk)
+
+
+def _rs_kernel(ne, nz, nx, nc, blk, part_ref, out_ref, recv_c, acc1, recv_b, acc2, recv_a, fin,
+               sem_local, send_c, rsem_c, send_b, rsem_b, send_a, rsem_a, send_d, rsem_d):
+    e = lax.axis_index("ep")
+    z = lax.axis_index("z")
+    x = lax.axis_index("x")
+    c = lax.axis_index("core")
+    mesh_id = pl.DeviceIdType.MESH
+    barrier = pltpu.get_barrier_semaphore()
+    for d in range(1, nz):
+        pl.semaphore_signal(barrier, inc=1, device_id=(e, (z + d) % nz, x, c), device_id_type=mesh_id)
+    for d in range(1, nx):
+        pl.semaphore_signal(barrier, inc=1, device_id=(e, z, (x + d) % nx, c), device_id_type=mesh_id)
+    for d in range(1, nc):
+        pl.semaphore_signal(barrier, inc=1, device_id=(e, z, x, (c + d) % nc), device_id_type=mesh_id)
+    for d in range(1, ne):
+        pl.semaphore_signal(barrier, inc=1, device_id=((e + d) % ne, z, x, c), device_id_type=mesh_id)
+    pl.semaphore_wait(barrier, (nz - 1) + (nx - 1) + (nc - 1) + (ne - 1))
+    sends = []
+
+    for d in range(1, nc):
+        cp = pltpu.make_async_remote_copy(
+            part_ref.at[(c + d) % nc], recv_c.at[d - 1], send_c.at[d - 1], rsem_c.at[d - 1],
+            device_id=(e, z, x, (c + d) % nc), device_id_type=mesh_id)
+        cp.start()
+        sends.append(cp)
+    for d in range(1, nc):
+        pltpu.make_async_remote_copy(
+            part_ref.at[c], recv_c.at[d - 1], send_c.at[d - 1], rsem_c.at[d - 1],
+            device_id=(e, z, x, (c + nc - d) % nc), device_id_type=mesh_id).wait_recv()
+    for i in range(nx):
+        total = part_ref[c, i]
+        for d in range(1, nc):
+            total = total + recv_c[d - 1, i]
+        acc1[i] = total
+
+    for d in range(1, nx):
+        cp = pltpu.make_async_remote_copy(
+            acc1.at[(x + d) % nx], recv_b.at[d - 1], send_b.at[d - 1], rsem_b.at[d - 1],
+            device_id=(e, z, (x + d) % nx, c), device_id_type=mesh_id)
+        cp.start()
+        sends.append(cp)
+    for d in range(1, nx):
+        pltpu.make_async_remote_copy(
+            acc1.at[x], recv_b.at[d - 1], send_b.at[d - 1], rsem_b.at[d - 1],
+            device_id=(e, z, (x + nx - d) % nx, c), device_id_type=mesh_id).wait_recv()
+    total = acc1[x]
+    for d in range(1, nx):
+        total = total + recv_b[d - 1]
+    acc2[...] = total
+
+    for d in range(1, nz):
+        cp = pltpu.make_async_remote_copy(
+            acc2.at[(z + d) % nz], recv_a.at[d - 1], send_a.at[d - 1], rsem_a.at[d - 1],
+            device_id=(e, (z + d) % nz, x, c), device_id_type=mesh_id)
+        cp.start()
+        sends.append(cp)
+    for d in range(1, nz):
+        pltpu.make_async_remote_copy(
+            acc2.at[z], recv_a.at[d - 1], send_a.at[d - 1], rsem_a.at[d - 1],
+            device_id=(e, (z + nz - d) % nz, x, c), device_id_type=mesh_id).wait_recv()
+    total = acc2[z]
+    for d in range(1, nz):
+        total = total + recv_a[d - 1]
+
+    pad_rows = fin.shape[1]
+    for b in range(ne):
+        fin[b, :blk] = total[b * blk:(b + 1) * blk]
+        fin[b, blk:] = jnp.zeros((pad_rows - blk, total.shape[1]), total.dtype)
+    local = pltpu.make_async_copy(fin.at[e], out_ref.at[e], sem_local.at[0])
+    local.start()
+    for d in range(1, ne):
+        cp = pltpu.make_async_remote_copy(
+            fin.at[(e + d) % ne], out_ref.at[e], send_d.at[d - 1], rsem_d.at[e],
+            device_id=((e + d) % ne, z, x, c), device_id_type=mesh_id)
+        cp.start()
+        sends.append(cp)
+    for d in range(1, ne):
+        src = (e + ne - d) % ne
+        pltpu.make_async_remote_copy(
+            fin.at[e], out_ref.at[src], send_d.at[d - 1], rsem_d.at[src],
+            device_id=(src, z, x, c), device_id_type=mesh_id).wait_recv()
+    local.wait()
+    for cp in sends:
+        cp.wait_send()
+
+
+def etp_reduce_scatter(part, ne, blk):
+    nc, nx, nz, rows, lanes = part.shape
+    pad_rows = -(-blk // 8) * 8
+    f32 = jnp.float32
+    vmem = pltpu.VMEM
+    dma = pltpu.SemaphoreType.DMA
+    return pl.pallas_call(
+        functools.partial(_rs_kernel, ne, nz, nx, nc, blk),
+        out_shape=jax.ShapeDtypeStruct((ne, pad_rows, lanes), f32),
+        in_specs=[pl.BlockSpec(memory_space=vmem)],
+        out_specs=pl.BlockSpec(memory_space=vmem),
+        scratch_shapes=[
+            pltpu.VMEM((max(nc - 1, 1), nx, nz, rows, lanes), f32),
+            pltpu.VMEM((nx, nz, rows, lanes), f32),
+            pltpu.VMEM((max(nx - 1, 1), nz, rows, lanes), f32),
+            pltpu.VMEM((nz, rows, lanes), f32),
+            pltpu.VMEM((max(nz - 1, 1), rows, lanes), f32),
+            pltpu.VMEM((ne, pad_rows, lanes), f32),
+            dma((1,)),
+            dma((max(nc - 1, 1),)),
+            dma((max(nc - 1, 1),)),
+            dma((max(nx - 1, 1),)),
+            dma((max(nx - 1, 1),)),
+            dma((max(nz - 1, 1),)),
+            dma((max(nz - 1, 1),)),
+            dma((max(ne - 1, 1),)),
+            dma((ne,)),
+        ],
+        compiler_params=pltpu.CompilerParams(collective_id=1, has_side_effects=True),
+    )(part)
 
 
 def per_device(tokens, routes, route_gates, cotangent, w_gate, w_up, w_down):
@@ -139,15 +257,17 @@
     grad_gate_w = lax.dot_general(rows_x, d_gate, (((0,), (0,)), ((), ())), preferred_element_type=jnp.float32)
     grad_up_w = lax.dot_general(rows_x, d_up, (((0,), (0,)), ((), ())), preferred_element_type=jnp.float32)
     inner = jnp.sum(output_part * cot_rows.astype(jnp.float32), axis=1)
-    part = output_part.reshape(rows, nz, nx, nc, width)
-    part = jnp.transpose(part, (3, 2, 1, 0, 4))
-    extra = jnp.broadcast_to(inner[None, None, None, :, None], (nc, nx, nz, rows, 1))
-    part = jnp.concatenate([part, extra], axis=4)
-    part = lax.psum_scatter(part, "core", scatter_dimension=0, tiled=True)
-    part = lax.psum_scatter(part, "x", scatter_dimension=1, tiled=True)
-    part = lax.psum_scatter(part, "z", scatter_dimension=2, tiled=True)
-    back = part.reshape(ep_count, CAP, width + 1)
-    returned = lax.all_to_all(back, "ep", 0, 0, tiled=True).reshape(EXPERTS * CAP, width + 1)
+    lanes = 128
+    blk_elems = CAP * (width + 1)
+    blk = -(-blk_elems // lanes)
+    part = output_part.reshape(ep_count, CAP, nz, nx, nc, width)
+    part = jnp.transpose(part, (4, 3, 2, 0, 1, 5))
+    extra = jnp.broadcast_to(inner.reshape(1, 1, 1, ep_count, CAP, 1), (nc, nx, nz, ep_count, CAP, 1))
+    part = jnp.concatenate([part, extra], axis=5).reshape(nc, nx, nz, ep_count, blk_elems)
+    part = jnp.pad(part, ((0, 0),) * 4 + ((0, blk * lanes - blk_elems),))
+    part = part.reshape(nc, nx, nz, ep_count * blk, lanes)
+    back = etp_reduce_scatter(part, ep_count, blk)
+    returned = back[:, :blk].reshape(ep_count, blk * lanes)[:, :blk_elems].reshape(EXPERTS * CAP, width + 1)
     pair_rows = returned[target].reshape(tok_count, 2, width + 1)
     mixed = jnp.sum(route_gates[:, :, None] * pair_rows[:, :, :width], axis=1).astype(jnp.bfloat16)
     grad_gates = pair_rows[:, :, width]

time: 217 us -> 198 us (0.912)
  waiting for transfers between devices: 82 us -> 12.3 us
  Pallas kernels: 33.1 us -> 74.9 us
  local copies, waits for them, and re-layouts: 35.1 us -> 63.7 us
  blocking collectives: 15.1 us -> 0 us
  between operations: 13.9 us -> 0.8 us
  other arithmetic: 13.7 us -> 24.9 us
  starting transfers between devices: 13.6 us -> 10.4 us
    reduce_scatter x3 -> x0, waiting for transfers between devices: 67.8 us -> none  [the longest x1 38.3 us: per_device(): part = lax.psum_scatter(part, 'z', scatter_dimension=2, tiled=True)]
    pallas_call x0 -> x1, Pallas kernels: none -> 42.7 us  [etp_reduce_scatter(): pl.pallas_call(functools.partial(_rs_kernel, ne, nz, nx, nc, blk), out_sh...]
    reshape x0 -> x4, local copies, waits for them, and re-layouts: none -> 21.5 us  [the longest x1 12.2 us: per_device(): part = output_part.reshape(ep_count, CAP, nz, nx, nc, width)]
    all_to_all x1 -> x0, blocking collectives: 15.1 us -> none  [per_device(): recv = lax.all_to_all(sent, 'ep', 0, 0, tiled=True)]
    concatenate x1, other arithmetic: 2.34 us -> 15.6 us  [per_device(): jnp.concatenate([part, extra], axis=5)]
    concatenate x1, local copies, waits for them, and re-layouts: 3.64 us -> 9.3 us  [per_device(): jnp.concatenate([part, extra], axis=5)]
    broadcast_in_dim x1 -> x2, local copies, waits for them, and re-layouts: 0.03 us -> 4.38 us  [per_device(): jnp.broadcast_to(inner.reshape(1, 1, 1, ep_count, CAP, 1), (nc, nx, nz, e...]
    dot_general x1 -> x0, local copies, waits for them, and re-layouts: 3.46 us -> none  [per_device(): output_part = jnp.dot(hidden, wd, preferred_element_type=jnp.float32)]
  transfers between devices with their start and end apart: 5 -> 2, of which waited for: 5 -> 2; matrix products, arithmetic and copies ran while one was open for 6% -> 2% of each run, Pallas kernels for 0% -> 0%
where the time goes in v3:
time: 198 us; the launch traced here: 197 us
  Pallas kernels  74.9 us (38%)
  local copies, waits for them, and re-layouts  63.7 us (32%)
  other arithmetic  24.9 us (13%)
  waiting for transfers between devices  12.3 us (6%)
  starting transfers between devices  10.4 us (5%)
  matrix products  9.6 us (5%)
    pallas_call x1, Pallas kernels, etp_reduce_scatter(): pl.pallas_call(functools.partial(_rs_kernel, ne, nz, nx, nc, blk), out_sh...  42.7 us
    pallas_call x1, Pallas kernels, etp_gather(): pl.pallas_call(functools.partial(_gather_kernel, nz, nx, nc), out_shape=j...  32.1 us
    concatenate x1, other arithmetic, per_device(): jnp.concatenate([part, extra], axis=5)  15.6 us
    reshape x1, local copies, waits for them, and re-layouts, per_device(): part = output_part.reshape(ep_count, CAP, nz, nx, nc, width)  12.2 us
    reshape x2, local copies, waits for them, and re-layouts, per_device(): g = etp_gather(chunk, nz, nx, nc).reshape(nc, nx, nz, rows, 2 * width)  10.6 us
    concatenate x1, local copies, waits for them, and re-layouts, per_device(): jnp.concatenate([part, extra], axis=5)  9.3 us
    all_to_all x1, starting transfers between devices, per_device(): lax.all_to_all(slot_gate.reshape(ep_count, CAP), 'ep', 0, 0, tiled=True)  7.1 us
    all_to_all x1, waiting for transfers between devices, per_device(): recv = lax.all_to_all(sent, 'ep', 0, 0, tiled=True)  6.85 us
  transfers between devices with their start and end apart: 2, of which 2 were waited for; matrix products, arithmetic and copies ran while one was open for 2% of the time, Pallas kernels for 0%

profile of v3, /device:TPU:6, one launch (start us, length us, event | category | flops | bytes accessed | tf_op | source)
XLA Modules:
  0.0 196.6 jit_solution(11783405267018711329)
XLA Ops:
  0.6 0.0 copy-start
  0.6 0.8 broadcast_multiply_fusion
  1.4 0.8 copy.21
  2.2 0.1 copy.20
  2.3 0.1 mul.71
  2.4 0.8 copy.19
  3.1 0.1 reshape.104
  3.3 0.1 eq.15
  3.4 0.1 fusion.15
  3.5 0.1 reduce_window_sum.11
  3.6 0.2 select_reduce_fusion
  3.8 0.9 scatter_custom_fusion
  4.7 0.1 pad_maximum_fusion.1
  4.8 1.5 gather_fusion.2
  6.4 0.7 all_to_all.10
  7.0 7.1 %all-to-all-start.1 = ((f32[8,1,24]{2,1,0:T(1,128)}), f32[8,1,24]{2,1,0:T(1,128)S(1)}, u32[]{:S(2)}, u32[]{:S(2)}) async-start(f32[8,1,24]{2,1,0:T(1,128)} %all_to_all.10), calls=%async_computation.1 | async-start | bytes 8192 | tf_op jit(solution)/shard_map/all_to_all | solution.py:237
  14.1 0.8 fusion.19
  14.9 1.4 gather_fusion
  16.3 5.4 %all-to-all-done.1 = f32[8,1,24]{2,1,0:T(1,128)S(1)} async-done(((f32[8,1,24]{2,1,0:T(1,128)}), f32[8,1,24]{2,1,0:T(1,128)S(1)}, u32[]{:S(2)}, u32[]{:S(2)}) %all-to-all-start.1) | async-done | bytes 800 | tf_op jit(solution)/shard_map/all_to_all | solution.py:237
  21.7 3.3 %all-to-all-start = ((bf16[8,24,96]{2,1,0:T(8,128)(2,1)}), bf16[8,24,96]{2,1,0:T(8,128)(2,1)S(1)}, u32[]{:S(2)}, u32[]{:S(2)}) async-start(bf16[8,24,96]{2,1,0:T(8,128)(2,1)} %bitcast.2), calls=%async_computation | async-start | bytes 98304 | tf_op jit(solution)/shard_map/all_to_all | solution.py:236
  25.1 0.5 broadcast.84
  25.6 0.7 reduce.3
  26.3 0.1 mul.77
  26.4 6.8 %all-to-all-done = bf16[8,24,96]{2,1,0:T(8,128)(2,1)S(1)} async-done(((bf16[8,24,96]{2,1,0:T(8,128)(2,1)}), bf16[8,24,96]{2,1,0:T(8,128)(2,1)S(1)}, u32[]{:S(2)}, u32[]{:S(2)}) %all-to-all-start) | async-done | bytes 36896 | tf_op jit(solution)/shard_map/all_to_all | solution.py:236
  33.2 0.7 reshape.95.chunk_ref
  34.0 32.1 %shard_map.110 = bf16[2,4,8,144,128]{4,3,2,1,0:T(8,128)(2,1)} custom-call(bf16[144,128]{1,0:T(8,128)(2,1)} %reshape.95.chunk_ref), custom_call_target="tpu_custom_call" | custom-call | tf_op jit(solution)/shard_map/pallas_call | solution.py:79
  66.1 5.8 %reshape.96 = bf16[2,4,8,192,96]{4,3,2,1,0:T(8,128)(2,1)} reshape(bf16[2,4,8,144,128]{4,3,2,1,0:T(8,128)(2,1)} %shard_map.110) | data formatting | bytes 4718592 | tf_op jit(solution)/shard_map/reshape | solution.py:241
  71.9 4.8 %copy.22 = bf16[2,4,8,192,96]{3,4,0,1,2:T(8,128)(2,1)} copy(bf16[2,4,8,192,96]{4,3,2,1,0:T(8,128)(2,1)} %reshape.96) | data formatting | bytes 4718592 | tf_op jit(solution)/shard_map/reshape | solution.py:241
  76.8 0.0 copy-start.2
  76.8 4.3 %slice_convert_fusion = (f32[192,8,4,2,48]{0,4,3,2,1:T(8,128)}, bf16[192,8,4,2,48]{0,4,3,2,1:T(8,128)(2,1)S(1)}) fusion(bf16[192,8,4,2,96]{0,4,3,2,1:T(8,128)(2,1)} %bitcast.62), kind=kLoop, calls=%fused_computation.14 | loop fusion | flops 589824 | bytes 5898240 | tf_op jit(solution)/shard_map/convert_element_type | solution.py:259
  81.0 0.0 copy-done.2
  81.0 1.6 multiply_convert_fusion.1
  82.6 0.0 copy-start.4
  82.6 3.5 %copy.23 = f32[192,3072]{1,0:T(8,128)} copy(f32[192,3072]{0,1:T(8,128)} %bitcast.55) | data formatting | bytes 4718592 | tf_op jit(solution)/shard_map/convert_element_type | solution.py:259
  86.0 0.0 copy-start.5
  86.0 0.0 copy-done.4
  86.0 0.0 copy-start.1
  86.0 0.6 fusion.10
  86.7 0.5 copy-done.5
  87.2 0.6 multiply_convert_fusion.5
  87.8 0.0 copy-start.3
  87.8 0.4 copy-done.1
  88.2 1.6 fusion.2
  89.7 0.0 copy-done
  89.7 0.0 copy-done.3
  89.7 1.9 multiply_reduce_fusion
  91.6 0.1 broadcast_in_dim.32
  91.7 12.2 %reshape.98 = f32[8,24,8,4,2,48]{5,4,3,2,1,0:T(2,128)} reshape(f32[192,3072]{1,0:T(8,128)} %get-tuple-element.12) | data formatting | bytes 4718592 | tf_op jit(solution)/shard_map/reshape | solution.py:263
  103.9 4.3 %broadcast_in_dim.33 = f32[2,4,8,8,24,1]{5,0,1,2,4,3:T(2,128)} broadcast(f32[8,24]{1,0:T(8,128)S(1)} %broadcast_in_dim.32), dimensions={3,4} | broadcast | bytes 49920 | tf_op jit(solution)/shard_map/broadcast_in_dim | solution.py:265
  108.2 15.6 %pad_maximum_fusion = f32[2,4,8,8,24,49]{5,0,1,2,4,3:T(2,128)} fusion(f32[2,4,8,8,24,1]{5,0,1,2,4,3:T(2,128)} %broadcast_in_dim.33, f32[2,4,8,8,24,48]{5,0,1,2,4,3:T(2,128)} %bitcast.57), kind=kLoop, calls=%fused_computation.4 | loop fusion | flops 602112 | bytes 4816896 | tf_op jit(solution)/shard_map/concatenate | solution.py:266
  123.8 9.3 %copy.24 = f32[2,4,8,8,24,49]{5,4,3,2,1,0:T(8,128)} copy(f32[2,4,8,8,24,49]{5,0,1,2,4,3:T(2,128)} %pad_maximum_fusion) | data formatting | bytes 4816896 | tf_op jit(solution)/shard_map/concatenate | solution.py:266
  133.1 5.7 %reshape.99 = f32[2,4,8,8,1176]{4,3,2,1,0:T(8,128)} reshape(f32[2,4,8,8,24,49]{5,4,3,2,1,0:T(8,128)} %copy.24) | data formatting | bytes 4816896 | tf_op jit(solution)/shard_map/reshape | solution.py:266
  138.8 3.4 %pad.5 = f32[2,4,8,8,1280]{4,3,2,1,0:T(8,128)} pad(f32[2,4,8,8,1176]{4,3,2,1,0:T(8,128)} %reshape.99, f32[]{:T(128)} %constant.40.clone.1), padding=0_0x0_0x0_0x0_0x0_104 | pad | bytes 5029892 | tf_op jit(solution)/shard_map/jit(_pad)/pad | solution.py:267
  142.2 3.6 %reshape.100.part_ref = f32[2,4,8,80,128]{4,3,2,1,0:T(8,128)} reshape(f32[2,4,8,8,1280]{4,3,2,1,0:T(8,128)} %pad.5) | data formatting | bytes 5242880 | tf_op jit(solution)/shard_map/reshape | solution.py:268
  145.8 42.7 %shard_map.111 = f32[8,16,128]{2,1,0:T(8,128)} custom-call(f32[2,4,8,80,128]{4,3,2,1,0:T(8,128)} %reshape.100.part_ref), custom_call_target="tpu_custom_call" | custom-call | tf_op jit(solution)/shard_map/pallas_call | solution.py:189
  188.6 0.8 slice_bitcast_fusion
  189.4 0.1 reshape.102
  189.6 0.6 gather_fusion.1
  190.2 0.7 fusion.13
  190.9 0.1 slice.34
  191.0 2.0 %fusion.4 = f32[192,128]{1,0:T(8,128)S(1)} fusion(bf16[192,3072]{0,1:T(8,128)(2,1)} %bitcast.64, bf16[1,128,3072]{2,1,0:T(8,128)(2,1)S(1)} %copy-done), kind=kOutput, calls=%fused_computation.16 | convolution fusion | flops 150994944 | bytes 2064384 | tf_op jit(solution)/shard_map/dot_general | solution.py:253
  193.0 1.5 fusion.1
  194.5 1.5 fusion
  196.0 0.6 copy.27
  (6 shorter events, 0.0 us)
Async XLA Ops:
  0.6 89.1 %copy-start = (bf16[1,128,3072]{2,1,0:T(8,128)(2,1)S(1)}, bf16[1,128,3072]{2,1,0:T(8,128)(2,1)}, u32[]{:S(2)}) copy-start(bf16[1,128,3072]{2,1,0:T(8,128)(2,1)} %param.13) | copy-start | bytes 2359300
  7.0 14.7 %all-to-all-start.1 = ((f32[8,1,24]{2,1,0:T(1,128)}), f32[8,1,24]{2,1,0:T(1,128)S(1)}, u32[]{:S(2)}, u32[]{:S(2)}) async-start(f32[8,1,24]{2,1,0:T(1,128)} %all_to_all.10), calls=%async_computation.1 | async-start | bytes 8192 | tf_op jit(solution)/shard_map/all_to_all | solution.py:237
  21.7 11.5 %all-to-all-start = ((bf16[8,24,96]{2,1,0:T(8,128)(2,1)}), bf16[8,24,96]{2,1,0:T(8,128)(2,1)S(1)}, u32[]{:S(2)}, u32[]{:S(2)}) async-start(bf16[8,24,96]{2,1,0:T(8,128)(2,1)} %bitcast.2), calls=%async_computation | async-start | bytes 98304 | tf_op jit(solution)/shard_map/all_to_all | solution.py:236
  76.8 4.3 %copy-start.2 = (bf16[2,4,8,192,96]{3,4,0,1,2:T(8,128)(2,1)S(1)}, bf16[2,4,8,192,96]{3,4,0,1,2:T(8,128)(2,1)}, u32[]{:S(2)}) copy-start(bf16[2,4,8,192,96]{3,4,0,1,2:T(8,128)(2,1)} %copy.22) | copy-start | bytes 7077892
  82.6 3.5 %copy-start.4 = (bf16[1,3072,128]{2,1,0:T(8,128)(2,1)S(1)}, bf16[1,3072,128]{2,1,0:T(8,128)(2,1)}, u32[]{:S(2)}) copy-start(bf16[1,3072,128]{2,1,0:T(8,128)(2,1)} %param.11) | copy-start | bytes 2359300
  86.0 1.1 copy-start.5
  86.0 2.1 %copy-start.1 = (f32[192,8,4,2,48]{0,4,3,2,1:T(8,128)S(1)}, f32[192,8,4,2,48]{0,4,3,2,1:T(8,128)}, u32[]{:S(2)}) copy-start(f32[192,8,4,2,48]{0,4,3,2,1:T(8,128)} %get-tuple-element.5) | copy-start | bytes 7077892
  87.8 2.0 copy-start.3

commit v4 on v1

v4 whole, which is shorter than its diff:
```python
import functools

import jax
import jax.numpy as jnp
import numpy as np
from jax import lax
from jax.experimental import pallas as pl
from jax.experimental.pallas import tpu as pltpu
from jax.sharding import Mesh
from jax.sharding import PartitionSpec as P

EXPERTS = 8
CAP = 24
SUB = ("z", "x", "core")
MESH_ID = pl.DeviceIdType.MESH


def sub_sizes(etp):
    if etp % 8 == 0:
        return (etp // 8, 4, 2)
    return (etp, 1, 1)


def _coords():
    return (lax.axis_index("ep"), lax.axis_index("z"), lax.axis_index("x"), lax.axis_index("core"))


def _barrier(ne, nz, nx, nc, with_ep):
    e, z, x, c = _coords()
    barrier = pltpu.get_barrier_semaphore()
    count = 0
    for d in range(1, nz):
        pl.semaphore_signal(barrier, inc=1, device_id=(e, (z + d) % nz, x, c), device_id_type=MESH_ID)
        count += 1
    for d in range(1, nx):
        pl.semaphore_signal(barrier, inc=1, device_id=(e, z, (x + d) % nx, c), device_id_type=MESH_ID)
        count += 1
    for d in range(1, nc):
        pl.semaphore_signal(barrier, inc=1, device_id=(e, z, x, (c + d) % nc), device_id_type=MESH_ID)
        count += 1
    if with_ep:
        for d in range(1, ne):
            pl.semaphore_signal(barrier, inc=1, device_id=((e + d) % ne, z, x, c), device_id_type=MESH_ID)
            count += 1
    pl.semaphore_wait(barrier, count)


def _gather_kernel(nz, nx, nc, xa_ref, ca_ref, xo_ref, co_ref, sem_local, send_a, recv_a, send_b, recv_b, send_c, recv_c):
    e, z, x, c = _coords()
    _barrier(1, nz, nx, nc, False)
    pairs = ((xa_ref, xo_ref), (ca_ref, co_ref))
    locals_ = []
    for t, (src, out) in enumerate(pairs):
        cp = pltpu.make_async_copy(src, out.at[z, x, c], sem_local.at[t])
        cp.start()
        locals_.append(cp)
    sends = []
    for t, (src, out) in enumerate(pairs):
        for d in range(1, nz):
            cp = pltpu.make_async_remote_copy(
                src, out.at[z, x, c], send_a.at[t, d - 1], recv_a.at[t, d - 1],
                device_id=(e, (z + d) % nz, x, c), device_id_type=MESH_ID)
            cp.start()
            sends.append(cp)
    for t, (src, out) in enumerate(pairs):
        for d in range(1, nz):
            zs = (z + nz - d) % nz
            pltpu.make_async_remote_copy(
                src, out.at[zs, x, c], send_a.at[t, d - 1], recv_a.at[t, d - 1],
                device_id=(e, zs, x, c), device_id_type=MESH_ID).wait_recv()
    for cp in locals_:
        cp.wait()
    for t, (src, out) in enumerate(pairs):
        for d in range(1, nx):
            cp = pltpu.make_async_remote_copy(
                out.at[:, x, c], out.at[:, x, c], send_b.at[t, d - 1], recv_b.at[t, d - 1],
                device_id=(e, z, (x + d) % nx, c), device_id_type=MESH_ID)
            cp.start()
            sends.append(cp)
    for t, (src, out) in enumerate(pairs):
        for d in range(1, nx):
            xs = (x + nx - d) % nx
            pltpu.make_async_remote_copy(
                out.at[:, xs, c], out.at[:, xs, c], send_b.at[t, d - 1], recv_b.at[t, d - 1],
                device_id=(e, z, xs, c), device_id_type=MESH_ID).wait_recv()
    for t, (src, out) in enumerate(pairs):
        for d in range(1, nc):
            cp = pltpu.make_async_remote_copy(
                out.at[:, :, c], out.at[:, :, c], send_c.at[t, d - 1], recv_c.at[t, d - 1],
                device_id=(e, z, x, (c + d) % nc), device_id_type=MESH_ID)
            cp.start()
            sends.append(cp)
    for t, (src, out) in enumerate(pairs):
        for d in range(1, nc):
            cs = (c + nc - d) % nc
            pltpu.make_async_remote_copy(
                out.at[:, :, cs], out.at[:, :, cs], send_c.at[t, d - 1], recv_c.at[t, d - 1],
                device_id=(e, z, x, cs), device_id_type=MESH_ID).wait_recv()
    for cp in sends:
        cp.wait_send()


def etp_gather(xa, ca, nz, nx, nc):
    rows, cols = xa.shape
    vmem = pltpu.VMEM
    dma = pltpu.SemaphoreType.DMA
    shape = jax.ShapeDtypeStruct((nz, nx, nc, rows, cols), xa.dtype)
    return pl.pallas_call(
        functools.partial(_gather_kernel, nz, nx, nc),
        out_shape=(shape, shape),
        in_specs=[pl.BlockSpec(memory_space=vmem)] * 2,
        out_specs=(pl.BlockSpec(memory_space=vmem),) * 2,
        scratch_shapes=[
            dma((2,)),
            dma((2, max(nz - 1, 1))),
            dma((2, max(nz - 1, 1))),
            dma((2, max(nx - 1, 1))),
            dma((2, max(nx - 1, 1))),
            dma((2, max(nc - 1, 1))),
            dma((2, max(nc - 1, 1))),
        ],
        compiler_params=pltpu.CompilerParams(collective_id=0, has_side_effects=True),
    )(xa, ca)


def _rs_kernel(ne, nz, nx, nc, part_ref, inner_ref, out_ref, recv_c, acc1, recv_b, acc2, recv_a,
               ir_c, in1, ir_b, in2, ir_a, fin,
               sem_local, send_c, rsem_c, send_b, rsem_b, send_a, rsem_a, send_d, rsem_d):
    e, z, x, c = _coords()
    _barrier(ne, nz, nx, nc, True)
    sends = []

    def exchange(pieces, peers_of, send_sem, recv_sem):
        n = len(peers_of)
        for t, (src_of, dst) in enumerate(pieces):
            for d in range(n):
                cp = pltpu.make_async_remote_copy(
                    src_of(d), dst.at[d], send_sem.at[t, d], recv_sem.at[t, d],
                    device_id=peers_of[d][0], device_id_type=MESH_ID)
                cp.start()
                sends.append(cp)
        for t, (src_of, dst) in enumerate(pieces):
            for d in range(n):
                pltpu.make_async_remote_copy(
                    dst.at[d], dst.at[d], send_sem.at[t, d], recv_sem.at[t, d],
                    device_id=peers_of[d][1], device_id_type=MESH_ID).wait_recv()

    peers = [((e, z, x, (c + d) % nc), (e, z, x, (c + nc - d) % nc)) for d in range(1, nc)]
    exchange([(lambda d: part_ref.at[:, :, (c + d + 1) % nc], recv_c), (lambda d: inner_ref, ir_c)],
             peers, send_c, rsem_c)

    def sum_c(i, carry):
        zi = i // nx
        xi = i % nx
        total = part_ref[zi, xi, c]
        for d in range(nc - 1):
            total = total + recv_c[d, zi, xi]
        acc1[zi, xi] = total
        return carry
    lax.fori_loop(0, nz * nx, sum_c, 0)
    total = inner_ref[...]
    for d in range(nc - 1):
        total = total + ir_c[d]
    in1[...] = total

    peers = [((e, z, (x + d) % nx, c), (e, z, (x + nx - d) % nx, c)) for d in range(1, nx)]
    exchange([(lambda d: acc1.at[:, (x + d + 1) % nx], recv_b), (lambda d: in1, ir_b)],
             peers, send_b, rsem_b)

    def sum_b(zi, carry):
        total = acc1[zi, x]
        for d in range(nx - 1):
            total = total + recv_b[d, zi]
        acc2[zi] = total
        return carry
    lax.fori_loop(0, nz, sum_b, 0)
    total = in1[...]
    for d in range(nx - 1):
        total = total + ir_b[d]
    in2[...] = total

    peers = [((e, (z + d) % nz, x, c), (e, (z + nz - d) % nz, x, c)) for d in range(1, nz)]
    exchange([(lambda d: acc2.at[(z + d + 1) % nz], recv_a), (lambda d: in2, ir_a)],
             peers, send_a, rsem_a)
    total = acc2[z]
    for d in range(nz - 1):
        total = total + recv_a[d]
    itotal = in2[...]
    for d in range(nz - 1):
        itotal = itotal + ir_a[d]

    feats = total.shape[0]
    blk = fin.shape[2]
    for b in range(ne):
        fin[b, :feats, :] = total[:, b * blk:(b + 1) * blk]
        fin[b, feats:feats + 1, :] = itotal[:, b * blk:(b + 1) * blk]
        fin[b, feats + 1:, :] = jnp.zeros((fin.shape[1] - feats - 1, blk), jnp.float32)
    local = pltpu.make_async_copy(fin.at[e], out_ref.at[e], sem_local.at[0])
    local.start()
    for d in range(1, ne):
        cp = pltpu.make_async_remote_copy(
            fin.at[(e + d) % ne], out_ref.at[e], send_d.at[d - 1], rsem_d.at[e],
            device_id=((e + d) % ne, z, x, c), device_id_type=MESH_ID)
        cp.start()
        sends.append(cp)
    for d in range(1, ne):
        src = (e + ne - d) % ne
        pltpu.make_async_remote_copy(
            fin.at[e], out_ref.at[src], send_d.at[d - 1], rsem_d.at[src],
            device_id=(src, z, x, c), device_id_type=MESH_ID).wait_recv()
    local.wait()
    for cp in sends:
        cp.wait_send()


def etp_reduce_scatter(part, inner, ne, blk):
    nz, nx, nc, feats, cols = part.shape
    pad_rows = -(-(feats + 1) // 8) * 8
    f32 = jnp.float32
    vmem = pltpu.VMEM
    dma = pltpu.SemaphoreType.DMA
    mc, mx, mz = max(nc - 1, 1), max(nx - 1, 1), max(nz - 1, 1)
    return pl.pallas_call(
        functools.partial(_rs_kernel, ne, nz, nx, nc),
        out_shape=jax.ShapeDtypeStruct((ne, pad_rows, blk), f32),
        in_specs=[pl.BlockSpec(memory_space=vmem)] * 2,
        out_specs=pl.BlockSpec(memory_space=vmem),
        scratch_shapes=[
            pltpu.VMEM((mc, nz, nx, feats, cols), f32),
            pltpu.VMEM((nz, nx, feats, cols), f32),
            pltpu.VMEM((mx, nz, feats, cols), f32),
            pltpu.VMEM((nz, feats, cols), f32),
            pltpu.VMEM((mz, feats, cols), f32),
            pltpu.VMEM((mc, 1, cols), f32),
            pltpu.VMEM((1, cols), f32),
            pltpu.VMEM((mx, 1, cols), f32),
            pltpu.VMEM((1, cols), f32),
            pltpu.VMEM((mz, 1, cols), f32),
            pltpu.VMEM((ne, pad_rows, blk), f32),
            dma((1,)),
            dma((2, mc)),
            dma((2, mc)),
            dma((2, mx)),
            dma((2, mx)),
            dma((2, mz)),
            dma((2, mz)),
            dma((max(ne - 1, 1),)),
            dma((ne,)),
        ],
        compiler_params=pltpu.CompilerParams(collective_id=1, has_side_effects=True),
    )(part, inner)


def per_device(tokens, routes, route_gates, cotangent, w_gate, w_up, w_down):
    ep_count = lax.axis_size("ep")
    nz, nx, nc = lax.axis_size("z"), lax.axis_size("x"), lax.axis_size("core")
    tok_count, width = tokens.shape
    flat_ids = routes.reshape(-1)
    pair_count = flat_ids.shape[0]
    onehot = (flat_ids[:, None] == jnp.arange(EXPERTS, dtype=jnp.int32)[None, :]).astype(jnp.int32)
    before = jnp.cumsum(onehot, axis=0) - onehot
    slot_id = jnp.sum(before * onehot, axis=1)
    target = flat_ids * CAP + slot_id
    slot_table = (
        jnp.full((EXPERTS * CAP,), pair_count, jnp.int32)
        .at[target]
        .set(jnp.arange(pair_count, dtype=jnp.int32))
    )
    token_of_slot = slot_table // 2
    gate_flat = jnp.concatenate([route_gates.reshape(-1), jnp.zeros((1,), jnp.float32)])
    slot_gate = gate_flat[slot_table]
    xc = jnp.concatenate([tokens, cotangent], axis=1)
    xc_pad = jnp.concatenate([xc, jnp.zeros((1, 2 * width), jnp.bfloat16)], axis=0)
    sent = xc_pad[token_of_slot].reshape(ep_count, CAP, 2 * width)
    recv = lax.all_to_all(sent, "ep", 0, 0, tiled=True)
    gates_recv = lax.all_to_all(slot_gate.reshape(ep_count, CAP), "ep", 0, 0, tiled=True)
    rows = ep_count * CAP
    recv_t = jnp.transpose(recv, (2, 0, 1)).reshape(2 * width, rows)
    xt_all, ct_all = etp_gather(recv_t[:width], recv_t[width:], nz, nx, nc)
    feat = nz * nx * nc * width
    xt = xt_all.reshape(feat, rows)
    ct = ct_all.reshape(feat, rows)
    slot_g = gates_recv.reshape(1, rows)
    dyt = (slot_g * ct.astype(jnp.float32)).astype(jnp.bfloat16)
    wg, wu, wd = w_gate[0], w_up[0], w_down[0]
    f32 = jnp.float32

    def dims(a, b):
        return (((a,), (b,)), ((), ()))
    gate_pre = lax.dot_general(xt, wg, dims(0, 0), preferred_element_type=f32)
    up_pre = lax.dot_general(xt, wu, dims(0, 0), preferred_element_type=f32)
    sigma = jax.nn.sigmoid(gate_pre)
    hidden = (jax.nn.silu(gate_pre) * up_pre).astype(jnp.bfloat16)
    out_t = lax.dot_general(wd, hidden, dims(0, 1), preferred_element_type=f32)
    d_hidden = lax.dot_general(dyt, wd, dims(0, 1), preferred_element_type=f32)
    d_up = (d_hidden * jax.nn.silu(gate_pre)).astype(jnp.bfloat16)
    d_gate = (d_hidden * up_pre * sigma * (1.0 + gate_pre * (1.0 - sigma))).astype(jnp.bfloat16)
    grad_down = lax.dot_general(hidden, dyt, dims(0, 1), preferred_element_type=f32)
    grad_gate_w = lax.dot_general(xt, d_gate, dims(1, 0), preferred_element_type=f32)
    grad_up_w = lax.dot_general(xt, d_up, dims(1, 0), preferred_element_type=f32)
    inner = jnp.sum(out_t * ct.astype(f32), axis=0, keepdims=True)
    back = etp_reduce_scatter(out_t.reshape(nz, nx, nc, width, rows), inner, ep_count, CAP)
    returned = jnp.transpose(back, (0, 2, 1)).reshape(EXPERTS * CAP, -1)
    pair_rows = returned[target].reshape(tok_count, 2, -1)
    mixed = jnp.sum(route_gates[:, :, None] * pair_rows[:, :, :width], axis=1).astype(jnp.bfloat16)
    grad_gates = pair_rows[:, :, width]
    return (
        mixed,
        grad_gates,
        grad_gate_w.astype(jnp.bfloat16)[None],
        grad_up_w.astype(jnp.bfloat16)[None],
        grad_down.astype(jnp.bfloat16)[None],
    )


def solution(mesh):
    ep = mesh.shape["ep"]
    etp = mesh.shape["etp"]
    nz, nx, nc = sub_sizes(etp)
    devs = np.asarray(mesh.devices).reshape(ep, nz, nx, nc)
    mesh2 = Mesh(devs, ("ep",) + SUB)
    in_specs = (
        P("ep", SUB),
        P("ep", None),
        P("ep", None),
        P("ep", SUB),
        P("ep", None, SUB),
        P("ep", None, SUB),
        P("ep", SUB, None),
    )
    out_specs = (
        P("ep", SUB),
        P("ep", None),
        P("ep", None, SUB),
        P("ep", None, SUB),
        P("ep", SUB, None),
    )
    return jax.shard_map(
        per_device, mesh=mesh2, in_specs=in_specs, out_specs=out_specs, check_vma=False
    )
```

time: 263 us -> 152 us (0.58)
  waiting for transfers between devices: 134 us -> 12.3 us
  Pallas kernels: 0 us -> 91.9 us
  blocking collectives: 48.5 us -> 0 us
  between operations: 14 us -> 0.8 us
  local copies, waits for them, and re-layouts: 28.6 us -> 18.7 us
  other arithmetic: 13.7 us -> 6.41 us
  starting transfers between devices: 13.6 us -> 10.4 us
    pallas_call x0 -> x2, Pallas kernels: none -> 91.9 us  [the longest x1 52.4 us: etp_reduce_scatter(): pl.pallas_call(functools.partial(_rs_kernel, ne, nz, nx, nc), out_shape=j...]
    reduce_scatter x3 -> x0, waiting for transfers between devices: 72 us -> none  [the longest x1 38.3 us: per_device(): part = lax.psum_scatter(part, 'z', scatter_dimension=2, tiled=True)]
    all_gather x2 -> x0, waiting for transfers between devices: 47.5 us -> none  [the longest x1 24 us: per_device(): g = lax.all_gather(g, 'x', axis=0)]
    all_gather x1 -> x0, blocking collectives: 33.5 us -> none  [per_device(): g = lax.all_gather(chunk, 'z', axis=0)]
    all_to_all x1 -> x0, blocking collectives: 15.1 us -> none  [per_device(): recv = lax.all_to_all(sent, 'ep', 0, 0, tiled=True)]
    all_gather x1 -> x0, local copies, waits for them, and re-layouts: 4.79 us -> none  [per_device(): g = lax.all_gather(g, 'core', axis=0)]
    convert_element_type x2 -> x1, other arithmetic: 7.15 us -> 2.95 us  [per_device(): dyt = (slot_g * ct.astype(jnp.float32)).astype(jnp.bfloat16)]
    concatenate x1 -> x0, local copies, waits for them, and re-layouts: 3.64 us -> none  [per_device(): part = jnp.concatenate([part, extra], axis=4)]
  transfers between devices with their start and end apart: 7 -> 2, of which waited for: 7 -> 2; matrix products, arithmetic and copies ran while one was open for 5% -> 2% of each run, Pallas kernels for 0% -> 0%
where the time goes in v4:
time: 152 us; the launch traced here: 151 us
  Pallas kernels  91.9 us (60%)
  local copies, waits for them, and re-layouts  18.7 us (12%)
  waiting for transfers between devices  12.3 us (8%)
  starting transfers between devices  10.4 us (7%)
  matrix products  10.2 us (7%)
  other arithmetic  6.41 us (4%)
    pallas_call x1, Pallas kernels, etp_reduce_scatter(): pl.pallas_call(functools.partial(_rs_kernel, ne, nz, nx, nc), out_shape=j...  52.4 us
    pallas_call x1, Pallas kernels, etp_gather(): pl.pallas_call(functools.partial(_gather_kernel, nz, nx, nc), out_shape=(...  39.4 us
    all_to_all x1, starting transfers between devices, per_device(): lax.all_to_all(slot_gate.reshape(ep_count, CAP), 'ep', 0, 0, tiled=True)  7.1 us
    all_to_all x1, waiting for transfers between devices, per_device(): recv = lax.all_to_all(sent, 'ep', 0, 0, tiled=True)  6.85 us
    all_to_all x1, waiting for transfers between devices, per_device(): lax.all_to_all(slot_gate.reshape(ep_count, CAP), 'ep', 0, 0, tiled=True)  5.41 us
    unnamed x15, local copies, waits for them, and re-layouts  3.5 us
    dot_general x1, local copies, waits for them, and re-layouts, per_device(): out_t = lax.dot_general(wd, hidden, dims(0, 1), preferred_element_type=f32)  3.41 us
    all_to_all x1, starting transfers between devices, per_device(): recv = lax.all_to_all(sent, 'ep', 0, 0, tiled=True)  3.35 us
  transfers between devices with their start and end apart: 2, of which 2 were waited for; matrix products, arithmetic and copies ran while one was open for 2% of the time, Pallas kernels for 0%

profile of v4, /device:TPU:6, one launch (start us, length us, event | category | flops | bytes accessed | tf_op | source)
XLA Modules:
  0.0 150.6 jit_solution(15013010075909812891)
XLA Ops:
  0.6 0.0 copy-start
  0.6 0.8 broadcast_multiply_fusion
  1.4 0.8 copy.22
  2.2 0.1 copy.21
  2.3 0.1 mul.71
  2.4 0.8 copy.20
  3.1 0.1 reshape.83
  3.3 0.1 eq.15
  3.4 0.1 fusion.14
  3.5 0.1 reduce_window_sum.11
  3.6 0.2 select_reduce_fusion
  3.8 0.9 scatter_custom_fusion
  4.7 0.1 pad_maximum_fusion
  4.8 1.5 %gather_fusion.2 = f32[192]{0:T(256)S(1)} fusion(f32[97]{0:T(128)S(1)} %pad_maximum_fusion, s32[1024]{0:T(1024)S(1)} %get-tuple-element.17), kind=kCustom, calls=%fused_computation.2 | custom fusion | bytes 2304 | tf_op jit(solution)/shard_map/gather | solution.py:271
  6.4 0.7 all_to_all.10
  7.0 7.1 %all-to-all-start.1 = ((f32[8,1,24]{2,1,0:T(1,128)}), f32[8,1,24]{2,1,0:T(1,128)S(1)}, u32[]{:S(2)}, u32[]{:S(2)}) async-start(f32[8,1,24]{2,1,0:T(1,128)} %all_to_all.10), calls=%async_computation.1 | async-start | bytes 8192 | tf_op jit(solution)/shard_map/all_to_all | solution.py:276
  14.1 0.8 fusion.18
  14.9 1.4 gather_fusion
  16.3 5.4 %all-to-all-done.1 = f32[8,1,24]{2,1,0:T(1,128)S(1)} async-done(((f32[8,1,24]{2,1,0:T(1,128)}), f32[8,1,24]{2,1,0:T(1,128)S(1)}, u32[]{:S(2)}, u32[]{:S(2)}) %all-to-all-start.1) | async-done | bytes 800 | tf_op jit(solution)/shard_map/all_to_all | solution.py:276
  21.7 3.3 %all-to-all-start = ((bf16[8,24,96]{2,1,0:T(8,128)(2,1)}), bf16[8,24,96]{2,1,0:T(8,128)(2,1)S(1)}, u32[]{:S(2)}, u32[]{:S(2)}) async-start(bf16[8,24,96]{2,1,0:T(8,128)(2,1)} %bitcast.2), calls=%async_computation | async-start | bytes 98304 | tf_op jit(solution)/shard_map/all_to_all | solution.py:275
  25.1 0.5 broadcast.81
  25.6 0.7 reduce.3
  26.3 0.1 mul.77
  26.4 6.8 %all-to-all-done = bf16[8,24,96]{2,1,0:T(8,128)(2,1)S(1)} async-done(((bf16[8,24,96]{2,1,0:T(8,128)(2,1)}), bf16[8,24,96]{2,1,0:T(8,128)(2,1)S(1)}, u32[]{:S(2)}, u32[]{:S(2)}) %all-to-all-start) | async-done | bytes 36896 | tf_op jit(solution)/shard_map/all_to_all | solution.py:275
  33.2 0.1 fusion.24
  33.3 0.7 copy.24.ca_ref
  34.0 0.7 copy.23.xa_ref
  34.7 39.4 %shard_map.110 = (bf16[8,4,2,48,192]{4,3,2,1,0:T(8,128)(2,1)}, bf16[8,4,2,48,192]{4,3,2,1,0:T(8,128)(2,1)}) custom-call(bf16[48,192]{1,0:T(8,128)(2,1)} %copy.23.xa_ref, bf16[48,192]{1,0:T(8,128)(2,1)} %copy.24.ca_ref), custom_call_target="tpu_custom_call" | custom-call | tf_op jit(solution)/shard_map/pallas_call | solution.py:108
  74.1 2.9 %multiply_convert_fusion.1 = bf16[8,4,2,48,192]{4,3,2,1,0:T(8,128)(2,1)} fusion(f32[192]{0:T(256)S(1)} %mul.77, bf16[8,4,2,48,192]{4,3,2,1,0:T(8,128)(2,1)} %get-tuple-element.8), kind=kLoop, calls=%fused_computation.12 | loop fusion | flops 1769472 | bytes 2360064 | tf_op jit(solution)/shard_map/convert_element_type | solution.py:284
  77.1 0.0 copy-start.1
  77.1 0.0 copy-start.4
  77.1 2.9 %copy.26 = f32[3072,192]{0,1:T(8,128)} copy(bf16[3072,192]{1,0:T(8,128)(2,1)} %bitcast.55) | data formatting | bytes 3538944 | tf_op jit(solution)/shard_map/convert_element_type | solution.py:301
  80.0 0.0 copy-start.5
  80.0 0.0 copy-done.1
  80.0 0.0 copy-done.4
  80.0 0.6 fusion.9
  80.7 0.5 copy-done.5
  81.2 0.0 copy-start.2
  81.2 0.6 multiply_convert_fusion.5
  81.8 0.0 copy-start.3
  81.8 0.8 copy-done.2
  82.6 1.6 %fusion.2 = bf16[1,128,3072]{2,1,0:T(8,128)(2,1)} fusion(bf16[192,128]{1,0:T(8,128)(2,1)S(1)} %get-tuple-element.13, f32[192]{0:T(256)S(1)} %mul.77, bf16[3072,192]{1,0:T(8,128)(2,1)S(1)} %bitcast.56), kind=kOutput, calls=%fused_computation.10 | convolution fusion | flops 153157632 | bytes 2016000 | tf_op jit(solution)/shard_map/dot_general | solution.py:298
  84.1 0.0 copy-done
  84.1 0.0 copy-done.3
  84.1 2.5 %multiply_reduce_fusion = (f32[192]{0:T(256)}, f32[3072,192]{0,1:T(8,128)}) fusion(f32[3072,192]{0,1:T(8,128)S(1)} %copy-done.3, bf16[192,128]{1,0:T(8,128)(2,1)S(1)} %get-tuple-element.13, bf16[1,128,3072]{2,1,0:T(8,128)(2,1)S(1)} %copy-done), kind=kOutput, calls=%fused_computation.13 | convolution fusion | flops 152174400 | bytes 5554944 | tf_op jit(solution)/shard_map/dot_general | solution.py:294
  86.6 3.4 %copy.25 = f32[3072,192]{1,0:T(8,128)} copy(f32[3072,192]{0,1:T(8,128)} %get-tuple-element.16) | data formatting | bytes 4718592 | tf_op jit(solution)/shard_map/dot_general | solution.py:294
  90.0 52.4 %shard_map.111 = f32[8,56,24]{2,1,0:T(8,128)} custom-call(f32[8,4,2,48,192]{4,3,2,1,0:T(8,128)} %bitcast.57, f32[1,192]{1,0:T(1,128)} %bitcast.66), custom_call_target="tpu_custom_call" | custom-call | tf_op jit(solution)/shard_map/pallas_call | solution.py:223
  142.5 1.0 copy.27
  143.5 0.6 gather_fusion.1
  144.2 0.7 fusion.12
  144.9 0.1 slice.33
  145.0 2.0 %fusion.4 = f32[192,128]{1,0:T(8,128)S(1)} fusion(bf16[3072,192]{1,0:T(8,128)(2,1)} %bitcast.58, bf16[1,128,3072]{2,1,0:T(8,128)(2,1)S(1)} %copy-done), kind=kOutput, calls=%fused_computation.15 | convolution fusion | flops 150994944 | bytes 2064384 | tf_op jit(solution)/shard_map/dot_general | solution.py:295
  147.0 1.5 fusion.1
  148.5 1.5 fusion
  149.9 0.6 copy.30
  (5 shorter events, 0.0 us)
Async XLA Ops:
  0.6 83.5 %copy-start = (bf16[1,128,3072]{2,1,0:T(8,128)(2,1)S(1)}, bf16[1,128,3072]{2,1,0:T(8,128)(2,1)}, u32[]{:S(2)}) copy-start(bf16[1,128,3072]{2,1,0:T(8,128)(2,1)} %param.13) | copy-start | bytes 2359300
  7.0 14.7 %all-to-all-start.1 = ((f32[8,1,24]{2,1,0:T(1,128)}), f32[8,1,24]{2,1,0:T(1,128)S(1)}, u32[]{:S(2)}, u32[]{:S(2)}) async-start(f32[8,1,24]{2,1,0:T(1,128)} %all_to_all.10), calls=%async_computation.1 | async-start | bytes 8192 | tf_op jit(solution)/shard_map/all_to_all | solution.py:276
  21.7 11.5 %all-to-all-start = ((bf16[8,24,96]{2,1,0:T(8,128)(2,1)}), bf16[8,24,96]{2,1,0:T(8,128)(2,1)S(1)}, u32[]{:S(2)}, u32[]{:S(2)}) async-start(bf16[8,24,96]{2,1,0:T(8,128)(2,1)} %bitcast.2), calls=%async_computation | async-start | bytes 98304 | tf_op jit(solution)/shard_map/all_to_all | solution.py:275
  77.1 3.0 %copy-start.1 = (bf16[8,4,2,48,192]{4,3,2,1,0:T(8,128)(2,1)S(1)}, bf16[8,4,2,48,192]{4,3,2,1,0:T(8,128)(2,1)}, u32[]{:S(2)}) copy-start(bf16[8,4,2,48,192]{4,3,2,1,0:T(8,128)(2,1)} %get-tuple-element.7) | copy-start | bytes 3538948
  77.1 3.0 %copy-start.4 = (bf16[1,3072,128]{2,1,0:T(8,128)(2,1)S(1)}, bf16[1,3072,128]{2,1,0:T(8,128)(2,1)}, u32[]{:S(2)}) copy-start(bf16[1,3072,128]{2,1,0:T(8,128)(2,1)} %param.11) | copy-start | bytes 2359300
  80.0 1.1 copy-start.5
  81.2 1.4 copy-start.2
  81.8 2.4 %copy-start.3 = (f32[3072,192]{0,1:T(8,128)S(1)}, f32[3072,192]{0,1:T(8,128)}, u32[]{:S(2)}) copy-start(f32[3072,192]{0,1:T(8,128)} %copy.26) | copy-start | bytes 7077892

commit v5 on v4

--- a/solution.py
+++ b/solution.py
@@ -45,16 +45,44 @@
     pl.semaphore_wait(barrier, count)
 
 
-def _gather_kernel(nz, nx, nc, xa_ref, ca_ref, xo_ref, co_ref, sem_local, send_a, recv_a, send_b, recv_b, send_c, recv_c):
+def _gather_kernel(ne, nz, nx, nc, sent_ref, g_ref, xo_ref, co_ref, go_ref, rbuf, rg, xa, ca,
+                   sem_local, send_0, rsem_0, send_a, recv_a, send_b, recv_b, send_c, recv_c):
     e, z, x, c = _coords()
-    _barrier(1, nz, nx, nc, False)
-    pairs = ((xa_ref, xo_ref), (ca_ref, co_ref))
+    _barrier(ne, nz, nx, nc, True)
+    sends = []
+    own = [pltpu.make_async_copy(sent_ref.at[e], rbuf.at[e], sem_local.at[0]),
+           pltpu.make_async_copy(g_ref.at[e], rg.at[e], sem_local.at[1])]
+    for cp in own:
+        cp.start()
+    for t, (src, dst) in enumerate(((sent_ref, rbuf), (g_ref, rg))):
+        for d in range(1, ne):
+            cp = pltpu.make_async_remote_copy(
+                src.at[(e + d) % ne], dst.at[e], send_0.at[t, d - 1], rsem_0.at[t, e],
+                device_id=((e + d) % ne, z, x, c), device_id_type=MESH_ID)
+            cp.start()
+            sends.append(cp)
+    for t, (src, dst) in enumerate(((sent_ref, rbuf), (g_ref, rg))):
+        for d in range(1, ne):
+            srce = (e + ne - d) % ne
+            pltpu.make_async_remote_copy(
+                src.at[e], dst.at[srce], send_0.at[t, d - 1], rsem_0.at[t, srce],
+                device_id=(srce, z, x, c), device_id_type=MESH_ID).wait_recv()
+    for cp in own:
+        cp.wait()
+    feats = xa.shape[0]
+    blk = rbuf.shape[2]
+    for b in range(ne):
+        piece = rbuf[b]
+        xa[:, b * blk:(b + 1) * blk] = piece[:feats]
+        ca[:, b * blk:(b + 1) * blk] = piece[feats:]
+        go_ref[:, b * blk:(b + 1) * blk] = rg[b]
+
+    pairs = ((xa, xo_ref), (ca, co_ref))
     locals_ = []
     for t, (src, out) in enumerate(pairs):
-        cp = pltpu.make_async_copy(src, out.at[z, x, c], sem_local.at[t])
+        cp = pltpu.make_async_copy(src, out.at[z, x, c], sem_local.at[2 + t])
         cp.start()
         locals_.append(cp)
-    sends = []
     for t, (src, out) in enumerate(pairs):
         for d in range(1, nz):
             cp = pltpu.make_async_remote_copy(
@@ -100,18 +128,26 @@
         cp.wait_send()
 
 
-def etp_gather(xa, ca, nz, nx, nc):
-    rows, cols = xa.shape
+def ep_etp_gather(sent, gsend, nz, nx, nc):
+    ne, two_feats, blk = sent.shape
+    feats = two_feats // 2
+    cols = ne * blk
     vmem = pltpu.VMEM
     dma = pltpu.SemaphoreType.DMA
-    shape = jax.ShapeDtypeStruct((nz, nx, nc, rows, cols), xa.dtype)
+    shape = jax.ShapeDtypeStruct((nz, nx, nc, feats, cols), sent.dtype)
     return pl.pallas_call(
-        functools.partial(_gather_kernel, nz, nx, nc),
-        out_shape=(shape, shape),
+        functools.partial(_gather_kernel, ne, nz, nx, nc),
+        out_shape=(shape, shape, jax.ShapeDtypeStruct((1, cols), gsend.dtype)),
         in_specs=[pl.BlockSpec(memory_space=vmem)] * 2,
-        out_specs=(pl.BlockSpec(memory_space=vmem),) * 2,
+        out_specs=(pl.BlockSpec(memory_space=vmem),) * 3,
         scratch_shapes=[
-            dma((2,)),
+            pltpu.VMEM((ne, two_feats, blk), sent.dtype),
+            pltpu.VMEM((ne, 1, blk), gsend.dtype),
+            pltpu.VMEM((feats, cols), sent.dtype),
+            pltpu.VMEM((feats, cols), sent.dtype),
+            dma((4,)),
+            dma((2, max(ne - 1, 1))),
+            dma((2, ne)),
             dma((2, max(nz - 1, 1))),
             dma((2, max(nz - 1, 1))),
             dma((2, max(nx - 1, 1))),
@@ -120,7 +156,7 @@
             dma((2, max(nc - 1, 1))),
         ],
         compiler_params=pltpu.CompilerParams(collective_id=0, has_side_effects=True),
-    )(xa, ca)
+    )(sent, gsend)
 
 
 def _rs_kernel(ne, nz, nx, nc, part_ref, inner_ref, out_ref, recv_c, acc1, recv_b, acc2, recv_a,
@@ -271,12 +307,10 @@
     slot_gate = gate_flat[slot_table]
     xc = jnp.concatenate([tokens, cotangent], axis=1)
     xc_pad = jnp.concatenate([xc, jnp.zeros((1, 2 * width), jnp.bfloat16)], axis=0)
-    sent = xc_pad[token_of_slot].reshape(ep_count, CAP, 2 * width)
-    recv = lax.all_to_all(sent, "ep", 0, 0, tiled=True)
-    gates_recv = lax.all_to_all(slot_gate.reshape(ep_count, CAP), "ep", 0, 0, tiled=True)
+    sent = jnp.transpose(xc_pad[token_of_slot].reshape(ep_count, CAP, 2 * width), (0, 2, 1))
+    gsend = slot_gate.reshape(ep_count, 1, CAP)
     rows = ep_count * CAP
-    recv_t = jnp.transpose(recv, (2, 0, 1)).reshape(2 * width, rows)
-    xt_all, ct_all = etp_gather(recv_t[:width], recv_t[width:], nz, nx, nc)
+    xt_all, ct_all, gates_recv = ep_etp_gather(sent, gsend, nz, nx, nc)
     feat = nz * nx * nc * width
     xt = xt_all.reshape(feat, rows)
     ct = ct_all.reshape(feat, rows)

time: 152 us -> 136 us (0.89)
  Pallas kernels: 91.9 us -> 106 us
  waiting for transfers between devices: 12.3 us -> 0 us
  starting transfers between devices: 10.4 us -> 0 us
  local copies, waits for them, and re-layouts: 18.7 us -> 14.3 us
  other arithmetic: 6.41 us -> 4.49 us
    pallas_call x1, Pallas kernels: 39.4 us -> 52.9 us  [ep_etp_gather(): pl.pallas_call(functools.partial(_gather_kernel, ne, nz, nx, nc), out_sha...]
    all_to_all x2 -> x0, waiting for transfers between devices: 12.3 us -> none  [the longest x1 6.85 us: per_device(): recv = lax.all_to_all(sent, 'ep', 0, 0, tiled=True)]
    all_to_all x2 -> x0, starting transfers between devices: 10.4 us -> none  [the longest x1 7.1 us: per_device(): lax.all_to_all(slot_gate.reshape(ep_count, CAP), 'ep', 0, 0, tiled=True)]
  transfers between devices with their start and end apart: 2 -> 0, of which waited for: 2 -> 0; matrix products, arithmetic and copies ran while one was open for 2% -> 0% of each run, Pallas kernels for 0% -> 0%
where the time goes in v5:
time: 136 us; the launch traced here: 134 us
  Pallas kernels  106 us (78%)
  local copies, waits for them, and re-layouts  14.3 us (11%)
  matrix products  9.09 us (7%)
  other arithmetic  4.49 us (3%)
    pallas_call x1, Pallas kernels, etp_reduce_scatter(): pl.pallas_call(functools.partial(_rs_kernel, ne, nz, nx, nc), out_shape=j...  52.9 us
    pallas_call x1, Pallas kernels, ep_etp_gather(): pl.pallas_call(functools.partial(_gather_kernel, ne, nz, nx, nc), out_sha...  52.9 us
    unnamed x15, local copies, waits for them, and re-layouts  3.26 us
    dot_general x1, matrix products, per_device(): out_t = lax.dot_general(wd, hidden, dims(0, 1), preferred_element_type=f32)  2.8 us

profile of v5, /device:TPU:6, one launch (start us, length us, event | category | flops | bytes accessed | tf_op | source)
XLA Modules:
  0.0 134.4 jit_solution(13126154069079787572)
XLA Ops:
  0.6 0.0 copy-start
  0.6 0.8 copy.21
  1.5 0.1 eq.15
  1.6 0.1 fusion.14
  1.7 0.1 reduce_window_sum.11
  1.8 0.2 select_reduce_fusion
  2.0 0.7 broadcast_multiply_fusion
  2.7 0.1 copy.20
  2.8 0.1 mul.71
  2.9 0.9 scatter_custom_fusion
  3.9 0.8 copy.19
  4.6 0.1 reshape.72
  4.7 0.1 pad_maximum_fusion
  4.8 1.6 %gather_fusion.1 = f32[192]{0:T(256)S(1)} fusion(f32[97]{0:T(128)S(1)} %pad_maximum_fusion, s32[1024]{0:T(1024)S(1)} %get-tuple-element.17), kind=kCustom, calls=%fused_computation.1 | custom fusion | bytes 2304 | tf_op jit(solution)/shard_map/gather | solution.py:307
  6.4 0.7 reshape.73.g_ref
  7.1 0.8 fusion.18
  7.9 0.8 gather_fusion
  8.7 0.8 copy.22
  9.5 52.9 %shard_map.110 = (bf16[8,4,2,48,192]{4,3,2,1,0:T(8,128)(2,1)}, bf16[8,4,2,48,192]{4,3,2,1,0:T(8,128)(2,1)}, f32[1,192]{1,0:T(1,128)}) custom-call(bf16[8,96,24]{2,1,0:T(8,128)(2,1)} %bitcast.59, f32[8,1,24]{2,1,0:T(1,128)} %reshape.73.g_ref), custom_call_target="tpu_custom_call" | custom-call | tf_op jit(solution)/shard_map/pallas_call | solution.py:138
  62.3 1.7 %multiply_convert_fusion.1 = bf16[8,4,2,48,192]{4,3,2,1,0:T(8,128)(2,1)S(1)} fusion(f32[192]{0:T(256)} %bitcast.63, bf16[8,4,2,48,192]{4,3,2,1,0:T(8,128)(2,1)} %get-tuple-element.9), kind=kLoop, calls=%fused_computation.12 | loop fusion | flops 1769472 | bytes 2360064 | tf_op jit(solution)/shard_map/convert_element_type | solution.py:318
  64.1 0.0 copy-start.2
  64.1 0.0 copy-start.3
  64.1 0.0 copy-done
  64.1 0.6 fusion.4
  64.7 0.8 copy-done.2
  65.5 0.2 copy-done.3
  65.7 0.6 fusion.9
  66.3 0.0 copy-start.5
  66.3 1.5 %fusion.1 = bf16[1,3072,128]{2,1,0:T(8,128)(2,1)} fusion(bf16[3072,192]{1,0:T(8,128)(2,1)S(1)} %bitcast.52, f32[192,128]{1,0:T(8,128)S(1)} %fusion.4, f32[192,128]{1,0:T(8,128)S(1)} %fusion.9), kind=kOutput, calls=%fused_computation.9 | convolution fusion | flops 151535616 | bytes 2162688 | tf_op jit(solution)/shard_map/dot_general | solution.py:334
  67.8 0.0 copy-done.5
  67.8 0.6 multiply_convert_fusion.5
  68.4 0.0 copy-start.1
  68.4 0.0 copy-start.4
  68.4 1.5 %fusion = bf16[1,3072,128]{2,1,0:T(8,128)(2,1)} fusion(bf16[3072,192]{1,0:T(8,128)(2,1)S(1)} %bitcast.54, f32[192,128]{1,0:T(8,128)S(1)} %fusion.9, f32[192,128]{1,0:T(8,128)S(1)} %fusion.4, f32[192,128]{1,0:T(8,128)S(1)} %get-tuple-element.14), kind=kOutput, calls=%fused_computation.8 | convolution fusion | flops 151633920 | bytes 2260992 | tf_op jit(solution)/shard_map/dot_general | solution.py:333
  69.9 0.0 copy-done.1
  69.9 0.0 copy-done.4
  69.9 1.6 %fusion.2 = bf16[1,128,3072]{2,1,0:T(8,128)(2,1)} fusion(bf16[192,128]{1,0:T(8,128)(2,1)S(1)} %get-tuple-element.13, f32[192]{0:T(256)S(1)} %bitcast.64, bf16[3072,192]{1,0:T(8,128)(2,1)S(1)} %bitcast.49), kind=kOutput, calls=%fused_computation.10 | convolution fusion | flops 153157632 | bytes 2016000 | tf_op jit(solution)/shard_map/dot_general | solution.py:332
  71.4 1.8 %copy.25 = f32[3072,192]{0,1:T(8,128)} copy(bf16[3072,192]{1,0:T(8,128)(2,1)S(1)} %bitcast.50) | data formatting | bytes 3538944 | tf_op jit(solution)/shard_map/convert_element_type | solution.py:335
  73.2 2.8 %multiply_reduce_fusion = (f32[192]{0:T(256)}, f32[3072,192]{0,1:T(8,128)S(1)}) fusion(f32[3072,192]{0,1:T(8,128)} %copy.25, bf16[192,128]{1,0:T(8,128)(2,1)S(1)} %get-tuple-element.13, bf16[1,128,3072]{2,1,0:T(8,128)(2,1)S(1)} %copy-done), kind=kOutput, calls=%fused_computation.13 | convolution fusion | flops 152174400 | bytes 5554944 | tf_op jit(solution)/shard_map/dot_general | solution.py:328
  76.0 2.3 %copy.24 = f32[3072,192]{1,0:T(8,128)} copy(f32[3072,192]{0,1:T(8,128)S(1)} %get-tuple-element.16) | data formatting | bytes 4718592 | tf_op jit(solution)/shard_map/dot_general | solution.py:328
  78.3 52.9 %shard_map.111 = f32[8,56,24]{2,1,0:T(8,128)} custom-call(f32[8,4,2,48,192]{4,3,2,1,0:T(8,128)} %bitcast.55, f32[1,192]{1,0:T(1,128)} %bitcast.65), custom_call_target="tpu_custom_call" | custom-call | tf_op jit(solution)/shard_map/pallas_call | solution.py:259
  131.2 1.0 copy.26
  132.3 0.6 gather_fusion.2
  132.9 0.1 slice.15
  133.0 0.7 copy.28
  133.7 0.7 fusion.12
  (5 shorter events, 0.0 us)
Async XLA Ops:
  0.6 63.5 %copy-start = (bf16[1,128,3072]{2,1,0:T(8,128)(2,1)S(1)}, bf16[1,128,3072]{2,1,0:T(8,128)(2,1)}, u32[]{:S(2)}) copy-start(bf16[1,128,3072]{2,1,0:T(8,128)(2,1)} %param.13) | copy-start | bytes 2359300
  64.1 1.4 %copy-start.2 = (bf16[8,4,2,48,192]{4,3,2,1,0:T(8,128)(2,1)S(1)}, bf16[8,4,2,48,192]{4,3,2,1,0:T(8,128)(2,1)}, u32[]{:S(2)}) copy-start(bf16[8,4,2,48,192]{4,3,2,1,0:T(8,128)(2,1)} %get-tuple-element.8) | copy-start | bytes 3538948
  64.1 1.6 %copy-start.3 = (bf16[1,3072,128]{2,1,0:T(8,128)(2,1)S(1)}, bf16[1,3072,128]{2,1,0:T(8,128)(2,1)}, u32[]{:S(2)}) copy-start(bf16[1,3072,128]{2,1,0:T(8,128)(2,1)} %param.11) | copy-start | bytes 2359300
  66.3 1.5 %copy-start.5 = (bf16[1,3072,128]{2,1,0:T(8,128)(2,1)S(1)}, bf16[1,3072,128]{2,1,0:T(8,128)(2,1)}, u32[]{:S(2)}) copy-start(bf16[1,3072,128]{2,1,0:T(8,128)(2,1)} %param.12) | copy-start | bytes 2359300
  68.4 1.5 %copy-start.1 = (bf16[8,4,2,48,192]{4,3,2,1,0:T(8,128)(2,1)S(1)}, bf16[8,4,2,48,192]{4,3,2,1,0:T(8,128)(2,1)}, u32[]{:S(2)}) copy-start(bf16[8,4,2,48,192]{4,3,2,1,0:T(8,128)(2,1)} %get-tuple-element.9) | copy-start | bytes 3538948
  68.4 1.5 %copy-start.4 = (f32[1,192]{1,0:T(1,128)S(1)}, f32[1,192]{1,0:T(1,128)}, u32[]{:S(2)}) copy-start(f32[1,192]{1,0:T(1,128)} %get-tuple-element.10) | copy-start | bytes 2308

commit v6 on v5

--- a/solution.py
+++ b/solution.py
@@ -45,7 +45,7 @@
     pl.semaphore_wait(barrier, count)
 
 
-def _gather_kernel(ne, nz, nx, nc, sent_ref, g_ref, xo_ref, co_ref, go_ref, rbuf, rg, xa, ca,
+def _gather_kernel(ne, nz, nx, nc, sent_ref, g_ref, xo_ref, go_ref, rbuf, rg, xa,
                    sem_local, send_0, rsem_0, send_a, recv_a, send_b, recv_b, send_c, recv_c):
     e, z, x, c = _coords()
     _barrier(ne, nz, nx, nc, True)
@@ -71,13 +71,14 @@
         cp.wait()
     feats = xa.shape[0]
     blk = rbuf.shape[2]
+    cols = ne * blk
     for b in range(ne):
         piece = rbuf[b]
         xa[:, b * blk:(b + 1) * blk] = piece[:feats]
-        ca[:, b * blk:(b + 1) * blk] = piece[feats:]
+        xa[:, cols + b * blk:cols + (b + 1) * blk] = piece[feats:]
         go_ref[:, b * blk:(b + 1) * blk] = rg[b]
 
-    pairs = ((xa, xo_ref), (ca, co_ref))
+    pairs = ((xa, xo_ref),)
     locals_ = []
     for t, (src, out) in enumerate(pairs):
         cp = pltpu.make_async_copy(src, out.at[z, x, c], sem_local.at[2 + t])
@@ -134,17 +135,16 @@
     cols = ne * blk
     vmem = pltpu.VMEM
     dma = pltpu.SemaphoreType.DMA
-    shape = jax.ShapeDtypeStruct((nz, nx, nc, feats, cols), sent.dtype)
+    shape = jax.ShapeDtypeStruct((nz, nx, nc, feats, 2 * cols), sent.dtype)
     return pl.pallas_call(
         functools.partial(_gather_kernel, ne, nz, nx, nc),
-        out_shape=(shape, shape, jax.ShapeDtypeStruct((1, cols), gsend.dtype)),
+        out_shape=(shape, jax.ShapeDtypeStruct((1, cols), gsend.dtype)),
         in_specs=[pl.BlockSpec(memory_space=vmem)] * 2,
-        out_specs=(pl.BlockSpec(memory_space=vmem),) * 3,
+        out_specs=(pl.BlockSpec(memory_space=vmem),) * 2,
         scratch_shapes=[
             pltpu.VMEM((ne, two_feats, blk), sent.dtype),
             pltpu.VMEM((ne, 1, blk), gsend.dtype),
-            pltpu.VMEM((feats, cols), sent.dtype),
-            pltpu.VMEM((feats, cols), sent.dtype),
+            pltpu.VMEM((feats, 2 * cols), sent.dtype),
             dma((4,)),
             dma((2, max(ne - 1, 1))),
             dma((2, ne)),
@@ -225,10 +225,13 @@
     for d in range(nz - 1):
         itotal = itotal + ir_a[d]
 
-    feats = total.shape[0]
+    half = total.shape[0]
+    feats = 2 * half
     blk = fin.shape[2]
+    cols = ne * blk
     for b in range(ne):
-        fin[b, :feats, :] = total[:, b * blk:(b + 1) * blk]
+        fin[b, :half, :] = total[:, b * blk:(b + 1) * blk]
+        fin[b, half:feats, :] = total[:, cols + b * blk:cols + (b + 1) * blk]
         fin[b, feats:feats + 1, :] = itotal[:, b * blk:(b + 1) * blk]
         fin[b, feats + 1:, :] = jnp.zeros((fin.shape[1] - feats - 1, blk), jnp.float32)
     local = pltpu.make_async_copy(fin.at[e], out_ref.at[e], sem_local.at[0])
@@ -251,7 +254,7 @@
 
 def etp_reduce_scatter(part, inner, ne, blk):
     nz, nx, nc, feats, cols = part.shape
-    pad_rows = -(-(feats + 1) // 8) * 8
+    pad_rows = -(-(2 * feats + 1) // 8) * 8
     f32 = jnp.float32
     vmem = pltpu.VMEM
     dma = pltpu.SemaphoreType.DMA
@@ -267,11 +270,11 @@
             pltpu.VMEM((mx, nz, feats, cols), f32),
             pltpu.VMEM((nz, feats, cols), f32),
             pltpu.VMEM((mz, feats, cols), f32),
-            pltpu.VMEM((mc, 1, cols), f32),
-            pltpu.VMEM((1, cols), f32),
-            pltpu.VMEM((mx, 1, cols), f32),
-            pltpu.VMEM((1, cols), f32),
-            pltpu.VMEM((mz, 1, cols), f32),
+            pltpu.VMEM((mc, 1, cols // 2), f32),
+            pltpu.VMEM((1, cols // 2), f32),
+            pltpu.VMEM((mx, 1, cols // 2), f32),
+            pltpu.VMEM((1, cols // 2), f32),
+            pltpu.VMEM((mz, 1, cols // 2), f32),
             pltpu.VMEM((ne, pad_rows, blk), f32),
             dma((1,)),
             dma((2, mc)),
@@ -310,10 +313,10 @@
     sent = jnp.transpose(xc_pad[token_of_slot].reshape(ep_count, CAP, 2 * width), (0, 2, 1))
     gsend = slot_gate.reshape(ep_count, 1, CAP)
     rows = ep_count * CAP
-    xt_all, ct_all, gates_recv = ep_etp_gather(sent, gsend, nz, nx, nc)
+    xc_all, gates_recv = ep_etp_gather(sent, gsend, nz, nx, nc)
     feat = nz * nx * nc * width
-    xt = xt_all.reshape(feat, rows)
-    ct = ct_all.reshape(feat, rows)
+    xt = xc_all[..., :rows].reshape(feat, rows)
+    ct = xc_all[..., rows:].reshape(feat, rows)
     slot_g = gates_recv.reshape(1, rows)
     dyt = (slot_g * ct.astype(jnp.float32)).astype(jnp.bfloat16)
     wg, wu, wd = w_gate[0], w_up[0], w_down[0]
@@ -333,11 +336,15 @@
     grad_gate_w = lax.dot_general(xt, d_gate, dims(1, 0), preferred_element_type=f32)
     grad_up_w = lax.dot_general(xt, d_up, dims(1, 0), preferred_element_type=f32)
     inner = jnp.sum(out_t * ct.astype(f32), axis=0, keepdims=True)
-    back = etp_reduce_scatter(out_t.reshape(nz, nx, nc, width, rows), inner, ep_count, CAP)
-    returned = jnp.transpose(back, (0, 2, 1)).reshape(EXPERTS * CAP, -1)
-    pair_rows = returned[target].reshape(tok_count, 2, -1)
-    mixed = jnp.sum(route_gates[:, :, None] * pair_rows[:, :, :width], axis=1).astype(jnp.bfloat16)
-    grad_gates = pair_rows[:, :, width]
+    part = out_t.reshape(nz, nx, nc, width // 2, 2 * rows)
+    back = etp_reduce_scatter(part, inner, ep_count, CAP)
+    half = width // 2
+    feats_back = back[:, :width].reshape(EXPERTS, 2, half, CAP)
+    feats_back = jnp.transpose(feats_back, (0, 3, 2, 1)).reshape(EXPERTS * CAP, width)
+    inner_back = back[:, width].reshape(EXPERTS * CAP)
+    pair_rows = feats_back[target].reshape(tok_count, 2, width)
+    mixed = jnp.sum(route_gates[:, :, None] * pair_rows, axis=1).astype(jnp.bfloat16)
+    grad_gates = inner_back[target].reshape(tok_count, 2)
     return (
         mixed,
         grad_gates,

time: 136 us -> 131 us (0.963)
  Pallas kernels: 106 us -> 91.1 us
  local copies, waits for them, and re-layouts: 14.3 us -> 22.9 us
    pallas_call x1, Pallas kernels: 52.9 us -> 45.5 us  [ep_etp_gather(): pl.pallas_call(functools.partial(_gather_kernel, ne, nz, nx, nc), out_sha...]
    pallas_call x1, Pallas kernels: 52.9 us -> 45.6 us  [etp_reduce_scatter(): pl.pallas_call(functools.partial(_rs_kernel, ne, nz, nx, nc), out_shape=j...]
    reshape x0 -> x5, local copies, waits for them, and re-layouts: none -> 4.61 us  [the longest x1 4.22 us: per_device(): part = out_t.reshape(nz, nx, nc, width // 2, 2 * rows)]
    slice x1 -> x2, local copies, waits for them, and re-layouts: 0.11 us -> 1.72 us  [the longest x1 0.95 us: per_device(): feats_back = back[:, :width].reshape(EXPERTS, 2, half, CAP)]
where the time goes in v6:
time: 131 us; the launch traced here: 129 us
  Pallas kernels  91.1 us (70%)
  local copies, waits for them, and re-layouts  22.9 us (17%)
  matrix products  8.77 us (7%)
  other arithmetic  5.6 us (4%)
    pallas_call x1, Pallas kernels, etp_reduce_scatter(): pl.pallas_call(functools.partial(_rs_kernel, ne, nz, nx, nc), out_shape=j...  45.6 us
    pallas_call x1, Pallas kernels, ep_etp_gather(): pl.pallas_call(functools.partial(_gather_kernel, ne, nz, nx, nc), out_sha...  45.5 us
    reshape x1, local copies, waits for them, and re-layouts, per_device(): part = out_t.reshape(nz, nx, nc, width // 2, 2 * rows)  4.22 us
    unnamed x15, local copies, waits for them, and re-layouts  3.68 us
    dot_general x1, local copies, waits for them, and re-layouts, per_device(): out_t = lax.dot_general(wd, hidden, dims(0, 1), preferred_element_type=f32)  3.41 us

profile of v6, /device:TPU:6, one launch (start us, length us, event | category | flops | bytes accessed | tf_op | source)
XLA Modules:
  0.0 129.2 jit_solution(3144545768431087935)
XLA Ops:
  0.6 0.0 copy-start
  0.6 0.8 copy.22
  1.5 0.1 eq.15
  1.6 0.1 fusion.13
  1.7 0.1 reduce_window_sum.11
  1.8 0.2 select_reduce_fusion
  2.0 0.7 broadcast_multiply_fusion
  2.7 0.1 copy.21
  2.8 0.1 mul.71
  2.9 0.9 scatter_custom_fusion
  3.9 0.8 copy.20
  4.6 0.1 reshape.78
  4.7 0.1 pad_maximum_fusion
  4.8 1.6 %gather_fusion.1 = f32[192]{0:T(256)S(1)} fusion(f32[97]{0:T(128)S(1)} %pad_maximum_fusion, s32[1024]{0:T(1024)S(1)} %get-tuple-element.27), kind=kCustom, calls=%fused_computation.1 | custom fusion | bytes 2304 | tf_op jit(solution)/shard_map/gather | solution.py:310
  6.4 0.7 reshape.79.g_ref
  7.1 0.8 fusion.17
  7.9 0.8 gather_fusion
  8.7 0.8 copy.23
  9.5 45.5 %shard_map.110 = (bf16[8,4,2,48,384]{4,3,2,1,0:T(8,128)(2,1)}, f32[1,192]{1,0:T(1,128)}) custom-call(bf16[8,96,24]{2,1,0:T(8,128)(2,1)} %bitcast.60, f32[8,1,24]{2,1,0:T(1,128)} %reshape.79.g_ref), custom_call_target="tpu_custom_call" | custom-call | tf_op jit(solution)/shard_map/pallas_call | solution.py:139
  54.9 2.1 %multiply_convert_fusion.1 = bf16[8,4,2,48,192]{4,3,2,1,0:T(8,128)(2,1)S(1)} fusion(f32[192]{0:T(256)} %bitcast.64, bf16[8,4,2,48,384]{4,3,2,1,0:T(8,128)(2,1)} %get-tuple-element.7), kind=kLoop, calls=%fused_computation.13 | loop fusion | flops 1769472 | bytes 2360064 | tf_op jit(solution)/shard_map/convert_element_type | solution.py:321
  57.0 0.0 copy-start.2
  57.1 0.0 copy-done
  57.1 0.6 fusion.4
  57.7 1.0 copy-done.2
  58.7 0.0 copy-start.3
  58.7 0.8 slice_convert_fusion
  59.5 0.0 copy-start.1
  59.5 0.4 copy-done.3
  59.8 0.6 fusion.9
  60.5 0.0 copy-start.5
  60.5 1.5 %fusion.1 = bf16[1,3072,128]{2,1,0:T(8,128)(2,1)} fusion(bf16[3072,192]{1,0:T(8,128)(2,1)S(1)} %bitcast.55, f32[192,128]{1,0:T(8,128)S(1)} %fusion.4, f32[192,128]{1,0:T(8,128)S(1)} %fusion.9), kind=kOutput, calls=%fused_computation.10 | convolution fusion | flops 151535616 | bytes 2162688 | tf_op jit(solution)/shard_map/dot_general | solution.py:337
  61.9 0.0 copy-done.5
  61.9 0.6 multiply_convert_fusion.5
  62.6 0.0 copy-start.4
  62.6 1.5 %fusion = bf16[1,3072,128]{2,1,0:T(8,128)(2,1)} fusion(bf16[3072,192]{1,0:T(8,128)(2,1)S(1)} %bitcast.57, f32[192,128]{1,0:T(8,128)S(1)} %fusion.9, f32[192,128]{1,0:T(8,128)S(1)} %fusion.4, f32[192,128]{1,0:T(8,128)S(1)} %get-tuple-element.24), kind=kOutput, calls=%fused_computation.9 | convolution fusion | flops 151633920 | bytes 2260992 | tf_op jit(solution)/shard_map/dot_general | solution.py:336
  64.0 0.0 copy-done.1
  64.0 0.0 copy-done.4
  64.0 1.6 %fusion.2 = bf16[1,128,3072]{2,1,0:T(8,128)(2,1)} fusion(bf16[192,128]{1,0:T(8,128)(2,1)S(1)} %get-tuple-element.23, f32[3072,192]{1,0:T(8,128)S(1)} %bitcast.52, f32[192]{0:T(256)S(1)} %bitcast.65), kind=kOutput, calls=%fused_computation.11 | convolution fusion | flops 152567808 | bytes 3195648 | tf_op jit(solution)/shard_map/dot_general | solution.py:335
  65.6 2.3 %copy.26 = f32[3072,192]{0,1:T(8,128)S(1)} copy(f32[3072,192]{1,0:T(8,128)} %bitcast.53) | data formatting | bytes 4718592 | tf_op jit(solution)/shard_map/convert_element_type | solution.py:338
  67.9 2.5 %multiply_reduce_fusion = (f32[192]{0:T(256)}, f32[3072,192]{0,1:T(8,128)}) fusion(f32[3072,192]{0,1:T(8,128)S(1)} %copy.26, bf16[192,128]{1,0:T(8,128)(2,1)S(1)} %get-tuple-element.23, bf16[1,128,3072]{2,1,0:T(8,128)(2,1)S(1)} %copy-done), kind=kOutput, calls=%fused_computation.14 | convolution fusion | flops 152174400 | bytes 5554944 | tf_op jit(solution)/shard_map/dot_general | solution.py:331
  70.4 3.4 %copy.25 = f32[3072,192]{1,0:T(8,128)} copy(f32[3072,192]{0,1:T(8,128)} %get-tuple-element.26) | data formatting | bytes 4718592 | tf_op jit(solution)/shard_map/dot_general | solution.py:331
  73.8 4.2 %reshape.81.part_ref = f32[8,4,2,24,384]{4,3,2,1,0:T(8,128)} reshape(f32[3072,192]{1,0:T(8,128)} %copy.25) | data formatting | bytes 4718592 | tf_op jit(solution)/shard_map/reshape | solution.py:339
  78.1 45.6 %shard_map.111 = f32[8,56,24]{2,1,0:T(8,128)} custom-call(f32[8,4,2,24,384]{4,3,2,1,0:T(8,128)} %reshape.81.part_ref, f32[1,192]{1,0:T(1,128)} %bitcast.66), custom_call_target="tpu_custom_call" | custom-call | tf_op jit(solution)/shard_map/pallas_call | solution.py:262
  123.7 0.9 slice.14
  124.6 0.1 copy.31
  124.7 0.1 reshape.83
  124.8 0.1 copy.28
  124.9 0.6 gather_fusion.2
  125.6 0.7 multiply_reduce_fusion.1
  126.3 0.8 slice_reduce_fusion
  127.1 0.1 reshape_squeeze.3
  127.2 1.3 gather_fusion.3
  128.4 0.1 reshape.85
  128.6 0.6 copy.29
  (5 shorter events, 0.0 us)
Async XLA Ops:
  0.6 56.4 %copy-start = (bf16[1,128,3072]{2,1,0:T(8,128)(2,1)S(1)}, bf16[1,128,3072]{2,1,0:T(8,128)(2,1)}, u32[]{:S(2)}) copy-start(bf16[1,128,3072]{2,1,0:T(8,128)(2,1)} %param.13) | copy-start | bytes 2359300
  57.0 1.7 %copy-start.2 = (bf16[8,4,2,48,384]{4,3,2,1,0:T(8,128)(2,1)S(1)}, bf16[8,4,2,48,384]{4,3,2,1,0:T(8,128)(2,1)}, u32[]{:S(2)}) copy-start(bf16[8,4,2,48,384]{4,3,2,1,0:T(8,128)(2,1)} %get-tuple-element.7) | copy-start | bytes 7077892
  58.7 1.1 copy-start.3
  59.5 4.5 %copy-start.1 = (f32[8,4,2,48,192]{4,3,2,1,0:T(8,128)}, f32[8,4,2,48,192]{4,3,2,1,0:T(8,128)S(1)}, u32[]{:S(2)}) copy-start(f32[8,4,2,48,192]{4,3,2,1,0:T(8,128)S(1)} %get-tuple-element.19) | copy-start | bytes 7077892
  60.5 1.5 %copy-start.5 = (bf16[1,3072,128]{2,1,0:T(8,128)(2,1)S(1)}, bf16[1,3072,128]{2,1,0:T(8,128)(2,1)}, u32[]{:S(2)}) copy-start(bf16[1,3072,128]{2,1,0:T(8,128)(2,1)} %param.12) | copy-start | bytes 2359300
  62.6 1.5 %copy-start.4 = (f32[1,192]{1,0:T(1,128)S(1)}, f32[1,192]{1,0:T(1,128)}, u32[]{:S(2)}) copy-start(f32[1,192]{1,0:T(1,128)} %get-tuple-element.8) | copy-start | bytes 2308

commit v7 on v6

--- a/solution.py
+++ b/solution.py
@@ -78,53 +78,53 @@
         xa[:, cols + b * blk:cols + (b + 1) * blk] = piece[feats:]
         go_ref[:, b * blk:(b + 1) * blk] = rg[b]
 
-    pairs = ((xa, xo_ref),)
-    locals_ = []
-    for t, (src, out) in enumerate(pairs):
-        cp = pltpu.make_async_copy(src, out.at[z, x, c], sem_local.at[2 + t])
+    out = xo_ref
+    local = pltpu.make_async_copy(xa, out.at[z, x, c], sem_local.at[2])
+    local.start()
+    for d in range(1, nz):
+        cp = pltpu.make_async_remote_copy(
+            xa, out.at[z, x, c], send_a.at[d - 1], recv_a.at[d - 1],
+            device_id=(e, (z + d) % nz, x, c), device_id_type=MESH_ID)
         cp.start()
-        locals_.append(cp)
-    for t, (src, out) in enumerate(pairs):
-        for d in range(1, nz):
+        sends.append(cp)
+
+    def forward(src, zz, xs, to_x):
+        if to_x:
+            for dx in range(1, nx):
+                cp = pltpu.make_async_remote_copy(
+                    src, out.at[zz, x, c], send_b.at[dx - 1, zz], recv_b.at[dx - 1, zz],
+                    device_id=(e, z, (x + dx) % nx, c), device_id_type=MESH_ID)
+                cp.start()
+                sends.append(cp)
+        for dc in range(1, nc):
             cp = pltpu.make_async_remote_copy(
-                src, out.at[z, x, c], send_a.at[t, d - 1], recv_a.at[t, d - 1],
-                device_id=(e, (z + d) % nz, x, c), device_id_type=MESH_ID)
+                src, out.at[zz, xs, c], send_c.at[dc - 1, xs, zz], recv_c.at[dc - 1, xs, zz],
+                device_id=(e, z, x, (c + dc) % nc), device_id_type=MESH_ID)
             cp.start()
             sends.append(cp)
-    for t, (src, out) in enumerate(pairs):
-        for d in range(1, nz):
-            zs = (z + nz - d) % nz
+
+    forward(xa, z, x, True)
+    for d in range(1, nz):
+        zs = (z + nz - d) % nz
+        pltpu.make_async_remote_copy(
+            xa, out.at[zs, x, c], send_a.at[d - 1], recv_a.at[d - 1],
+            device_id=(e, zs, x, c), device_id_type=MESH_ID).wait_recv()
+        forward(out.at[zs, x, c], zs, x, True)
+    for dx in range(1, nx):
+        xs = (x + nx - dx) % nx
+        for zz in range(nz):
             pltpu.make_async_remote_copy(
-                src, out.at[zs, x, c], send_a.at[t, d - 1], recv_a.at[t, d - 1],
-                device_id=(e, zs, x, c), device_id_type=MESH_ID).wait_recv()
-    for cp in locals_:
-        cp.wait()
-    for t, (src, out) in enumerate(pairs):
-        for d in range(1, nx):
-            cp = pltpu.make_async_remote_copy(
-                out.at[:, x, c], out.at[:, x, c], send_b.at[t, d - 1], recv_b.at[t, d - 1],
-                device_id=(e, z, (x + d) % nx, c), device_id_type=MESH_ID)
-            cp.start()
-            sends.append(cp)
-    for t, (src, out) in enumerate(pairs):
-        for d in range(1, nx):
-            xs = (x + nx - d) % nx
-            pltpu.make_async_remote_copy(
-                out.at[:, xs, c], out.at[:, xs, c], send_b.at[t, d - 1], recv_b.at[t, d - 1],
+                xa, out.at[zz, xs, c], send_b.at[dx - 1, zz], recv_b.at[dx - 1, zz],
                 device_id=(e, z, xs, c), device_id_type=MESH_ID).wait_recv()
-    for t, (src, out) in enumerate(pairs):
-        for d in range(1, nc):
-            cp = pltpu.make_async_remote_copy(
-                out.at[:, :, c], out.at[:, :, c], send_c.at[t, d - 1], recv_c.at[t, d - 1],
-                device_id=(e, z, x, (c + d) % nc), device_id_type=MESH_ID)
-            cp.start()
-            sends.append(cp)
-    for t, (src, out) in enumerate(pairs):
-        for d in range(1, nc):
-            cs = (c + nc - d) % nc
-            pltpu.make_async_remote_copy(
-                out.at[:, :, cs], out.at[:, :, cs], send_c.at[t, d - 1], recv_c.at[t, d - 1],
-                device_id=(e, z, x, cs), device_id_type=MESH_ID).wait_recv()
+            forward(out.at[zz, xs, c], zz, xs, False)
+    for dc in range(1, nc):
+        cs = (c + nc - dc) % nc
+        for xx in range(nx):
+            for zz in range(nz):
+                pltpu.make_async_remote_copy(
+                    xa, out.at[zz, xx, cs], send_c.at[dc - 1, xx, zz], recv_c.at[dc - 1, xx, zz],
+                    device_id=(e, z, x, cs), device_id_type=MESH_ID).wait_recv()
+    local.wait()
     for cp in sends:
         cp.wait_send()
 
@@ -145,15 +145,15 @@
             pltpu.VMEM((ne, two_feats, blk), sent.dtype),
             pltpu.VMEM((ne, 1, blk), gsend.dtype),
             pltpu.VMEM((feats, 2 * cols), sent.dtype),
-            dma((4,)),
+            dma((3,)),
             dma((2, max(ne - 1, 1))),
             dma((2, ne)),
-            dma((2, max(nz - 1, 1))),
-            dma((2, max(nz - 1, 1))),
-            dma((2, max(nx - 1, 1))),
-            dma((2, max(nx - 1, 1))),
-            dma((2, max(nc - 1, 1))),
-            dma((2, max(nc - 1, 1))),
+            dma((max(nz - 1, 1),)),
+            dma((max(nz - 1, 1),)),
+            dma((max(nx - 1, 1), nz)),
+            dma((max(nx - 1, 1), nz)),
+            dma((max(nc - 1, 1), nx, nz)),
+            dma((max(nc - 1, 1), nx, nz)),
         ],
         compiler_params=pltpu.CompilerParams(collective_id=0, has_side_effects=True),
     )(sent, gsend)

time: 131 us -> 126 us (0.962)
  Pallas kernels: 91.1 us -> 87.2 us
    pallas_call x1, Pallas kernels: 45.5 us -> 41.4 us  [ep_etp_gather(): pl.pallas_call(functools.partial(_gather_kernel, ne, nz, nx, nc), out_sha...]
where the time goes in v7:
time: 126 us; the launch traced here: 125 us
  Pallas kernels  87.2 us (69%)
  local copies, waits for them, and re-layouts  22.9 us (18%)
  matrix products  8.77 us (7%)
  other arithmetic  5.6 us (4%)
    pallas_call x1, Pallas kernels, etp_reduce_scatter(): pl.pallas_call(functools.partial(_rs_kernel, ne, nz, nx, nc), out_shape=j...  45.8 us
    pallas_call x1, Pallas kernels, ep_etp_gather(): pl.pallas_call(functools.partial(_gather_kernel, ne, nz, nx, nc), out_sha...  41.4 us
    reshape x1, local copies, waits for them, and re-layouts, per_device(): part = out_t.reshape(nz, nx, nc, width // 2, 2 * rows)  4.22 us
    unnamed x15, local copies, waits for them, and re-layouts  3.68 us
    dot_general x1, local copies, waits for them, and re-layouts, per_device(): out_t = lax.dot_general(wd, hidden, dims(0, 1), preferred_element_type=f32)  3.41 us

profile of v7, /device:TPU:6, one launch (start us, length us, event | category | flops | bytes accessed | tf_op | source)
XLA Modules:
  0.0 125.3 jit_solution(5453557064260397719)
XLA Ops:
  0.6 0.0 copy-start
  0.6 0.8 copy.22
  1.5 0.1 eq.15
  1.6 0.1 fusion.13
  1.7 0.1 reduce_window_sum.11
  1.8 0.2 select_reduce_fusion
  2.0 0.7 broadcast_multiply_fusion
  2.7 0.1 copy.21
  2.8 0.1 mul.71
  2.9 0.9 scatter_custom_fusion
  3.9 0.8 copy.20
  4.6 0.1 reshape.78
  4.7 0.1 pad_maximum_fusion
  4.8 1.6 %gather_fusion.1 = f32[192]{0:T(256)S(1)} fusion(f32[97]{0:T(128)S(1)} %pad_maximum_fusion, s32[1024]{0:T(1024)S(1)} %get-tuple-element.27), kind=kCustom, calls=%fused_computation.1 | custom fusion | bytes 2304 | tf_op jit(solution)/shard_map/gather | solution.py:310
  6.4 0.7 reshape.79.g_ref
  7.1 0.8 fusion.17
  7.9 0.8 gather_fusion
  8.7 0.8 copy.23
  9.5 41.4 %shard_map.110 = (bf16[8,4,2,48,384]{4,3,2,1,0:T(8,128)(2,1)}, f32[1,192]{1,0:T(1,128)}) custom-call(bf16[8,96,24]{2,1,0:T(8,128)(2,1)} %bitcast.60, f32[8,1,24]{2,1,0:T(1,128)} %reshape.79.g_ref), custom_call_target="tpu_custom_call" | custom-call | tf_op jit(solution)/shard_map/pallas_call | solution.py:139
  50.9 2.1 %multiply_convert_fusion.1 = bf16[8,4,2,48,192]{4,3,2,1,0:T(8,128)(2,1)S(1)} fusion(f32[192]{0:T(256)} %bitcast.64, bf16[8,4,2,48,384]{4,3,2,1,0:T(8,128)(2,1)} %get-tuple-element.7), kind=kLoop, calls=%fused_computation.13 | loop fusion | flops 1769472 | bytes 2360064 | tf_op jit(solution)/shard_map/convert_element_type | solution.py:321
  53.0 0.0 copy-start.2
  53.0 0.0 copy-done
  53.0 0.6 fusion.4
  53.6 1.0 copy-done.2
  54.7 0.0 copy-start.3
  54.7 0.8 slice_convert_fusion
  55.4 0.0 copy-start.1
  55.4 0.4 copy-done.3
  55.8 0.6 fusion.9
  56.4 0.0 copy-start.5
  56.4 1.5 %fusion.1 = bf16[1,3072,128]{2,1,0:T(8,128)(2,1)} fusion(bf16[3072,192]{1,0:T(8,128)(2,1)S(1)} %bitcast.55, f32[192,128]{1,0:T(8,128)S(1)} %fusion.4, f32[192,128]{1,0:T(8,128)S(1)} %fusion.9), kind=kOutput, calls=%fused_computation.10 | convolution fusion | flops 151535616 | bytes 2162688 | tf_op jit(solution)/shard_map/dot_general | solution.py:337
  57.9 0.0 copy-done.5
  57.9 0.6 multiply_convert_fusion.5
  58.5 0.0 copy-start.4
  58.5 1.5 %fusion = bf16[1,3072,128]{2,1,0:T(8,128)(2,1)} fusion(bf16[3072,192]{1,0:T(8,128)(2,1)S(1)} %bitcast.57, f32[192,128]{1,0:T(8,128)S(1)} %fusion.9, f32[192,128]{1,0:T(8,128)S(1)} %fusion.4, f32[192,128]{1,0:T(8,128)S(1)} %get-tuple-element.24), kind=kOutput, calls=%fused_computation.9 | convolution fusion | flops 151633920 | bytes 2260992 | tf_op jit(solution)/shard_map/dot_general | solution.py:336
  60.0 0.0 copy-done.1
  60.0 0.0 copy-done.4
  60.0 1.6 %fusion.2 = bf16[1,128,3072]{2,1,0:T(8,128)(2,1)} fusion(bf16[192,128]{1,0:T(8,128)(2,1)S(1)} %get-tuple-element.23, f32[3072,192]{1,0:T(8,128)S(1)} %bitcast.52, f32[192]{0:T(256)S(1)} %bitcast.65), kind=kOutput, calls=%fused_computation.11 | convolution fusion | flops 152567808 | bytes 3195648 | tf_op jit(solution)/shard_map/dot_general | solution.py:335
  61.6 2.3 %copy.26 = f32[3072,192]{0,1:T(8,128)S(1)} copy(f32[3072,192]{1,0:T(8,128)} %bitcast.53) | data formatting | bytes 4718592 | tf_op jit(solution)/shard_map/convert_element_type | solution.py:338
  63.9 2.5 %multiply_reduce_fusion = (f32[192]{0:T(256)}, f32[3072,192]{0,1:T(8,128)}) fusion(f32[3072,192]{0,1:T(8,128)S(1)} %copy.26, bf16[192,128]{1,0:T(8,128)(2,1)S(1)} %get-tuple-element.23, bf16[1,128,3072]{2,1,0:T(8,128)(2,1)S(1)} %copy-done), kind=kOutput, calls=%fused_computation.14 | convolution fusion | flops 152174400 | bytes 5554944 | tf_op jit(solution)/shard_map/dot_general | solution.py:331
  66.4 3.4 %copy.25 = f32[3072,192]{1,0:T(8,128)} copy(f32[3072,192]{0,1:T(8,128)} %get-tuple-element.26) | data formatting | bytes 4718592 | tf_op jit(solution)/shard_map/dot_general | solution.py:331
  69.8 4.2 %reshape.81.part_ref = f32[8,4,2,24,384]{4,3,2,1,0:T(8,128)} reshape(f32[3072,192]{1,0:T(8,128)} %copy.25) | data formatting | bytes 4718592 | tf_op jit(solution)/shard_map/reshape | solution.py:339
  74.0 45.8 %shard_map.111 = f32[8,56,24]{2,1,0:T(8,128)} custom-call(f32[8,4,2,24,384]{4,3,2,1,0:T(8,128)} %reshape.81.part_ref, f32[1,192]{1,0:T(1,128)} %bitcast.66), custom_call_target="tpu_custom_call" | custom-call | tf_op jit(solution)/shard_map/pallas_call | solution.py:262
  119.8 0.9 slice.14
  120.7 0.1 copy.31
  120.8 0.1 reshape.83
  120.9 0.1 copy.28
  121.0 0.6 gather_fusion.2
  121.7 0.7 multiply_reduce_fusion.1
  122.4 0.8 slice_reduce_fusion
  123.2 0.1 reshape_squeeze.3
  123.3 1.3 %gather_fusion.3 = f32[96]{0:T(128)S(1)} fusion(f32[192]{0:T(256)S(1)} %reshape_squeeze.3, s32[1024]{0:T(1024)S(1)} %pad_clamp_fusion), kind=kCustom, calls=%fused_computation.3 | custom fusion | bytes 1152 | tf_op jit(solution)/shard_map/gather | solution.py:347
  124.5 0.1 reshape.85
  124.7 0.6 copy.29
  (5 shorter events, 0.0 us)
Async XLA Ops:
  0.6 52.4 %copy-start = (bf16[1,128,3072]{2,1,0:T(8,128)(2,1)S(1)}, bf16[1,128,3072]{2,1,0:T(8,128)(2,1)}, u32[]{:S(2)}) copy-start(bf16[1,128,3072]{2,1,0:T(8,128)(2,1)} %param.13) | copy-start | bytes 2359300
  53.0 1.7 %copy-start.2 = (bf16[8,4,2,48,384]{4,3,2,1,0:T(8,128)(2,1)S(1)}, bf16[8,4,2,48,384]{4,3,2,1,0:T(8,128)(2,1)}, u32[]{:S(2)}) copy-start(bf16[8,4,2,48,384]{4,3,2,1,0:T(8,128)(2,1)} %get-tuple-element.7) | copy-start | bytes 7077892
  54.7 1.1 copy-start.3
  55.4 4.6 %copy-start.1 = (f32[8,4,2,48,192]{4,3,2,1,0:T(8,128)}, f32[8,4,2,48,192]{4,3,2,1,0:T(8,128)S(1)}, u32[]{:S(2)}) copy-start(f32[8,4,2,48,192]{4,3,2,1,0:T(8,128)S(1)} %get-tuple-element.19) | copy-start | bytes 7077892
  56.4 1.5 %copy-start.5 = (bf16[1,3072,128]{2,1,0:T(8,128)(2,1)S(1)}, bf16[1,3072,128]{2,1,0:T(8,128)(2,1)}, u32[]{:S(2)}) copy-start(bf16[1,3072,128]{2,1,0:T(8,128)(2,1)} %param.12) | copy-start | bytes 2359300
  58.5 1.5 %copy-start.4 = (f32[1,192]{1,0:T(1,128)S(1)}, f32[1,192]{1,0:T(1,128)}, u32[]{:S(2)}) copy-start(f32[1,192]{1,0:T(1,128)} %get-tuple-element.8) | copy-start | bytes 2308

commit v8 on v7

--- a/solution.py
+++ b/solution.py
@@ -159,8 +159,8 @@
     )(sent, gsend)
 
 
-def _rs_kernel(ne, nz, nx, nc, part_ref, inner_ref, out_ref, recv_c, acc1, recv_b, acc2, recv_a,
-               ir_c, in1, ir_b, in2, ir_a, fin,
+def _rs_kernel(ne, nz, nx, nc, part_ref, partb_ref, inner_ref, out_ref, recv_c, acc1, acc1b, recv_b, acc2, acc2b,
+               recv_a, ir_c, in1, ir_b, in2, ir_a, fin,
                sem_local, send_c, rsem_c, send_b, rsem_b, send_a, rsem_a, send_d, rsem_d):
     e, z, x, c = _coords()
     _barrier(ne, nz, nx, nc, True)
@@ -182,7 +182,7 @@
                     device_id=peers_of[d][1], device_id_type=MESH_ID).wait_recv()
 
     peers = [((e, z, x, (c + d) % nc), (e, z, x, (c + nc - d) % nc)) for d in range(1, nc)]
-    exchange([(lambda d: part_ref.at[:, :, (c + d + 1) % nc], recv_c), (lambda d: inner_ref, ir_c)],
+    exchange([(lambda d: partb_ref.at[:, :, (c + d + 1) % nc], recv_c), (lambda d: inner_ref, ir_c)],
              peers, send_c, rsem_c)
 
     def sum_c(i, carry):
@@ -190,8 +190,9 @@
         xi = i % nx
         total = part_ref[zi, xi, c]
         for d in range(nc - 1):
-            total = total + recv_c[d, zi, xi]
+            total = total + recv_c[d, zi, xi].astype(jnp.float32)
         acc1[zi, xi] = total
+        acc1b[zi, xi] = total.astype(acc1b.dtype)
         return carry
     lax.fori_loop(0, nz * nx, sum_c, 0)
     total = inner_ref[...]
@@ -200,14 +201,15 @@
     in1[...] = total
 
     peers = [((e, z, (x + d) % nx, c), (e, z, (x + nx - d) % nx, c)) for d in range(1, nx)]
-    exchange([(lambda d: acc1.at[:, (x + d + 1) % nx], recv_b), (lambda d: in1, ir_b)],
+    exchange([(lambda d: acc1b.at[:, (x + d + 1) % nx], recv_b), (lambda d: in1, ir_b)],
              peers, send_b, rsem_b)
 
     def sum_b(zi, carry):
         total = acc1[zi, x]
         for d in range(nx - 1):
-            total = total + recv_b[d, zi]
+            total = total + recv_b[d, zi].astype(jnp.float32)
         acc2[zi] = total
+        acc2b[zi] = total.astype(acc2b.dtype)
         return carry
     lax.fori_loop(0, nz, sum_b, 0)
     total = in1[...]
@@ -216,11 +218,11 @@
     in2[...] = total
 
     peers = [((e, (z + d) % nz, x, c), (e, (z + nz - d) % nz, x, c)) for d in range(1, nz)]
-    exchange([(lambda d: acc2.at[(z + d + 1) % nz], recv_a), (lambda d: in2, ir_a)],
+    exchange([(lambda d: acc2b.at[(z + d + 1) % nz], recv_a), (lambda d: in2, ir_a)],
              peers, send_a, rsem_a)
     total = acc2[z]
     for d in range(nz - 1):
-        total = total + recv_a[d]
+        total = total + recv_a[d].astype(jnp.float32)
     itotal = in2[...]
     for d in range(nz - 1):
         itotal = itotal + ir_a[d]
@@ -253,6 +255,7 @@
 
 
 def etp_reduce_scatter(part, inner, ne, blk):
+    bf16 = jnp.bfloat16
     nz, nx, nc, feats, cols = part.shape
     pad_rows = -(-(2 * feats + 1) // 8) * 8
     f32 = jnp.float32
@@ -262,14 +265,16 @@
     return pl.pallas_call(
         functools.partial(_rs_kernel, ne, nz, nx, nc),
         out_shape=jax.ShapeDtypeStruct((ne, pad_rows, blk), f32),
-        in_specs=[pl.BlockSpec(memory_space=vmem)] * 2,
+        in_specs=[pl.BlockSpec(memory_space=vmem)] * 3,
         out_specs=pl.BlockSpec(memory_space=vmem),
         scratch_shapes=[
-            pltpu.VMEM((mc, nz, nx, feats, cols), f32),
+            pltpu.VMEM((mc, nz, nx, feats, cols), bf16),
             pltpu.VMEM((nz, nx, feats, cols), f32),
-            pltpu.VMEM((mx, nz, feats, cols), f32),
+            pltpu.VMEM((nz, nx, feats, cols), bf16),
+            pltpu.VMEM((mx, nz, feats, cols), bf16),
             pltpu.VMEM((nz, feats, cols), f32),
-            pltpu.VMEM((mz, feats, cols), f32),
+            pltpu.VMEM((nz, feats, cols), bf16),
+            pltpu.VMEM((mz, feats, cols), bf16),
             pltpu.VMEM((mc, 1, cols // 2), f32),
             pltpu.VMEM((1, cols // 2), f32),
             pltpu.VMEM((mx, 1, cols // 2), f32),
@@ -287,7 +292,7 @@
             dma((ne,)),
         ],
         compiler_params=pltpu.CompilerParams(collective_id=1, has_side_effects=True),
-    )(part, inner)
+    )(part, part.astype(bf16), inner)
 
 
 def per_device(tokens, routes, route_gates, cotangent, w_gate, w_up, w_down):

time: 126 us -> 116 us (0.921)
  Pallas kernels: 87.2 us -> 76.7 us
  other arithmetic: 5.6 us -> 6.86 us
    pallas_call x1, Pallas kernels: 45.8 us -> 35.3 us  [etp_reduce_scatter(): pl.pallas_call(functools.partial(_rs_kernel, ne, nz, nx, nc), out_shape=j...]
    reshape x1, local copies, waits for them, and re-layouts: 4.22 us -> 2.88 us  [per_device(): part = out_t.reshape(nz, nx, nc, width // 2, 2 * rows)]
    convert_element_type x0 -> x1, other arithmetic: none -> 1.26 us  [etp_reduce_scatter(): part.astype(bf16)]
    unnamed x15 -> x17, local copies, waits for them, and re-layouts: 3.68 us -> 4.18 us
where the time goes in v8:
time: 116 us; the launch traced here: 115 us
  Pallas kernels  76.7 us (66%)
  local copies, waits for them, and re-layouts  22 us (19%)
  matrix products  8.77 us (8%)
  other arithmetic  6.86 us (6%)
    pallas_call x1, Pallas kernels, ep_etp_gather(): pl.pallas_call(functools.partial(_gather_kernel, ne, nz, nx, nc), out_sha...  41.4 us
    pallas_call x1, Pallas kernels, etp_reduce_scatter(): pl.pallas_call(functools.partial(_rs_kernel, ne, nz, nx, nc), out_shape=j...  35.3 us
    unnamed x17, local copies, waits for them, and re-layouts  4.18 us
    dot_general x1, local copies, waits for them, and re-layouts, per_device(): out_t = lax.dot_general(wd, hidden, dims(0, 1), preferred_element_type=f32)  3.41 us
    reshape x1, local copies, waits for them, and re-layouts, per_device(): part = out_t.reshape(nz, nx, nc, width // 2, 2 * rows)  2.88 us
    dot_general x1, matrix products, per_device(): out_t = lax.dot_general(wd, hidden, dims(0, 1), preferred_element_type=f32)  2.47 us
    convert_element_type x1, local copies, waits for them, and re-layouts, per_device(): inner = jnp.sum(out_t * ct.astype(f32), axis=0, keepdims=True)  2.35 us

profile of v8, /device:TPU:6, one launch (start us, length us, event | category | flops | bytes accessed | tf_op | source)
XLA Modules:
  0.0 115.3 jit_solution(7249064889687841456)
XLA Ops:
  0.6 0.0 copy-start
  0.6 0.8 copy.22
  1.5 0.1 eq.15
  1.6 0.1 fusion.13
  1.7 0.1 reduce_window_sum.11
  1.8 0.2 select_reduce_fusion
  2.0 0.7 broadcast_multiply_fusion
  2.7 0.1 copy.21
  2.8 0.1 mul.71
  2.9 0.9 scatter_custom_fusion
  3.9 0.8 copy.20
  4.6 0.1 reshape.78
  4.7 0.1 pad_maximum_fusion
  4.8 1.6 %gather_fusion.1 = f32[192]{0:T(256)S(1)} fusion(f32[97]{0:T(128)S(1)} %pad_maximum_fusion, s32[1024]{0:T(1024)S(1)} %get-tuple-element.27), kind=kCustom, calls=%fused_computation.1 | custom fusion | bytes 2304 | tf_op jit(solution)/shard_map/gather | solution.py:315
  6.4 0.7 reshape.79.g_ref
  7.1 0.8 fusion.17
  7.9 0.8 gather_fusion
  8.7 0.8 copy.23
  9.5 41.4 %shard_map.110 = (bf16[8,4,2,48,384]{4,3,2,1,0:T(8,128)(2,1)}, f32[1,192]{1,0:T(1,128)}) custom-call(bf16[8,96,24]{2,1,0:T(8,128)(2,1)} %bitcast.60, f32[8,1,24]{2,1,0:T(1,128)} %reshape.79.g_ref), custom_call_target="tpu_custom_call" | custom-call | tf_op jit(solution)/shard_map/pallas_call | solution.py:139
  50.9 2.1 %multiply_convert_fusion.1 = bf16[8,4,2,48,192]{4,3,2,1,0:T(8,128)(2,1)S(1)} fusion(f32[192]{0:T(256)} %bitcast.64, bf16[8,4,2,48,384]{4,3,2,1,0:T(8,128)(2,1)} %get-tuple-element.7), kind=kLoop, calls=%fused_computation.13 | loop fusion | flops 1769472 | bytes 2360064 | tf_op jit(solution)/shard_map/convert_element_type | solution.py:326
  53.0 0.0 copy-start.3
  53.0 0.0 copy-done
  53.0 0.6 fusion.4
  53.6 1.0 copy-done.3
  54.7 0.0 copy-start.4
  54.7 0.8 slice_convert_fusion
  55.4 0.0 copy-start.1
  55.4 0.4 copy-done.4
  55.8 0.6 fusion.9
  56.4 0.0 copy-start.6
  56.4 1.5 %fusion.1 = bf16[1,3072,128]{2,1,0:T(8,128)(2,1)} fusion(bf16[3072,192]{1,0:T(8,128)(2,1)S(1)} %bitcast.55, f32[192,128]{1,0:T(8,128)S(1)} %fusion.4, f32[192,128]{1,0:T(8,128)S(1)} %fusion.9), kind=kOutput, calls=%fused_computation.10 | convolution fusion | flops 151535616 | bytes 2162688 | tf_op jit(solution)/shard_map/dot_general | solution.py:342
  57.9 0.0 copy-done.6
  57.9 0.6 multiply_convert_fusion.5
  58.5 0.0 copy-start.5
  58.5 1.5 %fusion = bf16[1,3072,128]{2,1,0:T(8,128)(2,1)} fusion(bf16[3072,192]{1,0:T(8,128)(2,1)S(1)} %bitcast.57, f32[192,128]{1,0:T(8,128)S(1)} %fusion.9, f32[192,128]{1,0:T(8,128)S(1)} %fusion.4, f32[192,128]{1,0:T(8,128)S(1)} %get-tuple-element.24), kind=kOutput, calls=%fused_computation.9 | convolution fusion | flops 151633920 | bytes 2260992 | tf_op jit(solution)/shard_map/dot_general | solution.py:341
  60.0 0.0 copy-done.1
  60.0 0.0 copy-done.5
  60.0 1.6 %fusion.2 = bf16[1,128,3072]{2,1,0:T(8,128)(2,1)} fusion(bf16[192,128]{1,0:T(8,128)(2,1)S(1)} %get-tuple-element.23, f32[3072,192]{1,0:T(8,128)S(1)} %bitcast.52, f32[192]{0:T(256)S(1)} %bitcast.65), kind=kOutput, calls=%fused_computation.11 | convolution fusion | flops 152567808 | bytes 3195648 | tf_op jit(solution)/shard_map/dot_general | solution.py:340
  61.6 2.3 %copy.26 = f32[3072,192]{0,1:T(8,128)S(1)} copy(f32[3072,192]{1,0:T(8,128)} %bitcast.53) | data formatting | bytes 4718592 | tf_op jit(solution)/shard_map/convert_element_type | solution.py:343
  63.9 2.5 %multiply_reduce_fusion = (f32[192]{0:T(256)}, f32[3072,192]{0,1:T(8,128)}) fusion(f32[3072,192]{0,1:T(8,128)S(1)} %copy.26, bf16[192,128]{1,0:T(8,128)(2,1)S(1)} %get-tuple-element.23, bf16[1,128,3072]{2,1,0:T(8,128)(2,1)S(1)} %copy-done), kind=kOutput, calls=%fused_computation.14 | convolution fusion | flops 152174400 | bytes 5554944 | tf_op jit(solution)/shard_map/dot_general | solution.py:336
  66.4 3.4 %copy.25 = f32[3072,192]{1,0:T(8,128)} copy(f32[3072,192]{0,1:T(8,128)} %get-tuple-element.26) | data formatting | bytes 4718592 | tf_op jit(solution)/shard_map/dot_general | solution.py:336
  69.8 2.9 %reshape.81.part_ref = f32[8,4,2,24,384]{4,3,2,1,0:T(8,128)S(1)} reshape(f32[3072,192]{1,0:T(8,128)} %copy.25) | data formatting | bytes 4718592 | tf_op jit(solution)/shard_map/reshape | solution.py:344
  72.7 0.0 copy-start.2
  72.7 1.3 %convert_element_type.47.partb_ref = bf16[8,4,2,24,384]{4,3,2,1,0:T(8,128)(2,1)} convert(f32[8,4,2,24,384]{4,3,2,1,0:T(8,128)S(1)} %reshape.81.part_ref) | non-fusion elementwise | flops 589824 | bytes 3538944 | tf_op jit(solution)/shard_map/convert_element_type | solution.py:295
  73.9 0.5 copy-done.2
  74.4 35.3 %shard_map.111 = f32[8,56,24]{2,1,0:T(8,128)} custom-call(f32[8,4,2,24,384]{4,3,2,1,0:T(8,128)} %copy-done.2, bf16[8,4,2,24,384]{4,3,2,1,0:T(8,128)(2,1)} %convert_element_type.47.partb_ref, f32[1,192]{1,0:T(1,128)} %bitcast.66), custom_call_target="tpu_custom_call" | custom-call | tf_op jit(solution)/shard_map/pallas_call | solution.py:265
  109.8 0.9 slice.14
  110.7 0.1 copy.31
  110.8 0.1 reshape.83
  110.9 0.1 copy.28
  111.0 0.6 gather_fusion.2
  111.7 0.7 multiply_reduce_fusion.1
  112.4 0.8 slice_reduce_fusion
  113.2 0.1 reshape_squeeze.3
  113.3 1.3 %gather_fusion.3 = f32[96]{0:T(128)S(1)} fusion(f32[192]{0:T(256)S(1)} %reshape_squeeze.3, s32[1024]{0:T(1024)S(1)} %pad_clamp_fusion), kind=kCustom, calls=%fused_computation.3 | custom fusion | bytes 1152 | tf_op jit(solution)/shard_map/gather | solution.py:352
  114.5 0.1 reshape.85
  114.6 0.6 copy.29
  (5 shorter events, 0.0 us)
Async XLA Ops:
  0.6 52.4 %copy-start = (bf16[1,128,3072]{2,1,0:T(8,128)(2,1)S(1)}, bf16[1,128,3072]{2,1,0:T(8,128)(2,1)}, u32[]{:S(2)}) copy-start(bf16[1,128,3072]{2,1,0:T(8,128)(2,1)} %param.13) | copy-start | bytes 2359300
  53.0 1.7 %copy-start.3 = (bf16[8,4,2,48,384]{4,3,2,1,0:T(8,128)(2,1)S(1)}, bf16[8,4,2,48,384]{4,3,2,1,0:T(8,128)(2,1)}, u32[]{:S(2)}) copy-start(bf16[8,4,2,48,384]{4,3,2,1,0:T(8,128)(2,1)} %get-tuple-element.7) | copy-start | bytes 7077892
  54.7 1.1 copy-start.4
  55.4 4.5 %copy-start.1 = (f32[8,4,2,48,192]{4,3,2,1,0:T(8,128)}, f32[8,4,2,48,192]{4,3,2,1,0:T(8,128)S(1)}, u32[]{:S(2)}) copy-start(f32[8,4,2,48,192]{4,3,2,1,0:T(8,128)S(1)} %get-tuple-element.19) | copy-start | bytes 7077892
  56.4 1.5 %copy-start.6 = (bf16[1,3072,128]{2,1,0:T(8,128)(2,1)S(1)}, bf16[1,3072,128]{2,1,0:T(8,128)(2,1)}, u32[]{:S(2)}) copy-start(bf16[1,3072,128]{2,1,0:T(8,128)(2,1)} %param.12) | copy-start | bytes 2359300
  58.5 1.5 %copy-start.5 = (f32[1,192]{1,0:T(1,128)S(1)}, f32[1,192]{1,0:T(1,128)}, u32[]{:S(2)}) copy-start(f32[1,192]{1,0:T(1,128)} %get-tuple-element.8) | copy-start | bytes 2308
  72.7 1.8 %copy-start.2 = (f32[8,4,2,24,384]{4,3,2,1,0:T(8,128)}, f32[8,4,2,24,384]{4,3,2,1,0:T(8,128)S(1)}, u32[]{:S(2)}) copy-start(f32[8,4,2,24,384]{4,3,2,1,0:T(8,128)S(1)} %reshape.81.part_ref) | copy-start | bytes 7077892

commit v9 on v8

--- a/solution.py
+++ b/solution.py
@@ -340,7 +340,8 @@
     grad_down = lax.dot_general(hidden, dyt, dims(0, 1), preferred_element_type=f32)
     grad_gate_w = lax.dot_general(xt, d_gate, dims(1, 0), preferred_element_type=f32)
     grad_up_w = lax.dot_general(xt, d_up, dims(1, 0), preferred_element_type=f32)
-    inner = jnp.sum(out_t * ct.astype(f32), axis=0, keepdims=True)
+    wd_cot = lax.dot_general(wd, ct, dims(1, 0), preferred_element_type=f32)
+    inner = jnp.sum(hidden.astype(f32) * wd_cot.T, axis=1)[None, :]
     part = out_t.reshape(nz, nx, nc, width // 2, 2 * rows)
     back = etp_reduce_scatter(part, inner, ep_count, CAP)
     half = width // 2

time: 116 us -> 112 us (0.966)
  local copies, waits for them, and re-layouts: 22 us -> 19.6 us
    convert_element_type x1 -> x0, local copies, waits for them, and re-layouts: 2.35 us -> none  [per_device(): inner = jnp.sum(out_t * ct.astype(f32), axis=0, keepdims=True)]
    dot_general x1, matrix products: 2.47 us -> 0.45 us  [per_device(): out_t = lax.dot_general(wd, hidden, dims(0, 1), preferred_element_type=f32)]
    dot_general x0 -> x1, matrix products: none -> 1.36 us  [per_device(): wd_cot = lax.dot_general(wd, ct, dims(1, 0), preferred_element_type=f32)]
    unnamed x17 -> x15, local copies, waits for them, and re-layouts: 4.18 us -> 4.32 us
where the time goes in v9:
time: 112 us; the launch traced here: 111 us
  Pallas kernels  76.8 us (69%)
  local copies, waits for them, and re-layouts  19.6 us (18%)
  matrix products  8.12 us (7%)
  other arithmetic  6.17 us (6%)
    pallas_call x1, Pallas kernels, ep_etp_gather(): pl.pallas_call(functools.partial(_gather_kernel, ne, nz, nx, nc), out_sha...  41.4 us
    pallas_call x1, Pallas kernels, etp_reduce_scatter(): pl.pallas_call(functools.partial(_rs_kernel, ne, nz, nx, nc), out_shape=j...  35.3 us
    unnamed x15, local copies, waits for them, and re-layouts  4.32 us
    reshape x1, local copies, waits for them, and re-layouts, per_device(): part = out_t.reshape(nz, nx, nc, width // 2, 2 * rows)  2.88 us
    dot_general x1, local copies, waits for them, and re-layouts, per_device(): out_t = lax.dot_general(wd, hidden, dims(0, 1), preferred_element_type=f32)  2.32 us

profile of v9, /device:TPU:6, one launch (start us, length us, event | category | flops | bytes accessed | tf_op | source)
XLA Modules:
  0.0 111.5 jit_solution(9049189887752979081)
XLA Ops:
  0.6 0.0 copy-start
  0.7 0.8 broadcast_multiply_fusion
  1.4 0.8 fusion.19
  2.2 0.1 copy.20
  2.3 0.1 mul.71
  2.4 0.8 copy.19
  3.2 0.1 reshape.78
  3.3 0.1 pad_maximum_fusion
  3.4 0.8 copy.21
  4.2 0.1 eq.15
  4.3 0.1 fusion.15
  4.4 0.1 reduce_window_sum.11
  4.5 0.2 select_reduce_fusion
  4.7 0.9 scatter_custom_fusion
  5.6 1.6 %gather_fusion.1 = f32[192]{0:T(256)S(1)} fusion(f32[97]{0:T(128)S(1)} %pad_maximum_fusion, s32[1024]{0:T(1024)S(1)} %get-tuple-element.25), kind=kCustom, calls=%fused_computation.1 | custom fusion | bytes 2304 | tf_op jit(solution)/shard_map/gather | solution.py:315
  7.2 0.7 reshape.79.g_ref
  7.9 0.8 gather_fusion
  8.7 0.8 copy.22
  9.5 41.4 %shard_map.110 = (bf16[8,4,2,48,384]{4,3,2,1,0:T(8,128)(2,1)}, f32[1,192]{1,0:T(1,128)}) custom-call(bf16[8,96,24]{2,1,0:T(8,128)(2,1)} %bitcast.62, f32[8,1,24]{2,1,0:T(1,128)} %reshape.79.g_ref), custom_call_target="tpu_custom_call" | custom-call | tf_op jit(solution)/shard_map/pallas_call | solution.py:139
  50.9 2.1 %multiply_convert_fusion.1 = bf16[8,4,2,48,192]{4,3,2,1,0:T(8,128)(2,1)S(1)} fusion(f32[192]{0:T(256)} %bitcast.66, bf16[8,4,2,48,384]{4,3,2,1,0:T(8,128)(2,1)} %get-tuple-element.7), kind=kLoop, calls=%fused_computation.13 | loop fusion | flops 1769472 | bytes 2360064 | tf_op jit(solution)/shard_map/convert_element_type | solution.py:326
  53.0 0.0 copy-start.2
  53.0 0.0 copy-done
  53.0 0.6 fusion.5
  53.6 1.0 copy-done.2
  54.7 0.0 copy-start.3
  54.7 0.8 fusion.25
  55.5 0.0 copy-start.5
  55.5 0.3 copy-done.3
  55.8 0.6 fusion.11
  56.4 0.3 copy-done.5
  56.7 0.6 multiply_convert_fusion.5
  57.3 0.0 copy-start.4
  57.3 1.4 %fusion.4 = f32[192]{0:T(256)} fusion(bf16[3072,192]{1,0:T(8,128)(2,1)S(1)} %bitcast.58, bf16[1,128,3072]{2,1,0:T(8,128)(2,1)S(1)} %copy-done, bf16[192,128]{1,0:T(8,128)(2,1)S(1)} %get-tuple-element.23), kind=kOutput, calls=%fused_computation.16 | convolution fusion | flops 151068480 | bytes 2016000 | tf_op jit(solution)/shard_map/dot_general | solution.py:343
  58.7 0.0 copy-done.4
  58.7 1.6 %fusion.2 = bf16[1,128,3072]{2,1,0:T(8,128)(2,1)} fusion(bf16[192,128]{1,0:T(8,128)(2,1)S(1)} %get-tuple-element.23, bf16[3072,192]{1,0:T(8,128)(2,1)S(1)} %bitcast.59, f32[192]{0:T(256)S(1)} %bitcast.67), kind=kOutput, calls=%fused_computation.11 | convolution fusion | flops 153157632 | bytes 2016000 | tf_op jit(solution)/shard_map/dot_general | solution.py:340
  60.3 1.5 %fusion = bf16[1,3072,128]{2,1,0:T(8,128)(2,1)} fusion(bf16[3072,192]{1,0:T(8,128)(2,1)S(1)} %bitcast.56, f32[192,128]{1,0:T(8,128)S(1)} %fusion.11, f32[192,128]{1,0:T(8,128)S(1)} %fusion.5, f32[192,128]{1,0:T(8,128)S(1)} %get-tuple-element.24), kind=kOutput, calls=%fused_computation.9 | convolution fusion | flops 151633920 | bytes 2260992 | tf_op jit(solution)/shard_map/dot_general | solution.py:341
  61.7 1.5 %fusion.1 = bf16[1,3072,128]{2,1,0:T(8,128)(2,1)} fusion(bf16[3072,192]{1,0:T(8,128)(2,1)S(1)} %bitcast.57, f32[192,128]{1,0:T(8,128)S(1)} %fusion.5, f32[192,128]{1,0:T(8,128)S(1)} %fusion.11), kind=kOutput, calls=%fused_computation.10 | convolution fusion | flops 151535616 | bytes 2162688 | tf_op jit(solution)/shard_map/dot_general | solution.py:342
  63.2 0.5 convolution_bitcast_fusion
  63.7 2.3 %copy.24 = f32[3072,192]{1,0:T(8,128)} copy(f32[3072,192]{0,1:T(8,128)S(1)} %convolution_bitcast_fusion) | data formatting | bytes 4718592 | tf_op jit(solution)/shard_map/dot_general | solution.py:336
  66.0 2.9 %reshape.81.part_ref = f32[8,4,2,24,384]{4,3,2,1,0:T(8,128)S(1)} reshape(f32[3072,192]{1,0:T(8,128)} %copy.24) | data formatting | bytes 4718592 | tf_op jit(solution)/shard_map/reshape | solution.py:345
  68.9 0.0 copy-start.1
  68.9 1.3 %convert_element_type.46.partb_ref = bf16[8,4,2,24,384]{4,3,2,1,0:T(8,128)(2,1)} convert(f32[8,4,2,24,384]{4,3,2,1,0:T(8,128)S(1)} %reshape.81.part_ref) | non-fusion elementwise | flops 589824 | bytes 3538944 | tf_op jit(solution)/shard_map/convert_element_type | solution.py:295
  70.1 0.5 copy-done.1
  70.6 35.3 %shard_map.111 = f32[8,56,24]{2,1,0:T(8,128)} custom-call(f32[8,4,2,24,384]{4,3,2,1,0:T(8,128)} %copy-done.1, bf16[8,4,2,24,384]{4,3,2,1,0:T(8,128)(2,1)} %convert_element_type.46.partb_ref, f32[1,192]{1,0:T(1,128)} %bitcast.68), custom_call_target="tpu_custom_call" | custom-call | tf_op jit(solution)/shard_map/pallas_call | solution.py:265
  106.0 0.8 slice_reduce_fusion
  106.8 0.9 slice.14
  107.7 0.1 reshape_squeeze.3
  107.8 1.3 %gather_fusion.3 = f32[96]{0:T(128)S(1)} fusion(f32[192]{0:T(256)S(1)} %reshape_squeeze.3, s32[1024]{0:T(1024)S(1)} %pad_clamp_fusion), kind=kCustom, calls=%fused_computation.3 | custom fusion | bytes 1152 | tf_op jit(solution)/shard_map/gather | solution.py:353
  109.1 0.1 copy.29
  109.1 0.1 reshape.84
  109.3 0.1 reshape.86
  109.4 0.6 copy.27
  110.0 0.1 copy.26
  110.1 0.6 gather_fusion.2
  110.7 0.7 multiply_reduce_fusion
  (5 shorter events, 0.0 us)
Async XLA Ops:
  0.6 52.4 %copy-start = (bf16[1,128,3072]{2,1,0:T(8,128)(2,1)S(1)}, bf16[1,128,3072]{2,1,0:T(8,128)(2,1)}, u32[]{:S(2)}) copy-start(bf16[1,128,3072]{2,1,0:T(8,128)(2,1)} %param.13) | copy-start | bytes 2359300
  53.0 1.7 %copy-start.2 = (bf16[8,4,2,48,384]{4,3,2,1,0:T(8,128)(2,1)S(1)}, bf16[8,4,2,48,384]{4,3,2,1,0:T(8,128)(2,1)}, u32[]{:S(2)}) copy-start(bf16[8,4,2,48,384]{4,3,2,1,0:T(8,128)(2,1)} %get-tuple-element.7) | copy-start | bytes 7077892
  54.7 1.1 %copy-start.3 = (bf16[1,3072,128]{2,1,0:T(8,128)(2,1)S(1)}, bf16[1,3072,128]{2,1,0:T(8,128)(2,1)}, u32[]{:S(2)}) copy-start(bf16[1,3072,128]{2,1,0:T(8,128)(2,1)} %param.11) | copy-start | bytes 2359300
  55.5 1.2 %copy-start.5 = (bf16[1,3072,128]{2,1,0:T(8,128)(2,1)S(1)}, bf16[1,3072,128]{2,1,0:T(8,128)(2,1)}, u32[]{:S(2)}) copy-start(bf16[1,3072,128]{2,1,0:T(8,128)(2,1)} %param.12) | copy-start | bytes 2359300
  57.3 1.4 %copy-start.4 = (f32[1,192]{1,0:T(1,128)S(1)}, f32[1,192]{1,0:T(1,128)}, u32[]{:S(2)}) copy-start(f32[1,192]{1,0:T(1,128)} %get-tuple-element.8) | copy-start | bytes 2308
  68.9 1.8 %copy-start.1 = (f32[8,4,2,24,384]{4,3,2,1,0:T(8,128)}, f32[8,4,2,24,384]{4,3,2,1,0:T(8,128)S(1)}, u32[]{:S(2)}) copy-start(f32[8,4,2,24,384]{4,3,2,1,0:T(8,128)S(1)} %reshape.81.part_ref) | copy-start | bytes 7077892

commit v10 on v9

--- a/solution.py
+++ b/solution.py
@@ -227,13 +227,10 @@
     for d in range(nz - 1):
         itotal = itotal + ir_a[d]
 
-    half = total.shape[0]
-    feats = 2 * half
+    feats = total.shape[0]
     blk = fin.shape[2]
-    cols = ne * blk
     for b in range(ne):
-        fin[b, :half, :] = total[:, b * blk:(b + 1) * blk]
-        fin[b, half:feats, :] = total[:, cols + b * blk:cols + (b + 1) * blk]
+        fin[b, :feats, :] = total[:, b * blk:(b + 1) * blk]
         fin[b, feats:feats + 1, :] = itotal[:, b * blk:(b + 1) * blk]
         fin[b, feats + 1:, :] = jnp.zeros((fin.shape[1] - feats - 1, blk), jnp.float32)
     local = pltpu.make_async_copy(fin.at[e], out_ref.at[e], sem_local.at[0])
@@ -257,7 +254,7 @@
 def etp_reduce_scatter(part, inner, ne, blk):
     bf16 = jnp.bfloat16
     nz, nx, nc, feats, cols = part.shape
-    pad_rows = -(-(2 * feats + 1) // 8) * 8
+    pad_rows = -(-(feats + 1) // 8) * 8
     f32 = jnp.float32
     vmem = pltpu.VMEM
     dma = pltpu.SemaphoreType.DMA
@@ -275,11 +272,11 @@
             pltpu.VMEM((nz, feats, cols), f32),
             pltpu.VMEM((nz, feats, cols), bf16),
             pltpu.VMEM((mz, feats, cols), bf16),
-            pltpu.VMEM((mc, 1, cols // 2), f32),
-            pltpu.VMEM((1, cols // 2), f32),
-            pltpu.VMEM((mx, 1, cols // 2), f32),
-            pltpu.VMEM((1, cols // 2), f32),
-            pltpu.VMEM((mz, 1, cols // 2), f32),
+            pltpu.VMEM((mc, 1, cols), f32),
+            pltpu.VMEM((1, cols), f32),
+            pltpu.VMEM((mx, 1, cols), f32),
+            pltpu.VMEM((1, cols), f32),
+            pltpu.VMEM((mz, 1, cols), f32),
             pltpu.VMEM((ne, pad_rows, blk), f32),
             dma((1,)),
             dma((2, mc)),
@@ -342,11 +339,9 @@
     grad_up_w = lax.dot_general(xt, d_up, dims(1, 0), preferred_element_type=f32)
     wd_cot = lax.dot_general(wd, ct, dims(1, 0), preferred_element_type=f32)
     inner = jnp.sum(hidden.astype(f32) * wd_cot.T, axis=1)[None, :]
-    part = out_t.reshape(nz, nx, nc, width // 2, 2 * rows)
+    part = out_t.reshape(nz, nx, nc, width, rows)
     back = etp_reduce_scatter(part, inner, ep_count, CAP)
-    half = width // 2
-    feats_back = back[:, :width].reshape(EXPERTS, 2, half, CAP)
-    feats_back = jnp.transpose(feats_back, (0, 3, 2, 1)).reshape(EXPERTS * CAP, width)
+    feats_back = jnp.transpose(back[:, :width], (0, 2, 1)).reshape(EXPERTS * CAP, width)
     inner_back = back[:, width].reshape(EXPERTS * CAP)
     pair_rows = feats_back[target].reshape(tok_count, 2, width)
     mixed = jnp.sum(route_gates[:, :, None] * pair_rows, axis=1).astype(jnp.bfloat16)

time: 112 us -> 115 us (1.027)
  Pallas kernels: 76.8 us -> 81.2 us
  local copies, waits for them, and re-layouts: 19.6 us -> 15.8 us
  other arithmetic: 6.17 us -> 8.11 us
    pallas_call x1, Pallas kernels: 35.3 us -> 39.7 us  [etp_reduce_scatter(): pl.pallas_call(functools.partial(_rs_kernel, ne, nz, nx, nc), out_shape=j...]
    reshape x4 -> x0, local copies, waits for them, and re-layouts: 3.15 us -> none  [the longest x1 2.88 us: per_device(): part = out_t.reshape(nz, nx, nc, width // 2, 2 * rows)]
    convert_element_type x1, other arithmetic: 1.26 us -> 3.25 us  [etp_reduce_scatter(): part.astype(bf16)]
    unnamed x15 -> x13, local copies, waits for them, and re-layouts: 4.32 us -> 3.61 us
where the time goes in v10:
time: 115 us; the launch traced here: 114 us
  Pallas kernels  81.2 us (71%)
  local copies, waits for them, and re-layouts  15.8 us (14%)
  matrix products  8.12 us (7%)
  other arithmetic  8.11 us (7%)
    pallas_call x1, Pallas kernels, ep_etp_gather(): pl.pallas_call(functools.partial(_gather_kernel, ne, nz, nx, nc), out_sha...  41.4 us
    pallas_call x1, Pallas kernels, etp_reduce_scatter(): pl.pallas_call(functools.partial(_rs_kernel, ne, nz, nx, nc), out_shape=j...  39.7 us
    unnamed x13, local copies, waits for them, and re-layouts  3.61 us
    convert_element_type x1, other arithmetic, etp_reduce_scatter(): part.astype(bf16)  3.25 us
    dot_general x1, local copies, waits for them, and re-layouts, per_device(): out_t = lax.dot_general(wd, hidden, dims(0, 1), preferred_element_type=f32)  2.32 us

profile of v10, /device:TPU:6, one launch (start us, length us, event | category | flops | bytes accessed | tf_op | source)
XLA Modules:
  0.0 114.0 jit_solution(12530177366717405356)
XLA Ops:
  0.6 0.0 copy-start
  0.6 0.8 copy.20
  1.5 0.1 eq.15
  1.6 0.1 fusion.15
  1.7 0.1 reduce_window_sum.11
  1.8 0.2 select_reduce_fusion
  2.0 0.7 broadcast_multiply_fusion
  2.7 0.1 copy.19
  2.8 0.1 mul.71
  2.9 0.9 scatter_custom_fusion
  3.9 0.8 copy.18
  4.6 0.1 reshape.75
  4.7 0.1 pad_maximum_fusion
  4.8 1.6 %gather_fusion.1 = f32[192]{0:T(256)S(1)} fusion(f32[97]{0:T(128)S(1)} %pad_maximum_fusion, s32[1024]{0:T(1024)S(1)} %get-tuple-element.25), kind=kCustom, calls=%fused_computation.1 | custom fusion | bytes 2304 | tf_op jit(solution)/shard_map/gather | solution.py:312
  6.4 0.7 reshape.76.g_ref
  7.1 0.8 fusion.19
  7.9 0.8 gather_fusion
  8.7 0.8 copy.21
  9.5 41.4 %shard_map.110 = (bf16[8,4,2,48,384]{4,3,2,1,0:T(8,128)(2,1)}, f32[1,192]{1,0:T(1,128)}) custom-call(bf16[8,96,24]{2,1,0:T(8,128)(2,1)} %bitcast.59, f32[8,1,24]{2,1,0:T(1,128)} %reshape.76.g_ref), custom_call_target="tpu_custom_call" | custom-call | tf_op jit(solution)/shard_map/pallas_call | solution.py:139
  50.9 2.1 %multiply_convert_fusion.1 = bf16[8,4,2,48,192]{4,3,2,1,0:T(8,128)(2,1)S(1)} fusion(f32[192]{0:T(256)} %bitcast.62, bf16[8,4,2,48,384]{4,3,2,1,0:T(8,128)(2,1)} %get-tuple-element.7), kind=kLoop, calls=%fused_computation.13 | loop fusion | flops 1769472 | bytes 2360064 | tf_op jit(solution)/shard_map/convert_element_type | solution.py:323
  53.0 0.0 copy-start.1
  53.0 0.0 copy-done
  53.0 0.6 fusion.5
  53.6 1.0 copy-done.1
  54.7 0.0 copy-start.2
  54.7 0.8 fusion.25
  55.5 0.3 copy-done.2
  55.8 0.6 fusion.11
  56.4 0.0 copy-start.4
  56.4 1.5 %fusion.1 = bf16[1,3072,128]{2,1,0:T(8,128)(2,1)} fusion(bf16[3072,192]{1,0:T(8,128)(2,1)S(1)} %bitcast.52, f32[192,128]{1,0:T(8,128)S(1)} %fusion.5, f32[192,128]{1,0:T(8,128)S(1)} %fusion.11), kind=kOutput, calls=%fused_computation.10 | convolution fusion | flops 151535616 | bytes 2162688 | tf_op jit(solution)/shard_map/dot_general | solution.py:339
  57.9 0.0 copy-done.4
  57.9 0.6 multiply_convert_fusion.5
  58.5 0.0 copy-start.3
  58.5 1.5 %fusion = bf16[1,3072,128]{2,1,0:T(8,128)(2,1)} fusion(bf16[3072,192]{1,0:T(8,128)(2,1)S(1)} %bitcast.54, f32[192,128]{1,0:T(8,128)S(1)} %fusion.11, f32[192,128]{1,0:T(8,128)S(1)} %fusion.5, f32[192,128]{1,0:T(8,128)S(1)} %get-tuple-element.24), kind=kOutput, calls=%fused_computation.9 | convolution fusion | flops 151633920 | bytes 2260992 | tf_op jit(solution)/shard_map/dot_general | solution.py:338
  60.0 0.0 copy-done.3
  60.0 1.6 %fusion.2 = bf16[1,128,3072]{2,1,0:T(8,128)(2,1)} fusion(bf16[192,128]{1,0:T(8,128)(2,1)S(1)} %get-tuple-element.23, bf16[3072,192]{1,0:T(8,128)(2,1)S(1)} %bitcast.55, f32[192]{0:T(256)S(1)} %bitcast.63), kind=kOutput, calls=%fused_computation.11 | convolution fusion | flops 153157632 | bytes 2016000 | tf_op jit(solution)/shard_map/dot_general | solution.py:337
  61.6 1.4 %fusion.4 = f32[192]{0:T(256)} fusion(bf16[3072,192]{1,0:T(8,128)(2,1)S(1)} %bitcast.56, bf16[1,128,3072]{2,1,0:T(8,128)(2,1)S(1)} %copy-done, bf16[192,128]{1,0:T(8,128)(2,1)S(1)} %get-tuple-element.23), kind=kOutput, calls=%fused_computation.16 | convolution fusion | flops 151068480 | bytes 2016000 | tf_op jit(solution)/shard_map/dot_general | solution.py:340
  62.9 0.5 convolution_bitcast_fusion
  63.4 2.3 %copy.23 = f32[3072,192]{1,0:T(8,128)} copy(f32[3072,192]{0,1:T(8,128)S(1)} %convolution_bitcast_fusion) | data formatting | bytes 4718592 | tf_op jit(solution)/shard_map/dot_general | solution.py:333
  65.7 3.3 %convert_element_type.46.partb_ref = bf16[8,4,2,48,192]{4,3,2,1,0:T(8,128)(2,1)} convert(f32[8,4,2,48,192]{4,3,2,1,0:T(8,128)} %bitcast.49) | non-fusion elementwise | flops 589824 | bytes 3538944 | tf_op jit(solution)/shard_map/convert_element_type | solution.py:292
  68.9 39.7 %shard_map.111 = f32[8,56,24]{2,1,0:T(8,128)} custom-call(f32[8,4,2,48,192]{4,3,2,1,0:T(8,128)} %bitcast.50, bf16[8,4,2,48,192]{4,3,2,1,0:T(8,128)(2,1)} %convert_element_type.46.partb_ref, f32[1,192]{1,0:T(1,128)} %bitcast.64), custom_call_target="tpu_custom_call" | custom-call | tf_op jit(solution)/shard_map/pallas_call | solution.py:262
  108.7 0.9 slice_bitcast_fusion
  109.6 0.1 copy.24
  109.7 0.6 gather_fusion.2
  110.4 0.7 multiply_reduce_fusion
  111.1 0.8 slice_reduce_fusion
  111.9 0.1 reshape_squeeze.3
  112.0 1.3 %gather_fusion.3 = f32[96]{0:T(128)S(1)} fusion(f32[192]{0:T(256)S(1)} %reshape_squeeze.3, s32[1024]{0:T(1024)S(1)} %pad_clamp_fusion), kind=kCustom, calls=%fused_computation.3 | custom fusion | bytes 1152 | tf_op jit(solution)/shard_map/gather | solution.py:348
  113.3 0.1 reshape.82
  113.4 0.6 copy.25
  (5 shorter events, 0.0 us)
Async XLA Ops:
  0.6 52.4 %copy-start = (bf16[1,128,3072]{2,1,0:T(8,128)(2,1)S(1)}, bf16[1,128,3072]{2,1,0:T(8,128)(2,1)}, u32[]{:S(2)}) copy-start(bf16[1,128,3072]{2,1,0:T(8,128)(2,1)} %param.13) | copy-start | bytes 2359300
  53.0 1.7 %copy-start.1 = (bf16[8,4,2,48,384]{4,3,2,1,0:T(8,128)(2,1)S(1)}, bf16[8,4,2,48,384]{4,3,2,1,0:T(8,128)(2,1)}, u32[]{:S(2)}) copy-start(bf16[8,4,2,48,384]{4,3,2,1,0:T(8,128)(2,1)} %get-tuple-element.7) | copy-start | bytes 7077892
  54.7 1.1 copy-start.2
  56.4 1.5 %copy-start.4 = (bf16[1,3072,128]{2,1,0:T(8,128)(2,1)S(1)}, bf16[1,3072,128]{2,1,0:T(8,128)(2,1)}, u32[]{:S(2)}) copy-start(bf16[1,3072,128]{2,1,0:T(8,128)(2,1)} %param.12) | copy-start | bytes 2359300
  58.5 1.5 %copy-start.3 = (f32[1,192]{1,0:T(1,128)S(1)}, f32[1,192]{1,0:T(1,128)}, u32[]{:S(2)}) copy-start(f32[1,192]{1,0:T(1,128)} %get-tuple-element.8) | copy-start | bytes 2308

commit v11 on v9

--- a/solution.py
+++ b/solution.py
@@ -181,28 +181,64 @@
                     dst.at[d], dst.at[d], send_sem.at[t, d], recv_sem.at[t, d],
                     device_id=peers_of[d][1], device_id_type=MESH_ID).wait_recv()
 
-    peers = [((e, z, x, (c + d) % nc), (e, z, x, (c + nc - d) % nc)) for d in range(1, nc)]
-    exchange([(lambda d: partb_ref.at[:, :, (c + d + 1) % nc], recv_c), (lambda d: inner_ref, ir_c)],
-             peers, send_c, rsem_c)
-
-    def sum_c(i, carry):
-        zi = i // nx
-        xi = i % nx
-        total = part_ref[zi, xi, c]
-        for d in range(nc - 1):
-            total = total + recv_c[d, zi, xi].astype(jnp.float32)
-        acc1[zi, xi] = total
-        acc1b[zi, xi] = total.astype(acc1b.dtype)
-        return carry
-    lax.fori_loop(0, nz * nx, sum_c, 0)
+    order = [(x + k) % nx for k in range(1, nx)] + [x]
+    for d in range(1, nc):
+        cpeer = (e, z, x, (c + d) % nc)
+        for k, xx in enumerate(order):
+            cp = pltpu.make_async_remote_copy(
+                partb_ref.at[:, xx, (c + d) % nc], recv_c.at[d - 1, :, xx], send_c.at[d - 1, k], rsem_c.at[d - 1, k],
+                device_id=cpeer, device_id_type=MESH_ID)
+            cp.start()
+            sends.append(cp)
+        cp = pltpu.make_async_remote_copy(
+            inner_ref, ir_c.at[d - 1], send_c.at[d - 1, nx], rsem_c.at[d - 1, nx],
+            device_id=cpeer, device_id_type=MESH_ID)
+        cp.start()
+        sends.append(cp)
+    for k, xx in enumerate(order):
+        for d in range(1, nc):
+            src_peer = (e, z, x, (c + nc - d) % nc)
+            pltpu.make_async_remote_copy(
+                recv_c.at[d - 1, :, xx], recv_c.at[d - 1, :, xx], send_c.at[d - 1, k], rsem_c.at[d - 1, k],
+                device_id=src_peer, device_id_type=MESH_ID).wait_recv()
+
+        def sum_c(zi, carry, xx=xx):
+            total = part_ref[zi, xx, c]
+            for d in range(nc - 1):
+                total = total + recv_c[d, zi, xx].astype(jnp.float32)
+            acc1[zi, xx] = total
+            acc1b[zi, xx] = total.astype(acc1b.dtype)
+            return carry
+        lax.fori_loop(0, nz, sum_c, 0)
+        if k < nx - 1:
+            cp = pltpu.make_async_remote_copy(
+                acc1b.at[:, xx], recv_b.at[k], send_b.at[0, k], rsem_b.at[0, k],
+                device_id=(e, z, xx, c), device_id_type=MESH_ID)
+            cp.start()
+            sends.append(cp)
+    for d in range(1, nc):
+        pltpu.make_async_remote_copy(
+            ir_c.at[d - 1], ir_c.at[d - 1], send_c.at[d - 1, nx], rsem_c.at[d - 1, nx],
+            device_id=(e, z, x, (c + nc - d) % nc), device_id_type=MESH_ID).wait_recv()
     total = inner_ref[...]
     for d in range(nc - 1):
         total = total + ir_c[d]
     in1[...] = total
 
-    peers = [((e, z, (x + d) % nx, c), (e, z, (x + nx - d) % nx, c)) for d in range(1, nx)]
-    exchange([(lambda d: acc1b.at[:, (x + d + 1) % nx], recv_b), (lambda d: in1, ir_b)],
-             peers, send_b, rsem_b)
+    for k in range(nx - 1):
+        cp = pltpu.make_async_remote_copy(
+            in1, ir_b.at[k], send_b.at[1, k], rsem_b.at[1, k],
+            device_id=(e, z, (x + k + 1) % nx, c), device_id_type=MESH_ID)
+        cp.start()
+        sends.append(cp)
+    for k in range(nx - 1):
+        xs = (x + nx - k - 1) % nx
+        pltpu.make_async_remote_copy(
+            recv_b.at[k], recv_b.at[k], send_b.at[0, k], rsem_b.at[0, k],
+            device_id=(e, z, xs, c), device_id_type=MESH_ID).wait_recv()
+        pltpu.make_async_remote_copy(
+            ir_b.at[k], ir_b.at[k], send_b.at[1, k], rsem_b.at[1, k],
+            device_id=(e, z, xs, c), device_id_type=MESH_ID).wait_recv()
 
     def sum_b(zi, carry):
         total = acc1[zi, x]
@@ -282,8 +318,8 @@
             pltpu.VMEM((mz, 1, cols // 2), f32),
             pltpu.VMEM((ne, pad_rows, blk), f32),
             dma((1,)),
-            dma((2, mc)),
-            dma((2, mc)),
+            dma((mc, nx + 1)),
+            dma((mc, nx + 1)),
             dma((2, mx)),
             dma((2, mx)),
             dma((2, mz)),

time: 112 us -> 111 us (level)
  no operation moved by 1% of the time
where the time goes in v11:
time: 111 us
  Pallas kernels  75.8 us (68%)
  local copies, waits for them, and re-layouts  19.6 us (18%)
  matrix products  8.12 us (7%)
  other arithmetic  6.17 us (6%)
    pallas_call x1, Pallas kernels, ep_etp_gather(): pl.pallas_call(functools.partial(_gather_kernel, ne, nz, nx, nc), out_sha...  41.4 us
    pallas_call x1, Pallas kernels, etp_reduce_scatter(): pl.pallas_call(functools.partial(_rs_kernel, ne, nz, nx, nc), out_shape=j...  34.4 us
    unnamed x15, local copies, waits for them, and re-layouts  4.32 us
    reshape x1, local copies, waits for them, and re-layouts, per_device(): part = out_t.reshape(nz, nx, nc, width // 2, 2 * rows)  2.88 us
    dot_general x1, local copies, waits for them, and re-layouts, per_device(): out_t = lax.dot_general(wd, hidden, dims(0, 1), preferred_element_type=f32)  2.32 us

profile of v11, /device:TPU:6, one launch (start us, length us, event | category | flops | bytes accessed | tf_op | source)
XLA Modules:
  0.0 110.5 jit_solution(16669987729025510968)
XLA Ops:
  0.6 0.0 copy-start
  0.7 0.8 broadcast_multiply_fusion
  1.4 0.8 fusion.19
  2.2 0.1 copy.20
  2.3 0.1 mul.71
  2.4 0.8 copy.19
  3.2 0.1 reshape.78
  3.3 0.1 pad_maximum_fusion
  3.4 0.8 copy.21
  4.2 0.1 eq.15
  4.3 0.1 fusion.15
  4.4 0.1 reduce_window_sum.11
  4.5 0.2 select_reduce_fusion
  4.7 0.9 scatter_custom_fusion
  5.6 1.6 %gather_fusion.1 = f32[192]{0:T(256)S(1)} fusion(f32[97]{0:T(128)S(1)} %pad_maximum_fusion, s32[1024]{0:T(1024)S(1)} %get-tuple-element.25), kind=kCustom, calls=%fused_computation.1 | custom fusion | bytes 2304 | tf_op jit(solution)/shard_map/gather | solution.py:351
  7.2 0.7 reshape.79.g_ref
  7.9 0.8 gather_fusion
  8.7 0.8 copy.22
  9.5 41.4 %shard_map.110 = (bf16[8,4,2,48,384]{4,3,2,1,0:T(8,128)(2,1)}, f32[1,192]{1,0:T(1,128)}) custom-call(bf16[8,96,24]{2,1,0:T(8,128)(2,1)} %bitcast.62, f32[8,1,24]{2,1,0:T(1,128)} %reshape.79.g_ref), custom_call_target="tpu_custom_call" | custom-call | tf_op jit(solution)/shard_map/pallas_call | solution.py:139
  50.9 2.1 %multiply_convert_fusion.1 = bf16[8,4,2,48,192]{4,3,2,1,0:T(8,128)(2,1)S(1)} fusion(f32[192]{0:T(256)} %bitcast.66, bf16[8,4,2,48,384]{4,3,2,1,0:T(8,128)(2,1)} %get-tuple-element.7), kind=kLoop, calls=%fused_computation.13 | loop fusion | flops 1769472 | bytes 2360064 | tf_op jit(solution)/shard_map/convert_element_type | solution.py:362
  53.0 0.0 copy-start.2
  53.0 0.0 copy-done
  53.0 0.6 fusion.5
  53.6 1.0 copy-done.2
  54.7 0.0 copy-start.3
  54.7 0.8 fusion.25
  55.5 0.0 copy-start.5
  55.5 0.3 copy-done.3
  55.8 0.6 fusion.11
  56.4 0.3 copy-done.5
  56.7 0.6 multiply_convert_fusion.5
  57.3 0.0 copy-start.4
  57.3 1.4 %fusion.4 = f32[192]{0:T(256)} fusion(bf16[3072,192]{1,0:T(8,128)(2,1)S(1)} %bitcast.58, bf16[1,128,3072]{2,1,0:T(8,128)(2,1)S(1)} %copy-done, bf16[192,128]{1,0:T(8,128)(2,1)S(1)} %get-tuple-element.23), kind=kOutput, calls=%fused_computation.16 | convolution fusion | flops 151068480 | bytes 2016000 | tf_op jit(solution)/shard_map/dot_general | solution.py:379
  58.7 0.0 copy-done.4
  58.7 1.6 %fusion.2 = bf16[1,128,3072]{2,1,0:T(8,128)(2,1)} fusion(bf16[192,128]{1,0:T(8,128)(2,1)S(1)} %get-tuple-element.23, bf16[3072,192]{1,0:T(8,128)(2,1)S(1)} %bitcast.59, f32[192]{0:T(256)S(1)} %bitcast.67), kind=kOutput, calls=%fused_computation.11 | convolution fusion | flops 153157632 | bytes 2016000 | tf_op jit(solution)/shard_map/dot_general | solution.py:376
  60.3 1.5 %fusion = bf16[1,3072,128]{2,1,0:T(8,128)(2,1)} fusion(bf16[3072,192]{1,0:T(8,128)(2,1)S(1)} %bitcast.56, f32[192,128]{1,0:T(8,128)S(1)} %fusion.11, f32[192,128]{1,0:T(8,128)S(1)} %fusion.5, f32[192,128]{1,0:T(8,128)S(1)} %get-tuple-element.24), kind=kOutput, calls=%fused_computation.9 | convolution fusion | flops 151633920 | bytes 2260992 | tf_op jit(solution)/shard_map/dot_general | solution.py:377
  61.7 1.5 %fusion.1 = bf16[1,3072,128]{2,1,0:T(8,128)(2,1)} fusion(bf16[3072,192]{1,0:T(8,128)(2,1)S(1)} %bitcast.57, f32[192,128]{1,0:T(8,128)S(1)} %fusion.5, f32[192,128]{1,0:T(8,128)S(1)} %fusion.11), kind=kOutput, calls=%fused_computation.10 | convolution fusion | flops 151535616 | bytes 2162688 | tf_op jit(solution)/shard_map/dot_general | solution.py:378
  63.2 0.5 convolution_bitcast_fusion
  63.7 2.3 %copy.24 = f32[3072,192]{1,0:T(8,128)} copy(f32[3072,192]{0,1:T(8,128)S(1)} %convolution_bitcast_fusion) | data formatting | bytes 4718592 | tf_op jit(solution)/shard_map/dot_general | solution.py:372
  66.0 2.9 %reshape.81.part_ref = f32[8,4,2,24,384]{4,3,2,1,0:T(8,128)S(1)} reshape(f32[3072,192]{1,0:T(8,128)} %copy.24) | data formatting | bytes 4718592 | tf_op jit(solution)/shard_map/reshape | solution.py:381
  68.9 0.0 copy-start.1
  68.9 1.3 %convert_element_type.46.partb_ref = bf16[8,4,2,24,384]{4,3,2,1,0:T(8,128)(2,1)} convert(f32[8,4,2,24,384]{4,3,2,1,0:T(8,128)S(1)} %reshape.81.part_ref) | non-fusion elementwise | flops 589824 | bytes 3538944 | tf_op jit(solution)/shard_map/convert_element_type | solution.py:331
  70.1 0.5 copy-done.1
  70.6 34.4 %shard_map.111 = f32[8,56,24]{2,1,0:T(8,128)} custom-call(f32[8,4,2,24,384]{4,3,2,1,0:T(8,128)} %copy-done.1, bf16[8,4,2,24,384]{4,3,2,1,0:T(8,128)(2,1)} %convert_element_type.46.partb_ref, f32[1,192]{1,0:T(1,128)} %bitcast.68), custom_call_target="tpu_custom_call" | custom-call | tf_op jit(solution)/shard_map/pallas_call | solution.py:301
  105.0 0.8 slice_reduce_fusion
  105.8 0.9 slice.14
  106.7 0.1 reshape_squeeze.3
  106.8 1.3 %gather_fusion.3 = f32[96]{0:T(128)S(1)} fusion(f32[192]{0:T(256)S(1)} %reshape_squeeze.3, s32[1024]{0:T(1024)S(1)} %pad_clamp_fusion), kind=kCustom, calls=%fused_computation.3 | custom fusion | bytes 1152 | tf_op jit(solution)/shard_map/gather | solution.py:389
  108.1 0.1 copy.29
  108.2 0.1 reshape.84
  108.3 0.1 reshape.86
  108.4 0.6 copy.27
  109.1 0.1 copy.26
  109.2 0.6 gather_fusion.2
  109.8 0.7 multiply_reduce_fusion
  (5 shorter events, 0.0 us)
Async XLA Ops:
  0.6 52.4 %copy-start = (bf16[1,128,3072]{2,1,0:T(8,128)(2,1)S(1)}, bf16[1,128,3072]{2,1,0:T(8,128)(2,1)}, u32[]{:S(2)}) copy-start(bf16[1,128,3072]{2,1,0:T(8,128)(2,1)} %param.13) | copy-start | bytes 2359300
  53.0 1.7 %copy-start.2 = (bf16[8,4,2,48,384]{4,3,2,1,0:T(8,128)(2,1)S(1)}, bf16[8,4,2,48,384]{4,3,2,1,0:T(8,128)(2,1)}, u32[]{:S(2)}) copy-start(bf16[8,4,2,48,384]{4,3,2,1,0:T(8,128)(2,1)} %get-tuple-element.7) | copy-start | bytes 7077892
  54.7 1.1 %copy-start.3 = (bf16[1,3072,128]{2,1,0:T(8,128)(2,1)S(1)}, bf16[1,3072,128]{2,1,0:T(8,128)(2,1)}, u32[]{:S(2)}) copy-start(bf16[1,3072,128]{2,1,0:T(8,128)(2,1)} %param.11) | copy-start | bytes 2359300
  55.5 1.2 %copy-start.5 = (bf16[1,3072,128]{2,1,0:T(8,128)(2,1)S(1)}, bf16[1,3072,128]{2,1,0:T(8,128)(2,1)}, u32[]{:S(2)}) copy-start(bf16[1,3072,128]{2,1,0:T(8,128)(2,1)} %param.12) | copy-start | bytes 2359300
  57.3 1.4 %copy-start.4 = (f32[1,192]{1,0:T(1,128)S(1)}, f32[1,192]{1,0:T(1,128)}, u32[]{:S(2)}) copy-start(f32[1,192]{1,0:T(1,128)} %get-tuple-element.8) | copy-start | bytes 2308
  68.9 1.8 %copy-start.1 = (f32[8,4,2,24,384]{4,3,2,1,0:T(8,128)}, f32[8,4,2,24,384]{4,3,2,1,0:T(8,128)S(1)}, u32[]{:S(2)}) copy-start(f32[8,4,2,24,384]{4,3,2,1,0:T(8,128)S(1)} %reshape.81.part_ref) | copy-start | bytes 7077892

commit v12 on v11

--- a/solution.py
+++ b/solution.py
@@ -374,8 +374,10 @@
     d_up = (d_hidden * jax.nn.silu(gate_pre)).astype(jnp.bfloat16)
     d_gate = (d_hidden * up_pre * sigma * (1.0 + gate_pre * (1.0 - sigma))).astype(jnp.bfloat16)
     grad_down = lax.dot_general(hidden, dyt, dims(0, 1), preferred_element_type=f32)
-    grad_gate_w = lax.dot_general(xt, d_gate, dims(1, 0), preferred_element_type=f32)
-    grad_up_w = lax.dot_general(xt, d_up, dims(1, 0), preferred_element_type=f32)
+    hid = d_gate.shape[1]
+    grad_gu = lax.dot_general(xt, jnp.concatenate([d_gate, d_up], axis=1), dims(1, 0), preferred_element_type=f32)
+    grad_gate_w = grad_gu[:, :hid]
+    grad_up_w = grad_gu[:, hid:]
     wd_cot = lax.dot_general(wd, ct, dims(1, 0), preferred_element_type=f32)
     inner = jnp.sum(hidden.astype(f32) * wd_cot.T, axis=1)[None, :]
     part = out_t.reshape(nz, nx, nc, width // 2, 2 * rows)

time: 111 us -> 110 us (level)
  matrix products: 8.12 us -> 5.77 us
  local copies, waits for them, and re-layouts: 19.6 us -> 20.8 us
    dot_general x2 -> x1, matrix products: 2.93 us -> 0.56 us  [per_device(): lax.dot_general(xt, jnp.concatenate([d_gate, d_up], axis=1), dims(1, 0),...]
    broadcast_in_dim x0 -> x1, local copies, waits for them, and re-layouts: none -> 1.24 us  [per_device(): grad_up_w.astype(jnp.bfloat16)[None]]
where the time goes in v12:
time: 110 us
  Pallas kernels  75.9 us (69%)
  local copies, waits for them, and re-layouts  20.8 us (19%)
  other arithmetic  6.17 us (6%)
  matrix products  5.77 us (5%)
    pallas_call x1, Pallas kernels, ep_etp_gather(): pl.pallas_call(functools.partial(_gather_kernel, ne, nz, nx, nc), out_sha...  41.4 us
    pallas_call x1, Pallas kernels, etp_reduce_scatter(): pl.pallas_call(functools.partial(_rs_kernel, ne, nz, nx, nc), out_shape=j...  34.5 us
    unnamed x15, local copies, waits for them, and re-layouts  4.32 us
    reshape x1, local copies, waits for them, and re-layouts, per_device(): part = out_t.reshape(nz, nx, nc, width // 2, 2 * rows)  2.88 us
    dot_general x1, local copies, waits for them, and re-layouts, per_device(): out_t = lax.dot_general(wd, hidden, dims(0, 1), preferred_element_type=f32)  2.32 us

profile of v12, /device:TPU:6, one launch (start us, length us, event | category | flops | bytes accessed | tf_op | source)
XLA Modules:
  0.0 109.6 jit_solution(12841079363615144296)
XLA Ops:
  0.6 0.0 copy-start
  0.7 0.8 broadcast_multiply_fusion
  1.4 0.8 fusion.18
  2.2 0.1 copy.20
  2.3 0.1 mul.71
  2.4 0.8 copy.19
  3.2 0.1 reshape.78
  3.3 0.1 pad_maximum_fusion
  3.4 0.8 copy.21
  4.2 0.1 eq.15
  4.3 0.1 fusion.15
  4.4 0.1 reduce_window_sum.11
  4.5 0.2 select_reduce_fusion
  4.7 0.9 scatter_custom_fusion
  5.6 1.6 %gather_fusion.1 = f32[192]{0:T(256)S(1)} fusion(f32[97]{0:T(128)S(1)} %pad_maximum_fusion, s32[1024]{0:T(1024)S(1)} %get-tuple-element.28), kind=kCustom, calls=%fused_computation.1 | custom fusion | bytes 2304 | tf_op jit(solution)/shard_map/gather | solution.py:351
  7.2 0.7 reshape.79.g_ref
  7.9 0.8 gather_fusion
  8.7 0.8 copy.22
  9.5 41.4 %shard_map.110 = (bf16[8,4,2,48,384]{4,3,2,1,0:T(8,128)(2,1)}, f32[1,192]{1,0:T(1,128)}) custom-call(bf16[8,96,24]{2,1,0:T(8,128)(2,1)} %bitcast.60, f32[8,1,24]{2,1,0:T(1,128)} %reshape.79.g_ref), custom_call_target="tpu_custom_call" | custom-call | tf_op jit(solution)/shard_map/pallas_call | solution.py:139
  50.9 2.1 %multiply_convert_fusion.1 = bf16[8,4,2,48,192]{4,3,2,1,0:T(8,128)(2,1)S(1)} fusion(f32[192]{0:T(256)} %bitcast.64, bf16[8,4,2,48,384]{4,3,2,1,0:T(8,128)(2,1)} %get-tuple-element.7), kind=kLoop, calls=%fused_computation.10 | loop fusion | flops 1769472 | bytes 2360064 | tf_op jit(solution)/shard_map/convert_element_type | solution.py:362
  53.0 0.0 copy-start.2
  53.0 0.0 copy-done
  53.0 0.6 fusion.3
  53.6 1.0 copy-done.2
  54.7 0.0 copy-start.3
  54.7 0.8 fusion.23
  55.5 0.0 copy-start.5
  55.5 0.3 copy-done.3
  55.8 0.6 fusion.7
  56.4 0.3 copy-done.5
  56.7 0.6 multiply_convert_fusion.4
  57.4 0.6 convolution_convert_fusion
  57.9 1.2 %slice_bitcast_fusion = (bf16[1,3072,128]{2,1,0:T(8,128)(2,1)}, bf16[1,3072,128]{2,1,0:T(8,128)(2,1)}) fusion(bf16[3072,256]{1,0:T(8,128)(2,1)S(1)} %convolution_convert_fusion), kind=kLoop, calls=%fused_computation.14 | loop fusion | bytes 3145728 | tf_op jit(solution)/shard_map/broadcast_in_dim | solution.py:396
  59.2 0.0 copy-start.4
  59.2 1.4 %fusion.2 = f32[192]{0:T(256)} fusion(bf16[3072,192]{1,0:T(8,128)(2,1)S(1)} %bitcast.53, bf16[1,128,3072]{2,1,0:T(8,128)(2,1)S(1)} %copy-done, bf16[192,128]{1,0:T(8,128)(2,1)S(1)} %get-tuple-element.25), kind=kOutput, calls=%fused_computation.13 | convolution fusion | flops 151068480 | bytes 2016000 | tf_op jit(solution)/shard_map/dot_general | solution.py:381
  60.5 0.0 copy-done.4
  60.5 1.6 %fusion = bf16[1,128,3072]{2,1,0:T(8,128)(2,1)} fusion(bf16[192,128]{1,0:T(8,128)(2,1)S(1)} %get-tuple-element.25, bf16[3072,192]{1,0:T(8,128)(2,1)S(1)} %bitcast.54, f32[192]{0:T(256)S(1)} %bitcast.65), kind=kOutput, calls=%fused_computation.8 | convolution fusion | flops 153157632 | bytes 2016000 | tf_op jit(solution)/shard_map/dot_general | solution.py:376
  62.1 0.5 convolution_bitcast_fusion
  62.6 2.3 %copy.24 = f32[3072,192]{1,0:T(8,128)} copy(f32[3072,192]{0,1:T(8,128)S(1)} %convolution_bitcast_fusion) | data formatting | bytes 4718592 | tf_op jit(solution)/shard_map/dot_general | solution.py:372
  64.9 2.9 %reshape.81.part_ref = f32[8,4,2,24,384]{4,3,2,1,0:T(8,128)S(1)} reshape(f32[3072,192]{1,0:T(8,128)} %copy.24) | data formatting | bytes 4718592 | tf_op jit(solution)/shard_map/reshape | solution.py:383
  67.8 0.0 copy-start.1
  67.8 1.3 %convert_element_type.42.partb_ref = bf16[8,4,2,24,384]{4,3,2,1,0:T(8,128)(2,1)} convert(f32[8,4,2,24,384]{4,3,2,1,0:T(8,128)S(1)} %reshape.81.part_ref) | non-fusion elementwise | flops 589824 | bytes 3538944 | tf_op jit(solution)/shard_map/convert_element_type | solution.py:331
  69.0 0.5 copy-done.1
  69.5 34.5 %shard_map.111 = f32[8,56,24]{2,1,0:T(8,128)} custom-call(f32[8,4,2,24,384]{4,3,2,1,0:T(8,128)} %copy-done.1, bf16[8,4,2,24,384]{4,3,2,1,0:T(8,128)(2,1)} %convert_element_type.42.partb_ref, f32[1,192]{1,0:T(1,128)} %bitcast.66), custom_call_target="tpu_custom_call" | custom-call | tf_op jit(solution)/shard_map/pallas_call | solution.py:301
  104.1 0.8 slice_reduce_fusion
  104.8 0.9 slice.22
  105.8 0.1 reshape_squeeze.3
  105.9 1.3 %gather_fusion.3 = f32[96]{0:T(128)S(1)} fusion(f32[192]{0:T(256)S(1)} %reshape_squeeze.3, s32[1024]{0:T(1024)S(1)} %pad_clamp_fusion), kind=kCustom, calls=%fused_computation.3 | custom fusion | bytes 1152 | tf_op jit(solution)/shard_map/gather | solution.py:391
  107.1 0.1 copy.29
  107.2 0.1 reshape.84
  107.3 0.1 reshape.86
  107.5 0.6 copy.27
  108.1 0.1 copy.26
  108.2 0.6 gather_fusion.2
  108.8 0.7 multiply_reduce_fusion
  (5 shorter events, 0.0 us)
Async XLA Ops:
  0.6 52.4 %copy-start = (bf16[1,128,3072]{2,1,0:T(8,128)(2,1)S(1)}, bf16[1,128,3072]{2,1,0:T(8,128)(2,1)}, u32[]{:S(2)}) copy-start(bf16[1,128,3072]{2,1,0:T(8,128)(2,1)} %param.13) | copy-start | bytes 2359300
  53.0 1.7 %copy-start.2 = (bf16[8,4,2,48,384]{4,3,2,1,0:T(8,128)(2,1)S(1)}, bf16[8,4,2,48,384]{4,3,2,1,0:T(8,128)(2,1)}, u32[]{:S(2)}) copy-start(bf16[8,4,2,48,384]{4,3,2,1,0:T(8,128)(2,1)} %get-tuple-element.7) | copy-start | bytes 7077892
  54.7 1.1 %copy-start.3 = (bf16[1,3072,128]{2,1,0:T(8,128)(2,1)S(1)}, bf16[1,3072,128]{2,1,0:T(8,128)(2,1)}, u32[]{:S(2)}) copy-start(bf16[1,3072,128]{2,1,0:T(8,128)(2,1)} %param.12) | copy-start | bytes 2359300
  55.5 1.2 %copy-start.5 = (bf16[1,3072,128]{2,1,0:T(8,128)(2,1)S(1)}, bf16[1,3072,128]{2,1,0:T(8,128)(2,1)}, u32[]{:S(2)}) copy-start(bf16[1,3072,128]{2,1,0:T(8,128)(2,1)} %param.11) | copy-start | bytes 2359300
  59.2 1.4 %copy-start.4 = (f32[1,192]{1,0:T(1,128)S(1)}, f32[1,192]{1,0:T(1,128)}, u32[]{:S(2)}) copy-start(f32[1,192]{1,0:T(1,128)} %get-tuple-element.8) | copy-start | bytes 2308
  67.8 1.8 %copy-start.1 = (f32[8,4,2,24,384]{4,3,2,1,0:T(8,128)}, f32[8,4,2,24,384]{4,3,2,1,0:T(8,128)S(1)}, u32[]{:S(2)}) copy-start(f32[8,4,2,24,384]{4,3,2,1,0:T(8,128)S(1)} %reshape.81.part_ref) | copy-start | bytes 7077892

commit v13 on v12

--- a/solution.py
+++ b/solution.py
@@ -365,8 +365,9 @@
 
     def dims(a, b):
         return (((a,), (b,)), ((), ()))
-    gate_pre = lax.dot_general(xt, wg, dims(0, 0), preferred_element_type=f32)
-    up_pre = lax.dot_general(xt, wu, dims(0, 0), preferred_element_type=f32)
+    gu_pre = lax.dot_general(xt, jnp.concatenate([wg, wu], axis=1), dims(0, 0), preferred_element_type=f32)
+    gate_pre = gu_pre[:, :wg.shape[1]]
+    up_pre = gu_pre[:, wg.shape[1]:]
     sigma = jax.nn.sigmoid(gate_pre)
     hidden = (jax.nn.silu(gate_pre) * up_pre).astype(jnp.bfloat16)
     out_t = lax.dot_general(wd, hidden, dims(0, 1), preferred_element_type=f32)

time: 110 us -> 108 us (0.982)
  local copies, waits for them, and re-layouts: 20.8 us -> 19.7 us
    unnamed x15, local copies, waits for them, and re-layouts: 4.32 us -> 3.22 us
where the time goes in v13:
time: 108 us
  Pallas kernels  75.8 us (70%)
  local copies, waits for them, and re-layouts  19.7 us (18%)
  other arithmetic  6.32 us (6%)
  matrix products  5.22 us (5%)
    pallas_call x1, Pallas kernels, ep_etp_gather(): pl.pallas_call(functools.partial(_gather_kernel, ne, nz, nx, nc), out_sha...  41.4 us
    pallas_call x1, Pallas kernels, etp_reduce_scatter(): pl.pallas_call(functools.partial(_rs_kernel, ne, nz, nx, nc), out_shape=j...  34.4 us
    unnamed x15, local copies, waits for them, and re-layouts  3.22 us
    reshape x1, local copies, waits for them, and re-layouts, per_device(): part = out_t.reshape(nz, nx, nc, width // 2, 2 * rows)  2.88 us
    dot_general x1, local copies, waits for them, and re-layouts, per_device(): out_t = lax.dot_general(wd, hidden, dims(0, 1), preferred_element_type=f32)  2.32 us
    convert_element_type x1, other arithmetic, per_device(): dyt = (slot_g * ct.astype(jnp.float32)).astype(jnp.bfloat16)  2.26 us

profile of v13, /device:TPU:6, one launch (start us, length us, event | category | flops | bytes accessed | tf_op | source)
XLA Modules:
  0.0 108.0 jit_solution(1209188343688373756)
XLA Ops:
  0.6 0.0 copy-start
  0.7 0.8 broadcast_multiply_fusion
  1.4 0.8 fusion.18
  2.2 0.1 copy.20
  2.3 0.1 mul.71
  2.4 0.8 copy.19
  3.2 0.1 reshape.78
  3.3 0.1 pad_maximum_fusion
  3.4 0.8 copy.21
  4.2 0.1 eq.15
  4.3 0.1 fusion.15
  4.4 0.1 reduce_window_sum.11
  4.5 0.2 select_reduce_fusion
  4.7 0.9 scatter_custom_fusion
  5.6 1.6 %gather_fusion.1 = f32[192]{0:T(256)S(1)} fusion(f32[97]{0:T(128)S(1)} %pad_maximum_fusion, s32[1024]{0:T(1024)S(1)} %get-tuple-element.28), kind=kCustom, calls=%fused_computation.1 | custom fusion | bytes 2304 | tf_op jit(solution)/shard_map/gather | solution.py:351
  7.2 0.7 reshape.79.g_ref
  7.9 0.8 gather_fusion
  8.7 0.8 copy.22
  9.5 41.4 %shard_map.110 = (bf16[8,4,2,48,384]{4,3,2,1,0:T(8,128)(2,1)}, f32[1,192]{1,0:T(1,128)}) custom-call(bf16[8,96,24]{2,1,0:T(8,128)(2,1)} %bitcast.54, f32[8,1,24]{2,1,0:T(1,128)} %reshape.79.g_ref), custom_call_target="tpu_custom_call" | custom-call | tf_op jit(solution)/shard_map/pallas_call | solution.py:139
  50.9 0.0 copy-start.2
  50.9 2.3 %multiply_convert_fusion.1 = bf16[8,4,2,48,192]{4,3,2,1,0:T(8,128)(2,1)S(1)} fusion(f32[192]{0:T(256)} %bitcast.58, bf16[8,4,2,48,384]{4,3,2,1,0:T(8,128)(2,1)} %get-tuple-element.7), kind=kLoop, calls=%fused_computation.10 | loop fusion | flops 1769472 | bytes 2360064 | tf_op jit(solution)/shard_map/convert_element_type | solution.py:362
  53.2 0.0 copy-done.2
  53.2 0.0 copy-start.4
  53.2 0.0 copy-start.5
  53.2 0.8 fusion.24
  54.0 0.3 copy-done.4
  54.3 0.2 copy-done.5
  54.6 0.6 fusion.1
  55.2 0.0 copy-done
  55.2 0.7 multiply_convert_fusion.4
  55.9 0.6 convolution_convert_fusion
  56.4 1.2 %slice_bitcast_fusion = (bf16[1,3072,128]{2,1,0:T(8,128)(2,1)}, bf16[1,3072,128]{2,1,0:T(8,128)(2,1)}) fusion(bf16[3072,256]{1,0:T(8,128)(2,1)S(1)} %convolution_convert_fusion), kind=kLoop, calls=%fused_computation.18 | loop fusion | bytes 3145728 | tf_op jit(solution)/shard_map/broadcast_in_dim | solution.py:397
  57.7 0.0 copy-start.3
  57.7 1.4 %fusion.6 = f32[192]{0:T(256)} fusion(bf16[3072,192]{1,0:T(8,128)(2,1)S(1)} %bitcast.48, bf16[1,128,3072]{2,1,0:T(8,128)(2,1)S(1)} %copy-done, bf16[192,128]{1,0:T(8,128)(2,1)S(1)} %get-tuple-element.25), kind=kOutput, calls=%fused_computation.17 | convolution fusion | flops 151068480 | bytes 2016000 | tf_op jit(solution)/shard_map/dot_general | solution.py:382
  59.0 0.0 copy-done.3
  59.0 1.6 %fusion = bf16[1,128,3072]{2,1,0:T(8,128)(2,1)} fusion(bf16[192,128]{1,0:T(8,128)(2,1)S(1)} %get-tuple-element.25, bf16[3072,192]{1,0:T(8,128)(2,1)S(1)} %bitcast.49, f32[192]{0:T(256)S(1)} %bitcast.59), kind=kOutput, calls=%fused_computation.8 | convolution fusion | flops 153157632 | bytes 2016000 | tf_op jit(solution)/shard_map/dot_general | solution.py:377
  60.6 0.5 convolution_bitcast_fusion
  61.1 2.3 %copy.24 = f32[3072,192]{1,0:T(8,128)} copy(f32[3072,192]{0,1:T(8,128)S(1)} %convolution_bitcast_fusion) | data formatting | bytes 4718592 | tf_op jit(solution)/shard_map/dot_general | solution.py:373
  63.4 2.9 %reshape.81.part_ref = f32[8,4,2,24,384]{4,3,2,1,0:T(8,128)S(1)} reshape(f32[3072,192]{1,0:T(8,128)} %copy.24) | data formatting | bytes 4718592 | tf_op jit(solution)/shard_map/reshape | solution.py:384
  66.3 0.0 copy-start.1
  66.3 1.3 %convert_element_type.42.partb_ref = bf16[8,4,2,24,384]{4,3,2,1,0:T(8,128)(2,1)} convert(f32[8,4,2,24,384]{4,3,2,1,0:T(8,128)S(1)} %reshape.81.part_ref) | non-fusion elementwise | flops 589824 | bytes 3538944 | tf_op jit(solution)/shard_map/convert_element_type | solution.py:331
  67.5 0.5 copy-done.1
  68.0 34.4 %shard_map.111 = f32[8,56,24]{2,1,0:T(8,128)} custom-call(f32[8,4,2,24,384]{4,3,2,1,0:T(8,128)} %copy-done.1, bf16[8,4,2,24,384]{4,3,2,1,0:T(8,128)(2,1)} %convert_element_type.42.partb_ref, f32[1,192]{1,0:T(1,128)} %bitcast.60), custom_call_target="tpu_custom_call" | custom-call | tf_op jit(solution)/shard_map/pallas_call | solution.py:301
  102.5 0.8 slice_reduce_fusion
  103.2 0.9 slice.30
  104.2 0.1 reshape_squeeze.3
  104.3 1.3 %gather_fusion.3 = f32[96]{0:T(128)S(1)} fusion(f32[192]{0:T(256)S(1)} %reshape_squeeze.3, s32[1024]{0:T(1024)S(1)} %pad_clamp_fusion), kind=kCustom, calls=%fused_computation.3 | custom fusion | bytes 1152 | tf_op jit(solution)/shard_map/gather | solution.py:392
  105.5 0.1 copy.29
  105.6 0.1 reshape.84
  105.7 0.1 reshape.86
  105.9 0.6 copy.27
  106.5 0.1 copy.26
  106.6 0.6 gather_fusion.2
  107.2 0.7 multiply_reduce_fusion
  (5 shorter events, 0.0 us)
Async XLA Ops:
  0.6 54.5 %copy-start = (bf16[1,128,3072]{2,1,0:T(8,128)(2,1)S(1)}, bf16[1,128,3072]{2,1,0:T(8,128)(2,1)}, u32[]{:S(2)}) copy-start(bf16[1,128,3072]{2,1,0:T(8,128)(2,1)} %param.13) | copy-start | bytes 2359300
  50.9 2.3 %copy-start.2 = (bf16[8,4,2,48,384]{4,3,2,1,0:T(8,128)(2,1)S(1)}, bf16[8,4,2,48,384]{4,3,2,1,0:T(8,128)(2,1)}, u32[]{:S(2)}) copy-start(bf16[8,4,2,48,384]{4,3,2,1,0:T(8,128)(2,1)} %get-tuple-element.7) | copy-start | bytes 7077892
  53.2 1.1 %copy-start.4 = (bf16[1,3072,128]{2,1,0:T(8,128)(2,1)S(1)}, bf16[1,3072,128]{2,1,0:T(8,128)(2,1)}, u32[]{:S(2)}) copy-start(bf16[1,3072,128]{2,1,0:T(8,128)(2,1)} %param.12) | copy-start | bytes 2359300
  53.2 1.4 %copy-start.5 = (bf16[1,3072,128]{2,1,0:T(8,128)(2,1)S(1)}, bf16[1,3072,128]{2,1,0:T(8,128)(2,1)}, u32[]{:S(2)}) copy-start(bf16[1,3072,128]{2,1,0:T(8,128)(2,1)} %param.11) | copy-start | bytes 2359300
  57.7 1.4 %copy-start.3 = (f32[1,192]{1,0:T(1,128)S(1)}, f32[1,192]{1,0:T(1,128)}, u32[]{:S(2)}) copy-start(f32[1,192]{1,0:T(1,128)} %get-tuple-element.8) | copy-start | bytes 2308
  66.3 1.8 %copy-start.1 = (f32[8,4,2,24,384]{4,3,2,1,0:T(8,128)}, f32[8,4,2,24,384]{4,3,2,1,0:T(8,128)S(1)}, u32[]{:S(2)}) copy-start(f32[8,4,2,24,384]{4,3,2,1,0:T(8,128)S(1)} %reshape.81.part_ref) | copy-start | bytes 7077892

commit v14 on v13

--- a/solution.py
+++ b/solution.py
@@ -371,7 +371,8 @@
     sigma = jax.nn.sigmoid(gate_pre)
     hidden = (jax.nn.silu(gate_pre) * up_pre).astype(jnp.bfloat16)
     out_t = lax.dot_general(wd, hidden, dims(0, 1), preferred_element_type=f32)
-    d_hidden = lax.dot_general(dyt, wd, dims(0, 1), preferred_element_type=f32)
+    dh_wc = lax.dot_general(jnp.concatenate([dyt, ct], axis=1), wd, dims(0, 1), preferred_element_type=f32)
+    d_hidden = dh_wc[:rows]
     d_up = (d_hidden * jax.nn.silu(gate_pre)).astype(jnp.bfloat16)
     d_gate = (d_hidden * up_pre * sigma * (1.0 + gate_pre * (1.0 - sigma))).astype(jnp.bfloat16)
     grad_down = lax.dot_general(hidden, dyt, dims(0, 1), preferred_element_type=f32)
@@ -379,8 +380,7 @@
     grad_gu = lax.dot_general(xt, jnp.concatenate([d_gate, d_up], axis=1), dims(1, 0), preferred_element_type=f32)
     grad_gate_w = grad_gu[:, :hid]
     grad_up_w = grad_gu[:, hid:]
-    wd_cot = lax.dot_general(wd, ct, dims(1, 0), preferred_element_type=f32)
-    inner = jnp.sum(hidden.astype(f32) * wd_cot.T, axis=1)[None, :]
+    inner = jnp.sum(hidden.astype(f32) * dh_wc[rows:], axis=1)[None, :]
     part = out_t.reshape(nz, nx, nc, width // 2, 2 * rows)
     back = etp_reduce_scatter(part, inner, ep_count, CAP)
     half = width // 2

time: 108 us -> 108 us (level)
  local copies, waits for them, and re-layouts: 19.7 us -> 21.2 us
  other arithmetic: 6.32 us -> 5.2 us
    slice x1, local copies, waits for them, and re-layouts: 0.83 us -> 2.82 us  [per_device(): xt = xc_all[..., :rows].reshape(feat, rows)]
    convert_element_type x1, other arithmetic: 2.26 us -> 0.41 us  [per_device(): dyt = (slot_g * ct.astype(jnp.float32)).astype(jnp.bfloat16)]
    unnamed x15 -> x13, local copies, waits for them, and re-layouts: 3.22 us -> 2.71 us
where the time goes in v14:
time: 108 us
  Pallas kernels  75.8 us (70%)
  local copies, waits for them, and re-layouts  21.2 us (20%)
  other arithmetic  5.2 us (5%)
  matrix products  4.59 us (4%)
    pallas_call x1, Pallas kernels, ep_etp_gather(): pl.pallas_call(functools.partial(_gather_kernel, ne, nz, nx, nc), out_sha...  41.4 us
    pallas_call x1, Pallas kernels, etp_reduce_scatter(): pl.pallas_call(functools.partial(_rs_kernel, ne, nz, nx, nc), out_shape=j...  34.4 us
    reshape x1, local copies, waits for them, and re-layouts, per_device(): part = out_t.reshape(nz, nx, nc, width // 2, 2 * rows)  2.88 us
    slice x1, local copies, waits for them, and re-layouts, per_device(): xt = xc_all[..., :rows].reshape(feat, rows)  2.82 us
    unnamed x13, local copies, waits for them, and re-layouts  2.71 us
    dot_general x1, local copies, waits for them, and re-layouts, per_device(): out_t = lax.dot_general(wd, hidden, dims(0, 1), preferred_element_type=f32)  2.32 us

profile of v14, /device:TPU:6, one launch (start us, length us, event | category | flops | bytes accessed | tf_op | source)
XLA Modules:
  0.0 107.7 jit_solution(4765772187739207073)
XLA Ops:
  0.6 0.0 copy-start
  0.7 0.8 broadcast_multiply_fusion
  1.4 0.8 fusion.19
  2.2 0.1 copy.20
  2.3 0.1 mul.66
  2.4 0.8 copy.19
  3.2 0.1 reshape.72
  3.3 0.1 pad_maximum_fusion
  3.4 0.8 copy.21
  4.2 0.1 eq.15
  4.3 0.1 fusion.16
  4.4 0.1 reduce_window_sum.11
  4.5 0.2 select_reduce_fusion
  4.7 0.9 scatter_custom_fusion
  5.6 1.6 %gather_fusion.1 = f32[192]{0:T(256)S(1)} fusion(f32[97]{0:T(128)S(1)} %pad_maximum_fusion, s32[1024]{0:T(1024)S(1)} %get-tuple-element.31), kind=kCustom, calls=%fused_computation.1 | custom fusion | bytes 2304 | tf_op jit(solution)/shard_map/gather | solution.py:351
  7.2 0.7 reshape.73.g_ref
  7.9 0.8 gather_fusion
  8.7 0.8 copy.22
  9.5 41.4 %shard_map.110 = (bf16[8,4,2,48,384]{4,3,2,1,0:T(8,128)(2,1)}, f32[1,192]{1,0:T(1,128)}) custom-call(bf16[8,96,24]{2,1,0:T(8,128)(2,1)} %bitcast.47, f32[8,1,24]{2,1,0:T(1,128)} %reshape.73.g_ref), custom_call_target="tpu_custom_call" | custom-call | tf_op jit(solution)/shard_map/pallas_call | solution.py:139
  50.9 0.0 copy-start.3
  50.9 0.0 copy-start.4
  50.9 2.8 %fusion.26 = (bf16[8,4,2,48,192]{4,3,2,1,0:T(8,128)(2,1)S(1)}, bf16[8,4,2,48,192]{4,3,2,1,0:T(8,128)(2,1)S(1)}) fusion(bf16[8,4,2,48,384]{4,3,2,1,0:T(8,128)(2,1)} %get-tuple-element.7), kind=kLoop, calls=%fused_computation.61 | loop fusion | bytes 4718592 | tf_op jit(solution)/shard_map/slice | solution.py:359
  53.7 0.0 copy-done.3
  53.8 0.0 copy-done.4
  53.8 0.0 copy-start.2
  53.8 0.6 fusion.5
  54.4 0.0 copy-done.2
  54.4 0.4 multiply_convert_fusion
  54.8 0.0 copy-done
  54.8 1.4 %fusion.1 = f32[384,128]{1,0:T(8,128)S(1)} fusion(bf16[3072,192]{1,0:T(8,128)(2,1)S(1)} %bitcast.45, bf16[3072,192]{1,0:T(8,128)(2,1)S(1)} %multiply_convert_fusion, bf16[1,128,3072]{2,1,0:T(8,128)(2,1)S(1)} %copy-done), kind=kOutput, calls=%fused_computation.10 | convolution fusion | flops 306708480 | bytes 3342336 | tf_op jit(solution)/shard_map/dot_general | solution.py:374
  56.3 0.7 multiply_convert_fusion.2
  57.0 1.5 %fusion = bf16[1,128,3072]{2,1,0:T(8,128)(2,1)} fusion(bf16[192,128]{1,0:T(8,128)(2,1)S(1)} %get-tuple-element.28, bf16[3072,192]{1,0:T(8,128)(2,1)S(1)} %multiply_convert_fusion), kind=kOutput, calls=%fused_computation.8 | convolution fusion | flops 151388160 | bytes 2015232 | tf_op jit(solution)/shard_map/dot_general | solution.py:378
  58.5 0.6 convolution_convert_fusion
  59.1 1.2 %slice_bitcast_fusion = (bf16[1,3072,128]{2,1,0:T(8,128)(2,1)}, bf16[1,3072,128]{2,1,0:T(8,128)(2,1)}) fusion(bf16[3072,256]{1,0:T(8,128)(2,1)S(1)} %convolution_convert_fusion), kind=kLoop, calls=%fused_computation.18 | loop fusion | bytes 3145728 | tf_op jit(solution)/shard_map/broadcast_in_dim | solution.py:397
  60.3 0.5 convolution_bitcast_fusion
  60.8 2.3 %copy.24 = f32[3072,192]{1,0:T(8,128)} copy(f32[3072,192]{0,1:T(8,128)S(1)} %convolution_bitcast_fusion) | data formatting | bytes 4718592 | tf_op jit(solution)/shard_map/dot_general | solution.py:373
  63.1 2.9 %reshape.75.part_ref = f32[8,4,2,24,384]{4,3,2,1,0:T(8,128)S(1)} reshape(f32[3072,192]{1,0:T(8,128)} %copy.24) | data formatting | bytes 4718592 | tf_op jit(solution)/shard_map/reshape | solution.py:384
  66.0 0.0 copy-start.1
  66.0 1.3 %convert_element_type.34.partb_ref = bf16[8,4,2,24,384]{4,3,2,1,0:T(8,128)(2,1)} convert(f32[8,4,2,24,384]{4,3,2,1,0:T(8,128)S(1)} %reshape.75.part_ref) | non-fusion elementwise | flops 589824 | bytes 3538944 | tf_op jit(solution)/shard_map/convert_element_type | solution.py:331
  67.3 0.5 copy-done.1
  67.8 34.4 %shard_map.111 = f32[8,56,24]{2,1,0:T(8,128)} custom-call(f32[8,4,2,24,384]{4,3,2,1,0:T(8,128)} %copy-done.1, bf16[8,4,2,24,384]{4,3,2,1,0:T(8,128)(2,1)} %convert_element_type.34.partb_ref, f32[1,192]{1,0:T(1,128)} %bitcast.51), custom_call_target="tpu_custom_call" | custom-call | tf_op jit(solution)/shard_map/pallas_call | solution.py:301
  102.2 0.8 slice_reduce_fusion
  103.0 0.9 slice.37
  103.9 0.1 reshape_squeeze.3
  104.0 1.3 %gather_fusion.3 = f32[96]{0:T(128)S(1)} fusion(f32[192]{0:T(256)S(1)} %reshape_squeeze.3, s32[1024]{0:T(1024)S(1)} %pad_clamp_fusion), kind=kCustom, calls=%fused_computation.3 | custom fusion | bytes 1152 | tf_op jit(solution)/shard_map/gather | solution.py:392
  105.3 0.1 copy.29
  105.3 0.1 reshape.78
  105.5 0.1 reshape.80
  105.6 0.6 copy.27
  106.2 0.1 copy.26
  106.3 0.6 gather_fusion.2
  106.9 0.7 multiply_reduce_fusion
  (5 shorter events, 0.0 us)
Async XLA Ops:
  0.6 54.2 %copy-start = (bf16[1,128,3072]{2,1,0:T(8,128)(2,1)S(1)}, bf16[1,128,3072]{2,1,0:T(8,128)(2,1)}, u32[]{:S(2)}) copy-start(bf16[1,128,3072]{2,1,0:T(8,128)(2,1)} %param.13) | copy-start | bytes 2359300
  50.9 2.9 %copy-start.3 = (bf16[1,3072,128]{2,1,0:T(8,128)(2,1)S(1)}, bf16[1,3072,128]{2,1,0:T(8,128)(2,1)}, u32[]{:S(2)}) copy-start(bf16[1,3072,128]{2,1,0:T(8,128)(2,1)} %param.12) | copy-start | bytes 2359300
  50.9 2.8 %copy-start.4 = (bf16[1,3072,128]{2,1,0:T(8,128)(2,1)S(1)}, bf16[1,3072,128]{2,1,0:T(8,128)(2,1)}, u32[]{:S(2)}) copy-start(bf16[1,3072,128]{2,1,0:T(8,128)(2,1)} %param.11) | copy-start | bytes 2359300
  53.8 0.6 copy-start.2
  66.0 1.8 %copy-start.1 = (f32[8,4,2,24,384]{4,3,2,1,0:T(8,128)}, f32[8,4,2,24,384]{4,3,2,1,0:T(8,128)S(1)}, u32[]{:S(2)}) copy-start(f32[8,4,2,24,384]{4,3,2,1,0:T(8,128)S(1)} %reshape.75.part_ref) | copy-start | bytes 7077892

commit v15 on v14

--- a/solution.py
+++ b/solution.py
@@ -89,6 +89,12 @@
         sends.append(cp)
 
     def forward(src, zz, xs, to_x):
+        for dc in range(1, nc):
+            cp = pltpu.make_async_remote_copy(
+                src, out.at[zz, xs, c], send_c.at[dc - 1, xs, zz], recv_c.at[dc - 1, xs, zz],
+                device_id=(e, z, x, (c + dc) % nc), device_id_type=MESH_ID)
+            cp.start()
+            sends.append(cp)
         if to_x:
             for dx in range(1, nx):
                 cp = pltpu.make_async_remote_copy(
@@ -96,12 +102,6 @@
                     device_id=(e, z, (x + dx) % nx, c), device_id_type=MESH_ID)
                 cp.start()
                 sends.append(cp)
-        for dc in range(1, nc):
-            cp = pltpu.make_async_remote_copy(
-                src, out.at[zz, xs, c], send_c.at[dc - 1, xs, zz], recv_c.at[dc - 1, xs, zz],
-                device_id=(e, z, x, (c + dc) % nc), device_id_type=MESH_ID)
-            cp.start()
-            sends.append(cp)
 
     forward(xa, z, x, True)
     for d in range(1, nz):

time: 108 us -> 108 us (level)
  no operation moved by 1% of the time
where the time goes in v15:
time: 108 us
  Pallas kernels  76 us (70%)
  local copies, waits for them, and re-layouts  21.2 us (20%)
  other arithmetic  5.2 us (5%)
  matrix products  4.59 us (4%)
    pallas_call x1, Pallas kernels, ep_etp_gather(): pl.pallas_call(functools.partial(_gather_kernel, ne, nz, nx, nc), out_sha...  41.4 us
    pallas_call x1, Pallas kernels, etp_reduce_scatter(): pl.pallas_call(functools.partial(_rs_kernel, ne, nz, nx, nc), out_shape=j...  34.6 us
    reshape x1, local copies, waits for them, and re-layouts, per_device(): part = out_t.reshape(nz, nx, nc, width // 2, 2 * rows)  2.88 us
    slice x1, local copies, waits for them, and re-layouts, per_device(): xt = xc_all[..., :rows].reshape(feat, rows)  2.82 us
    unnamed x13, local copies, waits for them, and re-layouts  2.71 us
    dot_general x1, local copies, waits for them, and re-layouts, per_device(): out_t = lax.dot_general(wd, hidden, dims(0, 1), preferred_element_type=f32)  2.32 us

profile of v15, /device:TPU:6, one launch (start us, length us, event | category | flops | bytes accessed | tf_op | source)
XLA Modules:
  0.0 107.8 jit_solution(9526947951056121837)
XLA Ops:
  0.6 0.0 copy-start
  0.7 0.8 broadcast_multiply_fusion
  1.4 0.8 fusion.19
  2.2 0.1 copy.20
  2.3 0.1 mul.66
  2.4 0.8 copy.19
  3.2 0.1 reshape.72
  3.3 0.1 pad_maximum_fusion
  3.4 0.8 copy.21
  4.2 0.1 eq.15
  4.3 0.1 fusion.16
  4.4 0.1 reduce_window_sum.11
  4.5 0.2 select_reduce_fusion
  4.7 0.9 scatter_custom_fusion
  5.6 1.6 %gather_fusion.1 = f32[192]{0:T(256)S(1)} fusion(f32[97]{0:T(128)S(1)} %pad_maximum_fusion, s32[1024]{0:T(1024)S(1)} %get-tuple-element.31), kind=kCustom, calls=%fused_computation.1 | custom fusion | bytes 2304 | tf_op jit(solution)/shard_map/gather | solution.py:351
  7.2 0.7 reshape.73.g_ref
  7.9 0.8 gather_fusion
  8.7 0.8 copy.22
  9.5 41.4 %shard_map.110 = (bf16[8,4,2,48,384]{4,3,2,1,0:T(8,128)(2,1)}, f32[1,192]{1,0:T(1,128)}) custom-call(bf16[8,96,24]{2,1,0:T(8,128)(2,1)} %bitcast.47, f32[8,1,24]{2,1,0:T(1,128)} %reshape.73.g_ref), custom_call_target="tpu_custom_call" | custom-call | tf_op jit(solution)/shard_map/pallas_call | solution.py:139
  50.9 0.0 copy-start.3
  50.9 0.0 copy-start.4
  50.9 2.8 %fusion.26 = (bf16[8,4,2,48,192]{4,3,2,1,0:T(8,128)(2,1)S(1)}, bf16[8,4,2,48,192]{4,3,2,1,0:T(8,128)(2,1)S(1)}) fusion(bf16[8,4,2,48,384]{4,3,2,1,0:T(8,128)(2,1)} %get-tuple-element.7), kind=kLoop, calls=%fused_computation.61 | loop fusion | bytes 4718592 | tf_op jit(solution)/shard_map/slice | solution.py:359
  53.7 0.0 copy-done.3
  53.8 0.0 copy-done.4
  53.8 0.0 copy-start.2
  53.8 0.6 fusion.5
  54.4 0.0 copy-done.2
  54.4 0.4 multiply_convert_fusion
  54.8 0.0 copy-done
  54.8 1.4 %fusion.1 = f32[384,128]{1,0:T(8,128)S(1)} fusion(bf16[3072,192]{1,0:T(8,128)(2,1)S(1)} %bitcast.45, bf16[3072,192]{1,0:T(8,128)(2,1)S(1)} %multiply_convert_fusion, bf16[1,128,3072]{2,1,0:T(8,128)(2,1)S(1)} %copy-done), kind=kOutput, calls=%fused_computation.10 | convolution fusion | flops 306708480 | bytes 3342336 | tf_op jit(solution)/shard_map/dot_general | solution.py:374
  56.3 0.7 multiply_convert_fusion.2
  57.0 1.5 %fusion = bf16[1,128,3072]{2,1,0:T(8,128)(2,1)} fusion(bf16[192,128]{1,0:T(8,128)(2,1)S(1)} %get-tuple-element.28, bf16[3072,192]{1,0:T(8,128)(2,1)S(1)} %multiply_convert_fusion), kind=kOutput, calls=%fused_computation.8 | convolution fusion | flops 151388160 | bytes 2015232 | tf_op jit(solution)/shard_map/dot_general | solution.py:378
  58.5 0.6 convolution_convert_fusion
  59.1 1.2 %slice_bitcast_fusion = (bf16[1,3072,128]{2,1,0:T(8,128)(2,1)}, bf16[1,3072,128]{2,1,0:T(8,128)(2,1)}) fusion(bf16[3072,256]{1,0:T(8,128)(2,1)S(1)} %convolution_convert_fusion), kind=kLoop, calls=%fused_computation.18 | loop fusion | bytes 3145728 | tf_op jit(solution)/shard_map/broadcast_in_dim | solution.py:397
  60.3 0.5 convolution_bitcast_fusion
  60.8 2.3 %copy.24 = f32[3072,192]{1,0:T(8,128)} copy(f32[3072,192]{0,1:T(8,128)S(1)} %convolution_bitcast_fusion) | data formatting | bytes 4718592 | tf_op jit(solution)/shard_map/dot_general | solution.py:373
  63.1 2.9 %reshape.75.part_ref = f32[8,4,2,24,384]{4,3,2,1,0:T(8,128)S(1)} reshape(f32[3072,192]{1,0:T(8,128)} %copy.24) | data formatting | bytes 4718592 | tf_op jit(solution)/shard_map/reshape | solution.py:384
  66.0 0.0 copy-start.1
  66.0 1.3 %convert_element_type.34.partb_ref = bf16[8,4,2,24,384]{4,3,2,1,0:T(8,128)(2,1)} convert(f32[8,4,2,24,384]{4,3,2,1,0:T(8,128)S(1)} %reshape.75.part_ref) | non-fusion elementwise | flops 589824 | bytes 3538944 | tf_op jit(solution)/shard_map/convert_element_type | solution.py:331
  67.3 0.5 copy-done.1
  67.8 34.6 %shard_map.111 = f32[8,56,24]{2,1,0:T(8,128)} custom-call(f32[8,4,2,24,384]{4,3,2,1,0:T(8,128)} %copy-done.1, bf16[8,4,2,24,384]{4,3,2,1,0:T(8,128)(2,1)} %convert_element_type.34.partb_ref, f32[1,192]{1,0:T(1,128)} %bitcast.51), custom_call_target="tpu_custom_call" | custom-call | tf_op jit(solution)/shard_map/pallas_call | solution.py:301
  102.3 0.8 slice_reduce_fusion
  103.1 0.9 slice.37
  104.1 0.1 reshape_squeeze.3
  104.1 1.3 %gather_fusion.3 = f32[96]{0:T(128)S(1)} fusion(f32[192]{0:T(256)S(1)} %reshape_squeeze.3, s32[1024]{0:T(1024)S(1)} %pad_clamp_fusion), kind=kCustom, calls=%fused_computation.3 | custom fusion | bytes 1152 | tf_op jit(solution)/shard_map/gather | solution.py:392
  105.4 0.1 copy.29
  105.5 0.1 reshape.78
  105.6 0.1 reshape.80
  105.7 0.6 copy.27
  106.4 0.1 copy.26
  106.5 0.6 gather_fusion.2
  107.1 0.7 multiply_reduce_fusion
  (5 shorter events, 0.0 us)
Async XLA Ops:
  0.6 54.2 %copy-start = (bf16[1,128,3072]{2,1,0:T(8,128)(2,1)S(1)}, bf16[1,128,3072]{2,1,0:T(8,128)(2,1)}, u32[]{:S(2)}) copy-start(bf16[1,128,3072]{2,1,0:T(8,128)(2,1)} %param.13) | copy-start | bytes 2359300
  50.9 2.9 %copy-start.3 = (bf16[1,3072,128]{2,1,0:T(8,128)(2,1)S(1)}, bf16[1,3072,128]{2,1,0:T(8,128)(2,1)}, u32[]{:S(2)}) copy-start(bf16[1,3072,128]{2,1,0:T(8,128)(2,1)} %param.12) | copy-start | bytes 2359300
  50.9 2.8 %copy-start.4 = (bf16[1,3072,128]{2,1,0:T(8,128)(2,1)S(1)}, bf16[1,3072,128]{2,1,0:T(8,128)(2,1)}, u32[]{:S(2)}) copy-start(bf16[1,3072,128]{2,1,0:T(8,128)(2,1)} %param.11) | copy-start | bytes 2359300
  53.8 0.6 copy-start.2
  66.0 1.8 %copy-start.1 = (f32[8,4,2,24,384]{4,3,2,1,0:T(8,128)}, f32[8,4,2,24,384]{4,3,2,1,0:T(8,128)S(1)}, u32[]{:S(2)}) copy-start(f32[8,4,2,24,384]{4,3,2,1,0:T(8,128)S(1)} %reshape.75.part_ref) | copy-start | bytes 7077892

commit v16 on v14

--- a/solution.py
+++ b/solution.py
@@ -159,7 +159,7 @@
     )(sent, gsend)
 
 
-def _rs_kernel(ne, nz, nx, nc, part_ref, partb_ref, inner_ref, out_ref, recv_c, acc1, acc1b, recv_b, acc2, acc2b,
+def _rs_kernel(ne, nz, nx, nc, part_ref, inner_ref, out_ref, partb_ref, recv_c, acc1, acc1b, recv_b, acc2, acc2b,
                recv_a, ir_c, in1, ir_b, in2, ir_a, fin,
                sem_local, send_c, rsem_c, send_b, rsem_b, send_a, rsem_a, send_d, rsem_d):
     e, z, x, c = _coords()
@@ -182,11 +182,19 @@
                     device_id=peers_of[d][1], device_id_type=MESH_ID).wait_recv()
 
     order = [(x + k) % nx for k in range(1, nx)] + [x]
+
+    def cast_partner(i, carry):
+        zi = i // nx
+        xi = i % nx
+        for d in range(1, nc):
+            partb_ref[d - 1, zi, xi] = part_ref[zi, xi, (c + d) % nc].astype(partb_ref.dtype)
+        return carry
+    lax.fori_loop(0, nz * nx, cast_partner, 0)
     for d in range(1, nc):
         cpeer = (e, z, x, (c + d) % nc)
         for k, xx in enumerate(order):
             cp = pltpu.make_async_remote_copy(
-                partb_ref.at[:, xx, (c + d) % nc], recv_c.at[d - 1, :, xx], send_c.at[d - 1, k], rsem_c.at[d - 1, k],
+                partb_ref.at[d - 1, :, xx], recv_c.at[d - 1, :, xx], send_c.at[d - 1, k], rsem_c.at[d - 1, k],
                 device_id=cpeer, device_id_type=MESH_ID)
             cp.start()
             sends.append(cp)
@@ -301,9 +309,10 @@
     return pl.pallas_call(
         functools.partial(_rs_kernel, ne, nz, nx, nc),
         out_shape=jax.ShapeDtypeStruct((ne, pad_rows, blk), f32),
-        in_specs=[pl.BlockSpec(memory_space=vmem)] * 3,
+        in_specs=[pl.BlockSpec(memory_space=vmem)] * 2,
         out_specs=pl.BlockSpec(memory_space=vmem),
         scratch_shapes=[
+            pltpu.VMEM((mc, nz, nx, feats, cols), bf16),
             pltpu.VMEM((mc, nz, nx, feats, cols), bf16),
             pltpu.VMEM((nz, nx, feats, cols), f32),
             pltpu.VMEM((nz, nx, feats, cols), bf16),
@@ -328,7 +337,7 @@
             dma((ne,)),
         ],
         compiler_params=pltpu.CompilerParams(collective_id=1, has_side_effects=True),
-    )(part, part.astype(bf16), inner)
+    )(part, inner)
 
 
 def per_device(tokens, routes, route_gates, cotangent, w_gate, w_up, w_down):

time: 108 us -> 108 us (level)
  other arithmetic: 5.2 us -> 3.93 us
    reshape x1, local copies, waits for them, and re-layouts: 2.88 us -> 4.22 us  [per_device(): part = out_t.reshape(nz, nx, nc, width // 2, 2 * rows)]
    convert_element_type x1 -> x0, other arithmetic: 1.26 us -> none  [etp_reduce_scatter(): part.astype(bf16)]
    unnamed x13 -> x11, local copies, waits for them, and re-layouts: 2.71 us -> 2.21 us
where the time goes in v16:
time: 108 us; the launch traced here: 107 us
  Pallas kernels  75.9 us (70%)
  local copies, waits for them, and re-layouts  22 us (20%)
  matrix products  4.59 us (4%)
  other arithmetic  3.93 us (4%)
    pallas_call x1, Pallas kernels, ep_etp_gather(): pl.pallas_call(functools.partial(_gather_kernel, ne, nz, nx, nc), out_sha...  41.4 us
    pallas_call x1, Pallas kernels, etp_reduce_scatter(): pl.pallas_call(functools.partial(_rs_kernel, ne, nz, nx, nc), out_shape=j...  34.4 us
    reshape x1, local copies, waits for them, and re-layouts, per_device(): part = out_t.reshape(nz, nx, nc, width // 2, 2 * rows)  4.22 us
    slice x1, local copies, waits for them, and re-layouts, per_device(): xt = xc_all[..., :rows].reshape(feat, rows)  2.82 us
    dot_general x1, local copies, waits for them, and re-layouts, per_device(): out_t = lax.dot_general(wd, hidden, dims(0, 1), preferred_element_type=f32)  2.32 us
    unnamed x11, local copies, waits for them, and re-layouts  2.21 us

profile of v16, /device:TPU:6, one launch (start us, length us, event | category | flops | bytes accessed | tf_op | source)
XLA Modules:
  0.0 107.3 jit_solution(6536288676586829421)
XLA Ops:
  0.6 0.0 copy-start
  0.7 0.8 broadcast_multiply_fusion
  1.4 0.8 fusion.19
  2.2 0.1 copy.20
  2.3 0.1 mul.66
  2.4 0.8 copy.19
  3.2 0.1 reshape.72
  3.3 0.1 pad_maximum_fusion
  3.4 0.8 copy.21
  4.2 0.1 eq.15
  4.3 0.1 fusion.16
  4.4 0.1 reduce_window_sum.11
  4.5 0.2 select_reduce_fusion
  4.7 0.9 scatter_custom_fusion
  5.6 1.6 %gather_fusion.1 = f32[192]{0:T(256)S(1)} fusion(f32[97]{0:T(128)S(1)} %pad_maximum_fusion, s32[1024]{0:T(1024)S(1)} %get-tuple-element.31), kind=kCustom, calls=%fused_computation.1 | custom fusion | bytes 2304 | tf_op jit(solution)/shard_map/gather | solution.py:360
  7.2 0.7 reshape.73.g_ref
  7.9 0.8 gather_fusion
  8.7 0.8 copy.22
  9.5 41.4 %shard_map.110 = (bf16[8,4,2,48,384]{4,3,2,1,0:T(8,128)(2,1)}, f32[1,192]{1,0:T(1,128)}) custom-call(bf16[8,96,24]{2,1,0:T(8,128)(2,1)} %bitcast.47, f32[8,1,24]{2,1,0:T(1,128)} %reshape.73.g_ref), custom_call_target="tpu_custom_call" | custom-call | tf_op jit(solution)/shard_map/pallas_call | solution.py:139
  50.9 0.0 copy-start.2
  50.9 0.0 copy-start.3
  50.9 2.8 %fusion.26 = (bf16[8,4,2,48,192]{4,3,2,1,0:T(8,128)(2,1)S(1)}, bf16[8,4,2,48,192]{4,3,2,1,0:T(8,128)(2,1)S(1)}) fusion(bf16[8,4,2,48,384]{4,3,2,1,0:T(8,128)(2,1)} %get-tuple-element.7), kind=kLoop, calls=%fused_computation.61 | loop fusion | bytes 4718592 | tf_op jit(solution)/shard_map/slice | solution.py:368
  53.7 0.0 copy-done.2
  53.8 0.0 copy-done.3
  53.8 0.0 copy-start.1
  53.8 0.6 fusion.5
  54.4 0.0 copy-done.1
  54.4 0.4 multiply_convert_fusion
  54.8 0.0 copy-done
  54.8 1.4 %fusion.1 = f32[384,128]{1,0:T(8,128)S(1)} fusion(bf16[3072,192]{1,0:T(8,128)(2,1)S(1)} %bitcast.45, bf16[3072,192]{1,0:T(8,128)(2,1)S(1)} %multiply_convert_fusion, bf16[1,128,3072]{2,1,0:T(8,128)(2,1)S(1)} %copy-done), kind=kOutput, calls=%fused_computation.10 | convolution fusion | flops 306708480 | bytes 3342336 | tf_op jit(solution)/shard_map/dot_general | solution.py:383
  56.3 0.7 multiply_convert_fusion.2
  57.0 1.5 %fusion = bf16[1,128,3072]{2,1,0:T(8,128)(2,1)} fusion(bf16[192,128]{1,0:T(8,128)(2,1)S(1)} %get-tuple-element.28, bf16[3072,192]{1,0:T(8,128)(2,1)S(1)} %multiply_convert_fusion), kind=kOutput, calls=%fused_computation.8 | convolution fusion | flops 151388160 | bytes 2015232 | tf_op jit(solution)/shard_map/dot_general | solution.py:387
  58.5 0.6 convolution_convert_fusion
  59.1 1.2 %slice_bitcast_fusion = (bf16[1,3072,128]{2,1,0:T(8,128)(2,1)}, bf16[1,3072,128]{2,1,0:T(8,128)(2,1)}) fusion(bf16[3072,256]{1,0:T(8,128)(2,1)S(1)} %convolution_convert_fusion), kind=kLoop, calls=%fused_computation.18 | loop fusion | bytes 3145728 | tf_op jit(solution)/shard_map/broadcast_in_dim | solution.py:406
  60.3 0.5 convolution_bitcast_fusion
  60.8 2.3 %copy.24 = f32[3072,192]{1,0:T(8,128)} copy(f32[3072,192]{0,1:T(8,128)S(1)} %convolution_bitcast_fusion) | data formatting | bytes 4718592 | tf_op jit(solution)/shard_map/dot_general | solution.py:382
  63.1 4.2 %reshape.75.part_ref = f32[8,4,2,24,384]{4,3,2,1,0:T(8,128)} reshape(f32[3072,192]{1,0:T(8,128)} %copy.24) | data formatting | bytes 4718592 | tf_op jit(solution)/shard_map/reshape | solution.py:393
  67.3 34.4 %shard_map.111 = f32[8,56,24]{2,1,0:T(8,128)} custom-call(f32[8,4,2,24,384]{4,3,2,1,0:T(8,128)} %reshape.75.part_ref, f32[1,192]{1,0:T(1,128)} %bitcast.51), custom_call_target="tpu_custom_call" | custom-call | tf_op jit(solution)/shard_map/pallas_call | solution.py:309
  101.8 0.8 slice_reduce_fusion
  102.6 0.9 slice.37
  103.5 0.1 reshape_squeeze.3
  103.6 1.3 %gather_fusion.3 = f32[96]{0:T(128)S(1)} fusion(f32[192]{0:T(256)S(1)} %reshape_squeeze.3, s32[1024]{0:T(1024)S(1)} %pad_clamp_fusion), kind=kCustom, calls=%fused_computation.3 | custom fusion | bytes 1152 | tf_op jit(solution)/shard_map/gather | solution.py:401
  104.9 0.1 copy.29
  104.9 0.1 reshape.78
  105.0 0.1 reshape.80
  105.2 0.6 copy.27
  105.8 0.1 copy.26
  105.9 0.6 gather_fusion.2
  106.5 0.7 multiply_reduce_fusion
  (5 shorter events, 0.0 us)
Async XLA Ops:
  0.6 54.2 %copy-start = (bf16[1,128,3072]{2,1,0:T(8,128)(2,1)S(1)}, bf16[1,128,3072]{2,1,0:T(8,128)(2,1)}, u32[]{:S(2)}) copy-start(bf16[1,128,3072]{2,1,0:T(8,128)(2,1)} %param.13) | copy-start | bytes 2359300
  50.9 2.9 %copy-start.2 = (bf16[1,3072,128]{2,1,0:T(8,128)(2,1)S(1)}, bf16[1,3072,128]{2,1,0:T(8,128)(2,1)}, u32[]{:S(2)}) copy-start(bf16[1,3072,128]{2,1,0:T(8,128)(2,1)} %param.12) | copy-start | bytes 2359300
  50.9 2.8 %copy-start.3 = (bf16[1,3072,128]{2,1,0:T(8,128)(2,1)S(1)}, bf16[1,3072,128]{2,1,0:T(8,128)(2,1)}, u32[]{:S(2)}) copy-start(bf16[1,3072,128]{2,1,0:T(8,128)(2,1)} %param.11) | copy-start | bytes 2359300
  53.8 0.6 copy-start.1
